TPU v7x, 32 devices: a whole 2x2x4 slice. The times are simulated.
32 devices in a mesh: fsdp: 2 (over y), ctx: 4 (over x, core), tp: 4 (over z).
Axes of the slice: x: 2, y: 2, z: 4, core: 2. Of those that a mesh axis runs over, the one named last changes fastest.
Arguments:
- inputs: bfloat16 [4, 2048, 768], P('fsdp', 'ctx'), may hold values from -6 to 6
- segment_ids: int32 [4, 2048], P('fsdp'), may hold values from 0 to 31, never falling along the last dimension, each value on 1 to 1025 neighbouring positions
- query_weight: float32 [768, 768], P(('fsdp', 'ctx'), 'tp'), may hold values from -0.3125 to 0.3125
- query_bias: float32 [768], P('tp'), may hold values from -3 to 3
- key_weight: float32 [768, 768], P(('fsdp', 'ctx'), 'tp'), may hold values from -0.3125 to 0.3125
- value_weight: float32 [768, 768], P(('fsdp', 'ctx'), 'tp'), may hold values from -0.21875 to 0.21875
- value_bias: float32 [768], P('tp'), may hold values from -3 to 3
- output_weight: float32 [768, 768], P('tp', ('fsdp', 'ctx')), may hold values from -0.875 to 0.875
- output_bias: float32 [768], replicated, may hold values from -3 to 3
- first_gain: float32 [768], replicated, may hold values from 0.5 to 1.5
- first_shift: float32 [768], replicated, may hold values from -2 to 2
- up_weight: float32 [768, 3072], P(('fsdp', 'ctx'), 'tp'), may hold values from -0.21875 to 0.21875
- up_bias: float32 [3072], P('tp'), may hold values from -3 to 3
- down_weight: float32 [3072, 768], P('tp', ('fsdp', 'ctx')), may hold values from -0.109375 to 0.109375
- down_bias: float32 [768], replicated, may hold values from -3 to 3
- second_gain: float32 [768], replicated, may hold values from 0.5 to 1.5
- second_shift: float32 [768], replicated, may hold values from -2 to 2
- cotangent: bfloat16 [4, 2048, 768], P('fsdp', 'ctx'), may hold values from -6 to 6
Outputs:
- layer_output: bfloat16 [4, 2048, 768], P('fsdp', 'ctx')
- input_grad: bfloat16 [4, 2048, 768], P('fsdp', 'ctx')
- query_weight_grad: float32 [768, 768], P(('fsdp', 'ctx'), 'tp')
- query_bias_grad: float32 [768], P('tp')
- key_weight_grad: float32 [768, 768], P(('fsdp', 'ctx'), 'tp')
- value_weight_grad: float32 [768, 768], P(('fsdp', 'ctx'), 'tp')
- value_bias_grad: float32 [768], P('tp')
- output_weight_grad: float32 [768, 768], P('tp', ('fsdp', 'ctx'))
- output_bias_grad: float32 [768], replicated
- first_gain_grad: float32 [768], replicated
- first_shift_grad: float32 [768], replicated
- up_weight_grad: float32 [768, 3072], P(('fsdp', 'ctx'), 'tp')
- up_bias_grad: float32 [3072], P('tp')
- down_weight_grad: float32 [3072, 768], P('tp', ('fsdp', 'ctx'))
- down_bias_grad: float32 [768], replicated
- second_gain_grad: float32 [768], replicated
- second_shift_grad: float32 [768], replicated
Inputs may be any that keep to these rules, and one draw needn't show every extreme that they name: `segment_ids`: along a sequence the document numbers never fall; every number appears, a document holds 1 to 1025 tokens and in every sequence some document holds exactly 1025.
All inputs are finite; a program needn't handle non-finite values.
Results may differ from a plain program's by a relative error of at most 0.015.
The roundings to bfloat16 on the way count: a program that leaves them out, or rounds other values in their place, can miss the bound.
Values may be sent and summed in bfloat16 or wider, within the bound.
No kernel may reach another device: no remote copies, remote signals or barrier semaphores. Data moves between devices by JAX's collectives and lax.ppermute only.
A program may use at most 128 MiB of HBM per device.

v0:
```python
import math

import jax
import jax.numpy as jnp
from jax import lax
from jax.sharding import PartitionSpec as P

DH = 64


EPSILON = 1e-05
MASKED = -1e30
ROOT_HALF = 0.7071067811865476
ROOT_TWO_PI = 2.5066282746310002


def matmul(left, right):
    return jnp.dot(left, right, preferred_element_type=jnp.float32)


def inner_rows(left, right):
    return lax.dot_general(
        left, right, (((0,), (0,)), ((), ())), preferred_element_type=jnp.float32
    )


def outer_rows(left, right):
    return lax.dot_general(
        left, right, (((1,), (1,)), ((), ())), preferred_element_type=jnp.float32
    )


def head_total(partial_value):
    return lax.psum(partial_value, "tp")


def head_major(flat_rows, seq_count, rows, heads_local):
    return flat_rows.reshape(seq_count, rows, heads_local, DH).transpose(0, 2, 1, 3)


def token_major(heads_first):
    seq_count, heads_local, rows, size = heads_first.shape
    return heads_first.transpose(0, 2, 1, 3).reshape(seq_count * rows, heads_local * size)


def normalize(resid, gain, shift):
    center = resid - jnp.mean(resid, axis=-1, keepdims=True)
    inverse = lax.rsqrt(jnp.mean(center * center, axis=-1, keepdims=True) + EPSILON)
    normed = center * inverse
    return (normed * gain + shift, normed, inverse)


def norm_back(grad, normed, inverse, gain):
    scaled = grad * gain
    inner = (
        scaled
        - jnp.mean(scaled, axis=-1, keepdims=True)
        - normed * jnp.mean(scaled * normed, axis=-1, keepdims=True)
    )
    return (inner * inverse, jnp.sum(grad * normed, axis=0), jnp.sum(grad, axis=0))


def scores_of(query_seq, key_seq, query_docs, key_docs):
    raw = jnp.einsum("hqd,hkd->hqk", query_seq, key_seq, preferred_element_type=jnp.float32) * (
        1.0 / math.sqrt(DH)
    )
    allowed = query_docs[:, None] == key_docs[None, :]
    return jnp.where(allowed[None, :, :], raw, MASKED)


def attend_forward(item):
    query_seq, key_seq, value_seq, query_docs, key_docs = item
    masked = scores_of(query_seq, key_seq, query_docs, key_docs)
    top = jnp.max(masked, axis=-1, keepdims=True)
    powers = jnp.exp(masked - top)
    total = jnp.sum(powers, axis=-1, keepdims=True)
    weights = (powers / total).astype(jnp.bfloat16)
    mixed = jnp.einsum("hqk,hkd->hqd", weights, value_seq, preferred_element_type=jnp.float32)
    return (mixed.astype(jnp.bfloat16), top, total)


def attend_backward(item):
    query_seq, key_seq, value_seq, query_docs, key_docs, top, total, grad_mixed = item
    masked = scores_of(query_seq, key_seq, query_docs, key_docs)
    weights = jnp.exp(masked - top) / total
    rounded = weights.astype(jnp.bfloat16)
    grad_weights = jnp.einsum(
        "hqd,hkd->hqk", grad_mixed, value_seq, preferred_element_type=jnp.float32
    )
    along = jnp.sum(weights * grad_weights, axis=-1, keepdims=True)
    grad_scores = (weights * (grad_weights - along)).astype(jnp.bfloat16)
    scale = 1.0 / math.sqrt(DH)
    grad_query = (
        jnp.einsum("hqk,hkd->hqd", grad_scores, key_seq, preferred_element_type=jnp.float32) * scale
    ).astype(jnp.bfloat16)
    grad_key = (
        jnp.einsum("hqk,hqd->hkd", grad_scores, query_seq, preferred_element_type=jnp.float32)
        * scale
    )
    grad_value = jnp.einsum("hqk,hqd->hkd", rounded, grad_mixed, preferred_element_type=jnp.float32)
    return (grad_query, grad_key, grad_value)


def body(
    inputs,
    segment_ids,
    query_weight,
    query_bias,
    key_weight,
    value_weight,
    value_bias,
    output_weight,
    output_bias,
    first_gain,
    first_shift,
    up_weight,
    up_bias,
    down_weight,
    down_bias,
    second_gain,
    second_shift,
    cotangent,
):
    masters = (query_weight, key_weight, value_weight, up_weight, output_weight, down_weight)
    lowered = tuple((master.astype(jnp.bfloat16) for master in masters))
    gathered = (
        lax.all_gather(lowered[0], ("fsdp", "ctx"), axis=0, tiled=True),
        lax.all_gather(lowered[1], ("fsdp", "ctx"), axis=0, tiled=True),
        lax.all_gather(lowered[2], ("fsdp", "ctx"), axis=0, tiled=True),
        lax.all_gather(lowered[3], ("fsdp", "ctx"), axis=0, tiled=True),
        lax.all_gather(lowered[4], ("fsdp", "ctx"), axis=1, tiled=True),
        lax.all_gather(lowered[5], ("fsdp", "ctx"), axis=1, tiled=True),
    )
    query_full, key_full, value_full, up_full, output_full, down_full = gathered
    seq_count, rows, width = inputs.shape
    heads_local = query_full.shape[1] // DH
    flat = inputs.reshape(seq_count * rows, width)
    queries = (matmul(flat, query_full) + query_bias).astype(jnp.bfloat16)
    keys_mine = head_major(
        matmul(flat, key_full).astype(jnp.bfloat16), seq_count, rows, heads_local
    )
    values_mine = head_major(
        (matmul(flat, value_full) + value_bias).astype(jnp.bfloat16), seq_count, rows, heads_local
    )
    place = lax.axis_index("ctx")
    query_docs = lax.dynamic_slice_in_dim(segment_ids, place * rows, rows, 1)
    key_heads, value_heads = (
        lax.all_gather(keys_mine, "ctx", axis=2, tiled=True),
        lax.all_gather(values_mine, "ctx", axis=2, tiled=True),
    )
    query_heads = head_major(queries, seq_count, rows, heads_local)
    mixed, top, total = lax.map(
        attend_forward, (query_heads, key_heads, value_heads, query_docs, segment_ids)
    )
    mixed_flat = token_major(mixed)
    branch = head_total(matmul(mixed_flat, output_full)) + output_bias
    inputs_wide = flat.astype(jnp.float32)
    first, normed_one, inverse_one = normalize(inputs_wide + branch, first_gain, first_shift)
    first_low = first.astype(jnp.bfloat16)
    upper = matmul(first_low, up_full) + up_bias
    cumulative = 0.5 * (1.0 + lax.erf(upper * ROOT_HALF))
    active = (upper * cumulative).astype(jnp.bfloat16)
    down = head_total(matmul(active, down_full)) + down_bias
    result, normed_two, inverse_two = normalize(first + down, second_gain, second_shift)
    layer_output = result.astype(jnp.bfloat16).reshape(seq_count, rows, width)
    again = (
        lax.all_gather(lowered[0], ("fsdp", "ctx"), axis=0, tiled=True),
        lax.all_gather(lowered[1], ("fsdp", "ctx"), axis=0, tiled=True),
        lax.all_gather(lowered[2], ("fsdp", "ctx"), axis=0, tiled=True),
        lax.all_gather(lowered[3], ("fsdp", "ctx"), axis=0, tiled=True),
        lax.all_gather(lowered[4], ("fsdp", "ctx"), axis=1, tiled=True),
        lax.all_gather(lowered[5], ("fsdp", "ctx"), axis=1, tiled=True),
    )
    query_back, key_back, value_back, up_back, output_back, down_back = again
    grad_out = cotangent.reshape(seq_count * rows, width).astype(jnp.float32)
    grad_two, grad_second_gain, grad_second_shift = norm_back(
        grad_out, normed_two, inverse_two, second_gain
    )
    grad_down = grad_two.astype(jnp.bfloat16)
    grad_down_bias = jnp.sum(grad_down.astype(jnp.float32), axis=0)
    grad_down_weight = inner_rows(active, grad_down)
    grad_active = outer_rows(grad_down, down_back)
    density = jnp.exp(-0.5 * upper * upper) / ROOT_TWO_PI
    grad_upper = (grad_active * (cumulative + upper * density)).astype(jnp.bfloat16)
    grad_up_bias = jnp.sum(grad_upper.astype(jnp.float32), axis=0)
    grad_up_weight = inner_rows(first_low, grad_upper)
    grad_first = grad_two + head_total(outer_rows(grad_upper, up_back))
    grad_one, grad_first_gain, grad_first_shift = norm_back(
        grad_first, normed_one, inverse_one, first_gain
    )
    grad_branch = grad_one.astype(jnp.bfloat16)
    grad_output_bias = jnp.sum(grad_branch.astype(jnp.float32), axis=0)
    grad_output_weight = inner_rows(mixed_flat, grad_branch)
    grad_mixed = head_major(
        outer_rows(grad_branch, output_back).astype(jnp.bfloat16), seq_count, rows, heads_local
    )
    grad_query, grad_key_part, grad_value_part = lax.map(
        attend_backward,
        (query_heads, key_heads, value_heads, query_docs, segment_ids, top, total, grad_mixed),
    )
    grad_key_mine, grad_value_mine = (
        lax.psum_scatter(
            grad_key_part.astype(jnp.bfloat16), "ctx", scatter_dimension=2, tiled=True
        ).astype(jnp.float32),
        lax.psum_scatter(
            grad_value_part.astype(jnp.bfloat16), "ctx", scatter_dimension=2, tiled=True
        ).astype(jnp.float32),
    )
    grad_query_low = token_major(grad_query)
    grad_key_low = token_major(grad_key_mine.astype(jnp.bfloat16))
    grad_value_low = token_major(grad_value_mine.astype(jnp.bfloat16))
    grad_query_weight = inner_rows(flat, grad_query_low)
    grad_key_weight = inner_rows(flat, grad_key_low)
    grad_value_weight = inner_rows(flat, grad_value_low)
    grad_query_bias = jnp.sum(grad_query_low.astype(jnp.float32), axis=0)
    grad_value_bias = jnp.sum(grad_value_low.astype(jnp.float32), axis=0)
    input_part = (
        outer_rows(grad_query_low, query_back)
        + outer_rows(grad_key_low, key_back)
        + outer_rows(grad_value_low, value_back)
    )
    grad_inputs = (
        (grad_one + head_total(input_part)).astype(jnp.bfloat16).reshape(seq_count, rows, width)
    )
    grad_weights = (
        lax.psum_scatter(grad_query_weight, ("fsdp", "ctx"), scatter_dimension=0, tiled=True),
        lax.psum_scatter(grad_key_weight, ("fsdp", "ctx"), scatter_dimension=0, tiled=True),
        lax.psum_scatter(grad_value_weight, ("fsdp", "ctx"), scatter_dimension=0, tiled=True),
        lax.psum_scatter(grad_up_weight, ("fsdp", "ctx"), scatter_dimension=0, tiled=True),
        lax.psum_scatter(grad_output_weight, ("fsdp", "ctx"), scatter_dimension=1, tiled=True),
        lax.psum_scatter(grad_down_weight, ("fsdp", "ctx"), scatter_dimension=1, tiled=True),
    )
    grad_small = lax.psum(
        (
            grad_query_bias,
            grad_value_bias,
            grad_output_bias,
            grad_first_gain,
            grad_first_shift,
            grad_up_bias,
            grad_down_bias,
            grad_second_gain,
            grad_second_shift,
        ),
        ("fsdp", "ctx"),
    )
    return (
        layer_output,
        grad_inputs,
        grad_weights[0],
        grad_small[0],
        grad_weights[1],
        grad_weights[2],
        grad_small[1],
        grad_weights[4],
        grad_small[2],
        grad_small[3],
        grad_small[4],
        grad_weights[3],
        grad_small[5],
        grad_weights[5],
        grad_small[6],
        grad_small[7],
        grad_small[8],
    )


def solution(mesh):
    in_specs = (
        P("fsdp", "ctx", None),
        P("fsdp", None),
        P(("fsdp", "ctx"), "tp"),
        P("tp"),
        P(("fsdp", "ctx"), "tp"),
        P(("fsdp", "ctx"), "tp"),
        P("tp"),
        P("tp", ("fsdp", "ctx")),
        P(),
        P(),
        P(),
        P(("fsdp", "ctx"), "tp"),
        P("tp"),
        P("tp", ("fsdp", "ctx")),
        P(),
        P(),
        P(),
        P("fsdp", "ctx", None),
    )
    out_specs = (
        P("fsdp", "ctx", None),
        P("fsdp", "ctx", None),
        P(("fsdp", "ctx"), "tp"),
        P("tp"),
        P(("fsdp", "ctx"), "tp"),
        P(("fsdp", "ctx"), "tp"),
        P("tp"),
        P("tp", ("fsdp", "ctx")),
        P(),
        P(),
        P(),
        P(("fsdp", "ctx"), "tp"),
        P("tp"),
        P("tp", ("fsdp", "ctx")),
        P(),
        P(),
        P(),
    )
    return jax.shard_map(body, mesh=mesh, in_specs=in_specs, out_specs=out_specs, check_vma=False)
```

profile of v0, /device:TPU:1, one launch (start us, length us, event | category | flops | bytes accessed | tf_op | source)
XLA Modules:
  0.0 1002.2 jit_solution(7115701397755225684)
XLA Ops:
  9.1 10.9 %all_gather.31 = bf16[768,192]{1,0:T(8,128)(2,1)S(1)} all-gather(bf16[96,192]{1,0:T(8,128)(2,1)S(1)} %convert_element_type.109), channel_id=1, replica_groups=mesh['fsdp'=2,'ctx'=4,'tp'=4] {'fsdp','ctx'}, dimensions={0}, use_global_device_ids=true | all-gather | bytes 331776 | tf_op jit(solution)/shard_map/all_gather | solution.py:128
  24.1 9.6 all_gather.33
  36.4 9.2 all_gather.30
  47.3 9.7 all_gather.35
  57.1 9.3 all-gather.7.cloned.1.call-done
  66.4 43.0 %while.28 = (s32[]{:T(128)}, bf16[2,3,512,64]{2,3,1,0:T(8,128)(2,1)S(1)}, f32[2,3,512,1]{2,1,3,0:T(4,128)S(1)}, f32[2,3,512,1]{2,1,3,0:T(4,128)S(1)}, s32[2,512]...) while((s32[]{:T(128)}, ...), condition=%wide.region_3.4_spmd, body=%wide.region_0.3_spmd.sunk | while | flops 844198912 | bytes 50301076 | solution.py:152
  67.1 7.1 fusion.131
  74.2 6.9 fusion.132
  81.1 6.8 fusion.133
  88.6 7.1 fusion.131
  95.7 6.9 fusion.132
  102.6 6.8 fusion.133
  110.8 2.3 fusion.77
  114.7 119.2 %all-reduce.6.cloned.1.call-done = f32[1024,768]{1,0:T(8,128)} async-done(((f32[1024,768]{1,0:T(8,128)}), f32[1024,768]{1,0:T(8,128)}) %all-reduce.6.cloned.1.call-update) | async-done | bytes 3145744 | tf_op jit(solution)/shard_map/psum | solution.py:34
  233.9 2.8 fusion.73
  238.5 5.2 multiply_convert_fusion.1
  243.7 4.9 fusion.78
  248.8 2.7 convert_reduce_fusion
  252.2 116.7 %all-reduce.8.cloned.1.call-done = f32[1024,768]{1,0:T(8,128)} async-done(((f32[1024,768]{1,0:T(8,128)}), f32[1024,768]{1,0:T(8,128)}) %all-reduce.8.cloned.1.call-update) | async-done | bytes 3145744 | tf_op jit(solution)/shard_map/psum | solution.py:34
  368.8 2.9 fusion.72
  375.0 3.3 convert_reduce_fusion.1
  378.3 2.9 convert_reduce_fusion.2
  382.4 3.1 fusion.79
  385.5 120.2 %all-reduce.10.cloned.1.call-done = f32[1024,768]{1,0:T(8,128)} async-done(((f32[1024,768]{1,0:T(8,128)}), f32[1024,768]{1,0:T(8,128)}) %all-reduce.10.cloned.1.call-update) | async-done | bytes 3145744 | tf_op jit(solution)/shard_map/psum | solution.py:34
  505.7 4.9 multiply_reduce_fusion.1
  516.0 51.1 %while.29 = (s32[]{:T(128)}, bf16[2,3,512,64]{2,3,1,0:T(8,128)(2,1)}, bf16[2,3,2048,64]{2,3,1,0:T(8,128)(2,1)}, bf16[2,3,2048,64]{2,3,1,0:T(8,128)(2,1)}, s32[2,...) while((s32[]{:T(128)}, ...), condition=%wide.region_17.18_spmd, body=%wide.region_15.17_spmd.sunk | while | flops 2046360064 | bytes 189550000 | solution.py:197
  519.4 3.0 fusion.142
  522.4 7.7 multiply_reduce_fusion.7
  530.2 5.6 multiply_convert_fusion.3
  544.8 3.0 fusion.142
  547.8 7.7 multiply_reduce_fusion.7
  555.5 5.6 multiply_convert_fusion.3
  574.0 20.5 %reduce-scatter.17.cloned.1.call-done = bf16[2,3,512,64]{2,3,1,0:T(8,128)(2,1)} async-done(((bf16[2,3,2048,64]{2,3,1,0:T(8,128)(2,1)}), bf16[2,3,512,64]{2,3,1,0:T(8,128)(2,1)}) %reduce-scatter.17.cloned.1.call-update) | async-done | bytes 393232 | tf_op jit(solution)/shard_map/reduce_scatter | solution.py:202
  596.7 28.7 %reduce-scatter.19.cloned.1.call-done = bf16[2,3,512,64]{2,3,1,0:T(8,128)(2,1)} async-done(((bf16[2,3,2048,64]{2,3,1,0:T(8,128)(2,1)}), bf16[2,3,512,64]{2,3,1,0:T(8,128)(2,1)}) %reduce-scatter.19.cloned.1.call-update) | async-done | bytes 393232 | tf_op jit(solution)/shard_map/reduce_scatter | solution.py:205
  628.6 3.4 add_add_fusion
  632.2 5.5 fusion.68
  637.8 4.7 fusion.74
  642.5 2.1 convolution_bitcast_fusion.3
  649.0 2.4 copy.67
  652.9 10.4 %reduce-scatter.31.cloned.1.call-done = f32[96,192]{1,0:T(8,128)} async-done(((f32[768,192]{1,0:T(8,128)}), f32[96,192]{1,0:T(8,128)}) %reduce-scatter.31.cloned.1.call-update) | async-done | bytes 73744
  666.1 22.6 %all-reduce = (f32[192]{0:T(256)}, f32[192]{0:T(256)}, f32[768]{0:T(1024)}, f32[768]{0:T(1024)}, f32[768]{0:T(1024)}, /*index=5*/f32[768]{0:T(1024)}, f32[768]{0:T(1024)}, f32[768]{0:T(1024)}, f32[768]{0:T(1024)}) all-reduce(f32[192]{0:T(256)S(1)} %reduce_sum.184, ...), channel_id=1, replica_groups=mesh['fsdp'=2,'ctx'=4,'tp'=4] {'fsdp','ctx'}, use_global_device_ids=true, to_apply=%region_23.24 | all-reduce | flops 5760 | bytes 46080 | tf_op jit(solution)/shard_map/psum | solution.py:233
  688.7 98.3 %all-reduce.12.cloned.1.call-done = f32[1024,768]{1,0:T(8,128)} async-done(((f32[1024,768]{1,0:T(8,128)}), f32[1024,768]{1,0:T(8,128)}) %all-reduce.12.cloned.1.call-update) | async-done | bytes 3145744 | tf_op jit(solution)/shard_map/psum | solution.py:34
  787.0 3.3 add_convert_fusion
  790.4 42.0 %reduce-scatter.23.cloned.1.call-done = f32[768,96]{0,1:T(8,128)} async-done(((f32[768,768]{0,1:T(8,128)}), f32[768,96]{0,1:T(8,128)}) %reduce-scatter.23.cloned.1.call-update) | async-done | bytes 294928 | tf_op jit(solution)/shard_map/reduce_scatter | solution.py:231
  832.4 46.8 %reduce-scatter.21.cloned.1.call-done = f32[96,768]{1,0:T(8,128)} async-done(((f32[768,768]{1,0:T(8,128)}), f32[96,768]{1,0:T(8,128)}) %reduce-scatter.21.cloned.1.call-update) | async-done | bytes 294928 | tf_op jit(solution)/shard_map/reduce_scatter | solution.py:229
  879.2 38.3 %reduce-scatter.25.cloned.1.call-done = f32[96,192]{1,0:T(8,128)} async-done(((f32[768,192]{1,0:T(8,128)}), f32[96,192]{1,0:T(8,128)}) %reduce-scatter.25.cloned.1.call-update) | async-done | bytes 73744
  917.5 38.7 %reduce-scatter.29.cloned.1.call-done = f32[96,192]{1,0:T(8,128)} async-done(((f32[768,192]{1,0:T(8,128)}), f32[96,192]{1,0:T(8,128)}) %reduce-scatter.29.cloned.1.call-update) | async-done | bytes 73744
  956.2 38.6 %reduce-scatter.27.cloned.1.call-done = f32[96,192]{1,0:T(8,128)} async-done(((f32[768,192]{1,0:T(8,128)}), f32[96,192]{1,0:T(8,128)}) %reduce-scatter.27.cloned.1.call-update) | async-done | bytes 73744
  (250 shorter events, 65.1 us)
Async XLA Ops:
  8.0 26.4 %copy-start.3 = (bf16[2,512,768]{2,1,0:T(8,128)(2,1)S(1)}, bf16[2,512,768]{2,1,0:T(8,128)(2,1)}, u32[]{:S(2)}) copy-start(bf16[2,512,768]{2,1,0:T(8,128)(2,1)} %param.22) | copy-start | bytes 4718596
  8.0 16.0 %copy-start.36 = (f32[96,192]{1,0:T(8,128)S(1)}, f32[96,192]{1,0:T(8,128)}, u32[]{:S(2)}) copy-start(f32[96,192]{1,0:T(8,128)} %param.27) | copy-start | bytes 221188
  8.0 26.3 %copy-start.51 = (f32[192]{0:T(256)S(1)}, f32[192]{0:T(256)}, u32[]{:S(2)}) copy-start(f32[192]{0:T(256)} %param.28) | copy-start | bytes 2308
  8.1 49.0 %all-gather.5.cloned.1.call-start = ((), (), s32[]{:S(2)}) async-start(), calls=%async_computation.8 | async-start | bytes 1966080 | tf_op jit(solution)/shard_map/all_gather | solution.py:148
  23.2 13.1 %copy-start.37 = (f32[96,192]{1,0:T(8,128)S(1)}, f32[96,192]{1,0:T(8,128)}, u32[]{:S(2)}) copy-start(f32[96,192]{1,0:T(8,128)} %param.24) | copy-start | bytes 221188
  23.2 13.1 %copy-start.38 = (f32[192,96]{1,0:T(8,128)S(1)}, f32[192,96]{1,0:T(8,128)}, u32[]{:S(2)}) copy-start(f32[192,96]{1,0:T(8,128)} %param.29) | copy-start | bytes 221188
  24.0 22.3 %copy-start.52 = (f32[192]{0:T(256)S(1)}, f32[192]{0:T(256)}, u32[]{:S(2)}) copy-start(f32[192]{0:T(256)} %param.25) | copy-start | bytes 2308
  24.0 42.4 %all-gather.7.cloned.1.call-start = ((), (), s32[]{:S(2)}) async-start(), calls=%async_computation.9 | async-start | bytes 1966080 | tf_op jit(solution)/shard_map/all_gather | solution.py:149
  35.4 21.7 %copy-start.27 = (s32[2,2048]{1,0:T(2,128)S(1)}, s32[2,2048]{1,0:T(2,128)}, u32[]{:S(2)}) copy-start(s32[2,2048]{1,0:T(2,128)} %param.23) | copy-start | bytes 49156
  36.2 197.7 %all-reduce.6.cloned.1.call-start = ((), (), s32[]{:S(2)}) async-start(), calls=%async_computation.10 | async-start | bytes 6291456 | tf_op jit(solution)/shard_map/psum | solution.py:34
  74.2 6.9 copy-start.11
  95.7 6.9 copy-start.11
  109.4 3.7 copy-start.12
  109.4 3.7 copy-start.34
  109.4 3.7 copy-start.35
  113.1 125.4 %all-gather.9.cloned.1.call-start = ((), (), s32[]{:S(2)}) async-start(), calls=%async_computation.11 | async-start | bytes 1327104 | tf_op jit(solution)/shard_map/all_gather | solution.py:130
  113.9 129.8 %all-gather.11.cloned.1.call-start = ((), (), s32[]{:S(2)}) async-start(), calls=%async_computation.12 | async-start | bytes 1327104 | tf_op jit(solution)/shard_map/all_gather | solution.py:132
  114.7 254.1 %all-reduce.8.cloned.1.call-start = ((), (), s32[]{:S(2)}) async-start(), calls=%async_computation.13 | async-start | bytes 6291456 | tf_op jit(solution)/shard_map/psum | solution.py:34
  236.8 273.9 %copy-start.1 = (f32[1024,768]{1,0:T(8,128)}, f32[1024,768]{1,0:T(8,128)S(1)}, u32[]{:S(2)}) copy-start(f32[1024,768]{1,0:T(8,128)S(1)} %get-tuple-element.254) | copy-start | bytes 9437188
  248.6 257.2 %all-reduce.10.cloned.1.call-start = ((), (), s32[]{:S(2)}) async-start(), calls=%async_computation.14 | async-start | bytes 6291456 | tf_op jit(solution)/shard_map/psum | solution.py:34
  378.3 4.1 copy-start.53
  385.5 209.0 %reduce-scatter.17.cloned.1.call-start = ((), (), s32[]{:S(2)}) async-start(), calls=%async_computation.15 | async-start | bytes 1966080 | tf_op jit(solution)/shard_map/reduce_scatter | solution.py:202
  505.7 4.9 copy-start.32
  505.7 4.9 copy-start.39
  505.7 4.9 copy-start.41
  522.4 7.8 copy-start
  530.2 5.6 copy-start.23
  547.8 7.8 copy-start
  555.5 5.6 copy-start.23
  567.1 58.3 %reduce-scatter.19.cloned.1.call-start = ((), (), s32[]{:S(2)}) async-start(), calls=%async_computation.16 | async-start | bytes 1966080 | tf_op jit(solution)/shard_map/reduce_scatter | solution.py:205
  567.9 95.4 %reduce-scatter.31.cloned.1.call-start = ((), (), s32[]{:S(2)}) async-start(), calls=%async_computation.23 | async-start | bytes 884736
  572.0 215.0 %all-reduce.12.cloned.1.call-start = ((), (), s32[]{:S(2)}) async-start(), calls=%async_computation.17 | async-start | bytes 6291456 | tf_op jit(solution)/shard_map/psum | solution.py:34
  632.0 5.7 copy-start.2
  632.1 5.7 copy-start.33
  632.1 5.7 copy-start.40
  632.1 5.7 copy-start.42
  632.1 5.7 copy-start.50
  632.1 200.3 %reduce-scatter.23.cloned.1.call-start = ((), (), s32[]{:S(2)}) async-start(), calls=%async_computation.19 | async-start | bytes 2654208 | tf_op jit(solution)/shard_map/reduce_scatter | solution.py:231
  637.7 241.6 %reduce-scatter.21.cloned.1.call-start = ((), (), s32[]{:S(2)}) async-start(), calls=%async_computation.18 | async-start | bytes 2654208 | tf_op jit(solution)/shard_map/reduce_scatter | solution.py:229
  642.5 275.0 %reduce-scatter.25.cloned.1.call-start = ((), (), s32[]{:S(2)}) async-start(), calls=%async_computation.20 | async-start | bytes 884736
  645.8 310.4 %reduce-scatter.29.cloned.1.call-start = ((), (), s32[]{:S(2)}) async-start(), calls=%async_computation.22 | async-start | bytes 884736
  646.4 5.0 copy-start.17
  647.6 18.5 %copy-start.44 = (f32[768]{0:T(1024)S(1)}, f32[768]{0:T(1024)}, u32[]{:S(2)}) copy-start(f32[768]{0:T(1024)} %get-tuple-element.246) | copy-start | bytes 9220
  647.6 18.5 %copy-start.45 = (f32[768]{0:T(1024)S(1)}, f32[768]{0:T(1024)}, u32[]{:S(2)}) copy-start(f32[768]{0:T(1024)} %get-tuple-element.187) | copy-start | bytes 9220
  647.6 18.5 %copy-start.46 = (f32[768]{0:T(1024)S(1)}, f32[768]{0:T(1024)}, u32[]{:S(2)}) copy-start(f32[768]{0:T(1024)} %get-tuple-element.192) | copy-start | bytes 9220
  647.6 18.5 %copy-start.48 = (f32[768]{0:T(1024)S(1)}, f32[768]{0:T(1024)}, u32[]{:S(2)}) copy-start(f32[768]{0:T(1024)} %get-tuple-element.193) | copy-start | bytes 9220
  647.6 347.2 %reduce-scatter.27.cloned.1.call-start = ((), (), s32[]{:S(2)}) async-start(), calls=%async_computation.21 | async-start | bytes 884736
  649.0 138.1 %copy-start.7 = (f32[1024,768]{1,0:T(8,128)S(1)}, f32[1024,768]{1,0:T(8,128)}, u32[]{:S(2)}) copy-start(f32[1024,768]{1,0:T(8,128)} %copy-done.5) | copy-start | bytes 9437188
  (36 other events, 69.8 us)
Sparse Core Ops, SparseCore 0:
  24.1 20.4 all-gather.4
  46.8 19.5 all-gather.6
  113.2 120.6 all-reduce.5
  248.7 120.0 all-reduce.7
  385.6 120.0 all-reduce.9
  567.2 27.2 reduce-scatter.16
  597.2 28.1 reduce-scatter.18
  628.5 34.6 reduce-scatter.30
  665.6 121.3 all-reduce.11
  790.8 41.5 reduce-scatter.22
  836.7 42.4 reduce-scatter.20
  882.8 34.6 reduce-scatter.24
  921.2 34.9 reduce-scatter.28
  959.8 34.9 reduce-scatter.26
Sparse Core Ops, SparseCore 1:
  116.1 23.9 all-gather.8
  142.4 23.9 all-gather.10
where the time goes:
time: 1010 us; the launch traced here: 1000 us
  waiting for transfers between devices  729 us (72%)
  matrix products  103 us (10%)
  blocking collectives  62 us (6%)
  other arithmetic  59 us (6%)
  local copies, waits for them, and re-layouts  31.5 us (3%)
  between operations  16.2 us (2%)
    psum x4, waiting for transfers between devices, head_total(): return lax.psum(partial_value, 'tp')  454 us
    unnamed x20, waiting for transfers between devices  127 us
    reduce_scatter x1, waiting for transfers between devices, body(): lax.psum_scatter(grad_up_weight, ('fsdp', 'ctx'), scatter_dimension=0, ti...  46.8 us
    reduce_scatter x1, waiting for transfers between devices, body(): lax.psum_scatter(grad_down_weight, ('fsdp', 'ctx'), scatter_dimension=1,...  42 us
    dot_general x4, matrix products, scores_of(): jnp.einsum('hqd,hkd->hqk', query_seq, key_seq, preferred_element_type=jnp...  29.7 us
    reduce_scatter x1, waiting for transfers between devices, body(): lax.psum_scatter(grad_value_part.astype(jnp.bfloat16), 'ctx', scatter_dim...  28.7 us
    psum x1, blocking collectives, body(): lax.psum((grad_query_bias, grad_value_bias, grad_output_bias, grad_first_...  22.6 us
    reduce_scatter x1, waiting for transfers between devices, body(): lax.psum_scatter(grad_key_part.astype(jnp.bfloat16), 'ctx', scatter_dimen...  20.5 us
  transfers between devices with their start and end apart: 16, of which 13 were waited for; matrix products, arithmetic and copies ran while one was open for 6% of the time, Pallas kernels for 0%

commit v1 on v0

v1 whole, which is shorter than its diff:
```python
import functools

import jax
import jax.numpy as jnp
from jax import lax
from jax.experimental import pallas as pl
from jax.experimental.pallas import tpu as pltpu
from jax.sharding import Mesh
from jax.sharding import PartitionSpec as P

DH = 64
EPSILON = 1e-05
MASKED = -1e30
ROOT_HALF = 0.7071067811865476
ROOT_TWO_PI = 2.5066282746310002
LOW = jnp.bfloat16
WIDE = jnp.float32
VMEM = pltpu.VMEM
TILE = 256

K_AT = ((0, 0), (0, 1), (1, 0))
V_AT = ((1, 1), (2, 0), (2, 1))
Q_AT = ((0, 0), (0, 1), (1, 0))
O_AT = ((0, 1), (1, 0), (1, 1))


def nn(left, right):
    return jnp.dot(left, right, preferred_element_type=WIDE)


def nt(left, right):
    return lax.dot_general(left, right, (((1,), (1,)), ((), ())), preferred_element_type=WIDE)


def tn(left, right):
    return lax.dot_general(left, right, (((0,), (0,)), ((), ())), preferred_element_type=WIDE)


def lanes(group):
    return slice(group * 128, (group + 1) * 128)


def fold(block):
    return jnp.sum(block.reshape(-1, 8, block.shape[-1]), axis=0)


def half_mask(block, upper):
    place = lax.broadcasted_iota(jnp.int32, block.shape, 1)
    keep = (place >= DH) if upper else (place < DH)
    return jnp.where(keep, block, jnp.zeros_like(block))


def forward_kernel(flags, q_ref, kv_ref, docs_q, docs_k, o_ref, lse_ref, qm, top, total, acc, held):
    active = Active(flags)
    rows = q_ref.shape[0]
    chunks = kv_ref.shape[0] // TILE
    for part in range(2):
        for head in range(3):
            group, upper = Q_AT[head]
            qm[part * 3 + head] = half_mask(q_ref[:, lanes(part * 2 + group)], upper)
    for tile in range(rows // TILE):
        across = slice(tile * TILE, (tile + 1) * TILE)
        top[...] = jnp.full_like(top, MASKED)
        total[...] = jnp.zeros_like(total)
        acc[...] = jnp.zeros_like(acc)

        def score(c, carry):
            @pl.when(active[tile, c] == 1)
            def _():
                down = pl.ds(pl.multiple_of(c * TILE, TILE), TILE)
                same = docs_k[down, :] == docs_q[:, across]
                for at in range(6):
                    keys = kv_ref[down, lanes(at // 3 * 3 + K_AT[at % 3][0])]
                    block = jnp.where(same, nt(keys, qm[at, across, :]), MASKED)
                    held[at, down, :] = block
                    most = jnp.max(block.reshape(-1, 8, TILE), axis=0)
                    top[at] = jnp.maximum(top[at], most)

            return carry

        lax.fori_loop(0, chunks, score, 0)
        for at in range(6):
            top[at] = jnp.broadcast_to(jnp.max(top[at], axis=0, keepdims=True), (8, TILE))

        def mix(c, carry):
            @pl.when(active[tile, c] == 1)
            def _():
                down = pl.ds(pl.multiple_of(c * TILE, TILE), TILE)
                for part in range(2):
                    turned = {g: kv_ref[down, lanes(part * 3 + g)].T for g in (1, 2)}
                    for head in range(3):
                        at = part * 3 + head
                        power = jnp.exp(held[at, down, :] - top[at, 0:1, :])
                        total[at] = total[at] + jnp.sum(power.reshape(-1, 8, TILE), axis=0)
                        group, upper = V_AT[head]
                        values = turned[group][upper * DH : upper * DH + DH, :]
                        span = slice(at * DH, at * DH + DH)
                        acc[span, :] = acc[span, :] + nn(values, power.astype(LOW))

            return carry

        lax.fori_loop(0, chunks, mix, 0)
        sums = [jnp.sum(total[at], axis=0, keepdims=True) for at in range(6)]
        for at in range(6):
            lse_ref[at : at + 1, across] = top[at, 0:1, :] + jnp.log(sums[at])
        lse_ref[6:8, across] = jnp.zeros((2, TILE), WIDE)
        for part in range(2):
            mixed = [
                acc[(part * 3 + head) * DH : (part * 3 + head + 1) * DH, :]
                / sums[part * 3 + head]
                for head in range(3)
            ]
            first = jnp.concatenate([jnp.zeros_like(mixed[0]), mixed[0]], axis=0)
            second = jnp.concatenate([mixed[1], mixed[2]], axis=0)
            o_ref[across, lanes(part * 2)] = first.T.astype(LOW)
            o_ref[across, lanes(part * 2 + 1)] = second.T.astype(LOW)


def backward_kernel(
    stage, active, spot, q_ref, kv_ref, docs_q, docs_k, o_ref, go_ref, lse_ref, wkv_ref, *refs
):
    if stage == 0:
        dq_out, dkv_ref, near_ref, far_ref, sum_ref = refs[:5]
    elif stage == 1:
        dq_in, dq_out, dkv_ref, near_ref, sum_ref = refs[:5]
    else:
        dq_in, wq_ref, extra_ref, block_a, dq_ref, dkv_ref, near_ref, far_ref, sum_ref, sum_q = (
            refs[:10]
        )
    qm, gm, along, dq_acc, dkv_acc, grads_acc = refs[-6:]
    sum_ref[...] = jnp.zeros_like(sum_ref)
    rows = q_ref.shape[0]
    chunks = dkv_ref.shape[0] // TILE
    first_tile = (4, 0, 2)[stage]
    for part in range(2):
        for head in range(3):
            at = part * 3 + head
            group, upper = Q_AT[head]
            qm[at] = half_mask(q_ref[:, lanes(part * 2 + group)], upper)
            group, upper = O_AT[head]
            gm[at] = half_mask(go_ref[:, lanes(part * 2 + group)], upper)
        for tile in range(rows // TILE):
            across = slice(tile * TILE, (tile + 1) * TILE)
            for group in range(2):
                both = (
                    go_ref[across, lanes(part * 2 + group)].astype(WIDE)
                    * o_ref[across, lanes(part * 2 + group)].astype(WIDE)
                ).T
                for head in range(3):
                    if O_AT[head][0] == group:
                        upper = O_AT[head][1]
                        at = part * 3 + head
                        along[at : at + 1, across] = jnp.sum(
                            both[upper * DH : upper * DH + DH, :], axis=0, keepdims=True
                        )
    dq_acc[...] = dq_in[...] if stage else jnp.zeros_like(dq_acc)

    def chunk(c, carry):
        here = down = pl.ds(pl.multiple_of(c * TILE, TILE), TILE)
        number = first_tile + c
        dkv_acc[...] = jnp.zeros_like(dkv_acc)
        for tile in range(rows // TILE):
            across = slice(tile * TILE, (tile + 1) * TILE)

            @pl.when(active[tile, number] == 1)
            def _():
                same = docs_k[down, :] == docs_q[:, across]
                for part in range(2):
                    turned = {g: kv_ref[down, lanes(part * 3 + g)].T for g in (0, 1)}
                    for head in range(3):
                        at = part * 3 + head
                        group, upper = K_AT[head]
                        of_k, of_v = lanes(part * 3 + group), lanes(part * 3 + V_AT[head][0])
                        queries, grads = qm[at, across, :], gm[at, across, :]
                        score = nt(kv_ref[down, of_k], queries)
                        weight = jnp.where(
                            same, jnp.exp(score - lse_ref[at : at + 1, across]), 0.0
                        )
                        pull = nt(kv_ref[down, of_v], grads)
                        slope = (weight * (pull - along[at : at + 1, across])).astype(LOW)
                        dkv_acc[:, of_k] += nn(slope, queries)
                        dkv_acc[:, of_v] += nn(weight.astype(LOW), grads)
                        keys = turned[group][upper * DH : upper * DH + DH, :]
                        dq_acc[at * DH : at * DH + DH, across] += nn(keys, slope)

        dkv = dkv_acc[...].astype(LOW)
        dkv_ref[here, :] = dkv
        grads_acc[here, :] = nt(dkv, wkv_ref[...])
        sum_ref[...] += fold(dkv.astype(WIDE))
        return carry

    lax.fori_loop(0, chunks, chunk, 0)
    if stage == 2:
        scale = 1.0 / DH**0.5
        for part in range(2):
            for tile in range(rows // TILE):
                across = slice(tile * TILE, (tile + 1) * TILE)
                at = part * 3 * DH
                first = dq_acc[at : at + 2 * DH, across] * scale
                second = dq_acc[at + 2 * DH : at + 3 * DH, across] * scale
                second = jnp.concatenate([second, jnp.zeros_like(second)], axis=0)
                dq_ref[across, lanes(part * 2)] = first.T.astype(LOW)
                dq_ref[across, lanes(part * 2 + 1)] = second.T.astype(LOW)
        sum_q[...] = fold(dq_ref[...].astype(WIDE))
        half = rows // 2
        k, l = spot[0], spot[1]
        own = pl.ds(pl.multiple_of(k * half, half), half)
        peer = pl.ds(pl.multiple_of((1 - k) * half, half), half)
        near_ref[...] = block_a[...]
        for flag, target in ((True, near_ref), (False, grads_acc)):
            @pl.when((k == l) == flag)
            def _():
                target[own, :] += nt(dq_ref[:half, :], wq_ref[...]) + extra_ref[...]
                target[peer, :] += nt(dq_ref[half:, :], wq_ref[...])
        far_ref[...] = grads_acc[...].astype(LOW)
    else:
        dq_out[...] = dq_acc[...]
        near_ref[...] = grads_acc[:rows, :]
        if stage == 0:
            far_ref[...] = grads_acc[rows:, :].astype(LOW)


class Order:
    def __init__(self):
        self.last = ()

    def __call__(
        self, kernel, name, scalars, arrays, outs, scratch=(), limit=6, far=(False, False), after=(), hbm=False
    ):
        whole = pl.BlockSpec(memory_space=VMEM)
        outside = pl.BlockSpec(memory_space=pltpu.HBM)
        waits = tuple(self.last) + tuple(after)
        count, untouched = len(arrays), len(waits)
        far_in = far[0] if isinstance(far[0], tuple) else (far[0],) * count
        far_out = far[1] if isinstance(far[1], tuple) else (far[1],) * len(outs)
        held = [VMEM(a.shape, a.dtype) for a, out in zip(arrays, far_in) if out]
        held += [VMEM(shape, kind) for (shape, kind), out in zip(outs, far_out) if out]
        if held:
            held.append(pltpu.SemaphoreType.DMA((len(held),)))

        def run(*refs):
            scalar, ins = refs[0], list(refs[1 : 1 + count])
            results = list(refs[1 + count + untouched : 1 + count + untouched + len(outs)])
            rest = list(refs[1 + count + untouched + len(outs) :])
            extra = rest[len(rest) - len(held) :] if held else []
            rest = rest[: len(rest) - len(held)]
            sem, at, copies = (extra[-1] if held else None), 0, []
            for i, ref in enumerate(ins):
                if far_in[i]:
                    copies.append(pltpu.make_async_copy(ref, extra[at], sem.at[at]))
                    ins[i] = extra[at]
                    at += 1
            for copy in copies:
                copy.start()
            for copy in copies:
                copy.wait()
            copies = []
            for i, target in enumerate(results):
                if far_out[i]:
                    copies.append(pltpu.make_async_copy(extra[at], target, sem.at[at]))
                    results[i] = extra[at]
                    at += 1
            kernel(scalar, *ins, *results, *rest)
            for copy in copies:
                copy.start()
            for copy in copies:
                copy.wait()

        arrays = [
            pltpu.with_memory_space_constraint(a, pltpu.HBM) if out or hbm else a
            for a, out in zip(arrays, far_in)
        ]
        results = pl.pallas_call(
            run,
            out_shape=tuple(jax.ShapeDtypeStruct(shape, kind) for shape, kind in outs),
            in_specs=[pl.BlockSpec(memory_space=pltpu.SMEM)]
            + [outside if out or hbm else whole for out in far_in]
            + [pl.BlockSpec(memory_space=pl.ANY)] * untouched,
            out_specs=tuple(outside if out else whole for out in far_out),
            scratch_shapes=list(scratch) + held,
            compiler_params=pltpu.CompilerParams(vmem_limit_bytes=limit << 20),
            cost_estimate=pl.CostEstimate(flops=1, bytes_accessed=1, transcendentals=0),
            name=name,
        )(scalars, *arrays, *waits)
        self.last = (min(results, key=lambda r: r.size * r.dtype.itemsize),)
        return results


def attention_forward(call, flags, q, kv, docs_q, docs_k):
    rows = q.shape[0]
    return call(
        forward_kernel, "attend", flags, [q, kv, docs_q, docs_k],
        [((rows, 512), LOW), ((8, rows), WIDE)],
        [
            VMEM((6, rows, 128), LOW),
            VMEM((6, 8, TILE), WIDE),
            VMEM((6, 8, TILE), WIDE),
            VMEM((6 * DH, TILE), WIDE),
            VMEM((6, kv.shape[0], TILE), WIDE),
        ], 20,
    )


def attention_backward(call, stage, flags, arrays, more):
    q, kv, wkv = arrays[0], arrays[1], arrays[-1]
    rows, keys, width = q.shape[0], kv.shape[0], wkv.shape[0]
    part, part_low = ((rows, width), WIDE), ((rows, width), LOW)
    dq_out = ((rows, 512), LOW) if stage == 2 else ((6 * DH, rows), WIDE)
    outs = [dq_out, ((keys, 768), LOW), part]
    outs += [] if stage == 1 else [part_low]
    outs += [((8, 768), WIDE)]
    outs += [((8, 512), WIDE)] if stage == 2 else []

    def kernel(flags, *refs):
        backward_kernel(stage, Active(flags), flags, *refs)

    return call(
        kernel, ("attend_cd", "attend_a", "attend_b")[stage], flags, list(arrays) + list(more),
        outs,
        [
            VMEM((6, rows, 128), LOW),
            VMEM((6, rows, 128), LOW),
            VMEM((8, rows), WIDE),
            VMEM((6 * DH, rows), WIDE),
            VMEM((TILE, 768), WIDE),
            VMEM((keys, width), WIDE),
        ], 18,
        far=(
            (True, True, False, True, False, False, False, True)
            + tuple(i == 1 for i in range(len(more))),
            False,
        ),
    )


class Active:
    def __init__(self, flags):
        self.flags = flags

    def __getitem__(self, where):
        tile, number = where
        return self.flags[4 + tile * 8 + number]


def pick_kernel(spot, inputs, cotangent, block, beside, kept, sem):
    h, k = spot[2], spot[0]
    rows, half = block.shape[0], kept.shape[0]
    mine = pl.ds(pl.multiple_of(k * half, half), half)
    other = pl.ds(pl.multiple_of((1 - k) * half, half), half)
    copies = [
        pltpu.make_async_copy(inputs.at[h], block, sem.at[0]),
        pltpu.make_async_copy(cotangent.at[h, other], beside.at[rows : rows + half], sem.at[1]),
        pltpu.make_async_copy(cotangent.at[h, mine], kept, sem.at[2]),
    ]
    for copy in copies:
        copy.start()
    for copy in copies:
        copy.wait()
    beside[:rows] = block[...]


def own_kernel(spot, block, got, kept, own, peer, grad):
    k = spot[0]
    rows, half = block.shape[0], own.shape[0]
    mine = pl.ds(pl.multiple_of(k * half, half), half)
    other = pl.ds(pl.multiple_of((1 - k) * half, half), half)

    @pl.when(k == spot[1])
    def _():
        own[...] = block[mine, :]
        peer[...] = block[other, :]
        grad[...] = kept[...]

    @pl.when(k != spot[1])
    def _():
        own[...] = got[mine, :]
        peer[...] = got[other, :]
        grad[...] = got[rows:, :]


def pack_kernel(_, key, value, query, bias, down, own_a, own_d):
    count = key.shape[0]
    own_a[0:16, :] = bias[...].astype(LOW)
    body = jnp.concatenate(
        [key[...], value[...], query[...], jnp.zeros((count, DH), WIDE)], axis=1
    )
    own_a[16 : 16 + count, :] = body.astype(LOW)
    own_d[...] = down[...].astype(LOW)


def pack_uo_kernel(_, up, output, own_uo):
    count, hidden = up.shape
    own_uo[:, :hidden] = up[...].astype(LOW)
    turned = jnp.concatenate([jnp.zeros((count, DH), WIDE), output[...].T], axis=1)
    own_uo[:, hidden : hidden + 256] = turned.astype(LOW)
    own_uo[:, hidden + 256 :] = jnp.zeros((count, own_uo.shape[1] - hidden - 256), LOW)


def spread_kernel(spot, mine, got, out, bias):
    count = out.shape[2]
    l, h = spot[1], spot[2]
    for part, ql in ((mine, l), (got, 1 - l)):
        for a in range(2):
            out[h ^ a, ql] = part[a, 16 : 16 + count, :]
        bias[ql] = part[0, 0:16, :]


def project_kernel(where, *refs):
    parts, (a, b, c, d, own, peer, kv_bias, q_bias) = refs[:4], refs[4:12]
    kv, q, wkv, wq, far_a, far_b, far_cd, far_q = refs[12:20]
    for i, part in enumerate(parts):
        for row in range(2):
            for ql in range(2):
                at_kv, at_q = slice(ql * 384, ql * 384 + 384), slice(ql * 256, ql * 256 + 256)
                wkv[where[i], row, :, at_kv] = part[row, ql, :, 0:384]
                wq[where[i], row, :, at_q] = part[row, ql, :, 384:640]
    width = 8 * wkv.shape[2]
    of_kv, of_q = wkv[...].reshape(width, 768), wq[...].reshape(width, 512)
    rows = a.shape[0]
    for i, block in enumerate((a, b, c, d)):
        part = (nn(block[:rows, :], of_kv) + kv_bias[...]).astype(LOW)
        kv[i * rows : (i + 1) * rows, :] = part
        target = (far_a, far_b, far_cd, far_cd)[i]
        start = rows if i == 3 else 0
        target[start : start + rows, :] = part
    half, scale = rows // 2, jnp.asarray(1.0 / DH**0.5, LOW)
    for i, block in enumerate((own, peer)):
        part = (nn(block[...], of_q) + q_bias[...]).astype(LOW) * scale
        q[i * half : (i + 1) * half, :] = part
        far_q[i * half : (i + 1) * half, :] = part


def copy_kernel(_, source, out):
    out[...] = source[...]


def give_kernel(spot, gathered, out):
    for i in range(2):
        out[i] = gathered[2 * (1 - spot[0]) + i, :, : out.shape[2]]


def give_groups_kernel(spot, gathered, out):
    for i in range(2):
        out[i] = gathered[2 * (1 - spot[0]) + i]


def two_halves(result, own, peer):
    half = own.shape[0]
    own[...] = result[:half]
    peer[...] = result[half:].astype(LOW)


def branch_kernel(where, *refs):
    parts, o, (wu, wo, own, peer) = refs[:4], refs[4], refs[5:9]
    for i, part in enumerate(parts):
        for row in range(2):
            for ql in range(2):
                at_u, at_o = slice(ql * 768, ql * 768 + 768), slice(ql * 256, ql * 256 + 256)
                wu[where[i], row, :, at_u] = part[row, ql, :, 0:768]
                wo[where[i], row, :, at_o] = part[row, ql, :, 768:1024]
    two_halves(nt(o[...], wo[...].reshape(8 * wo.shape[2], 512)), own, peer)


def standard(resid):
    center = resid - jnp.mean(resid, axis=-1, keepdims=True)
    inverse = lax.rsqrt(jnp.mean(center * center, axis=-1, keepdims=True) + EPSILON)
    return center * inverse, inverse


def slope_of_norm(grad, normed, inverse, gain):
    scaled = grad * gain
    inner = (
        scaled
        - jnp.mean(scaled, axis=-1, keepdims=True)
        - normed * jnp.mean(scaled * normed, axis=-1, keepdims=True)
    )
    return inner * inverse


OUT_BIAS, GAIN_ONE, SHIFT_ONE, DOWN_BIAS, GAIN_TWO, SHIFT_TWO = range(6)


def row_of(params, i):
    return params[i : i + 1, :]


def norm_one_kernel(_, own, got, tokens, params, low, normed_ref, inverse_ref):
    branch = own[...] + got[...].astype(WIDE) + row_of(params, OUT_BIAS)
    normed, inverse = standard(tokens[...].astype(WIDE) + branch)
    normed_ref[...] = normed
    inverse_ref[...] = inverse
    low[...] = (normed * row_of(params, GAIN_ONE) + row_of(params, SHIFT_ONE)).astype(LOW)


def up_kernel(_, own, peer, wu, bias, act, slope):
    half = own.shape[0]
    step = 256
    for i, block in enumerate((own, peer)):
        rows = slice(i * half, (i + 1) * half)
        for c in range(0, wu.shape[1], step):
            columns = slice(c, c + step)
            upper = nn(block[...], wu[:, columns]) + bias[:, columns]
            share = 0.5 * (1.0 + lax.erf(upper * ROOT_HALF))
            act[rows, columns] = (upper * share).astype(LOW)
            slope[rows, columns] = share + upper * (
                jnp.exp(-0.5 * upper * upper) * (1.0 / ROOT_TWO_PI)
            )


def down_join_kernel(where, gathered, got, act, wd, own, peer):
    k = where[4]
    for i in range(4):
        for ql in range(2):
            columns = slice(ql * 768, ql * 768 + 768)
            wd[where[i], k, :, columns] = gathered[2 * k + ql, i]
            wd[where[i], 1 - k, :, columns] = got[ql, i]
    two_halves(nt(act[...], wd[...].reshape(8 * wd.shape[2], wd.shape[3])), own, peer)


def down_kernel(_, wd, act, own, peer):
    two_halves(nt(act[...], wd[...]), own, peer)


def norm_two_kernel(_, own, got, normed_one, params, cot, out, grad, low, sums):
    first = normed_one[...] * row_of(params, GAIN_ONE) + row_of(params, SHIFT_ONE)
    down = own[...] + got[...].astype(WIDE) + row_of(params, DOWN_BIAS)
    normed, inverse = standard(first + down)
    out[...] = (normed * row_of(params, GAIN_TWO) + row_of(params, SHIFT_TWO)).astype(LOW)
    given = cot[...].astype(WIDE)
    slope = slope_of_norm(given, normed, inverse, row_of(params, GAIN_TWO))
    grad[...] = slope
    e = slope.astype(LOW)
    low[...] = e
    sums[0] = fold(e.astype(WIDE))
    sums[1] = fold(given * normed)
    sums[2] = fold(given)


def units_kernel(_, own, peer, wd, wu, slope, units, out_own, out_peer, sums):
    half = own.shape[0]
    step = 256
    sums[...] = jnp.zeros_like(sums)
    for i, (block, out) in enumerate(((own, out_own), (peer, out_peer))):
        rows = slice(i * half, (i + 1) * half)
        for c in range(0, wd.shape[1], step):
            columns = slice(c, c + step)
            du = (nn(block[...], wd[:, columns]) * slope[rows, columns]).astype(LOW)
            units[rows, columns] = du
            sums[:, columns] += fold(du.astype(WIDE))
        out[...] = nt(units[rows, :], wu[...]).astype(out.dtype)


def norm_one_back_kernel(_, own, got, grad_two, normed_ref, inverse_ref, params, grad, low, sums):
    given = grad_two[...] + (own[...] + got[...].astype(WIDE))
    normed = normed_ref[...]
    slope = slope_of_norm(given, normed, inverse_ref[...], row_of(params, GAIN_ONE))
    grad[...] = slope
    e = slope.astype(LOW)
    low[...] = e
    sums[0] = fold(e.astype(WIDE))
    sums[1] = fold(given * normed)
    sums[2] = fold(given)


def mixed_grad_kernel(_, own, peer, wo, out):
    half = own.shape[0]
    out[:half, :] = nn(own[...], wo[...]).astype(LOW)
    out[half:, :] = nn(peer[...], wo[...]).astype(LOW)


def turn(lefts, turned):
    start = 0
    for left in lefts:
        for i in range(0, left.shape[0], 256):
            turned[:, start + i : start + i + 256] = left[i : i + 256, :].T
        start += left.shape[0]


RIDE = 16


def split_sum(value):
    high = value.astype(LOW)
    return high, (value - high.astype(WIDE)).astype(LOW)


def ride_of(block):
    half = RIDE // 2
    return block[:half].astype(WIDE) + block[half:RIDE].astype(WIDE)


def group_rows(me, i, count):
    return pl.ds(pl.multiple_of((me[0] ^ i) * count, 64), count)


def grad_d_kernel(me, own, peer, act, kept, sent, turned, whole):
    turn((own, peer), turned)
    for c in range(0, whole.shape[1], 256):
        whole[:, c : c + 256] = nn(turned[...], act[:, c : c + 256]).astype(LOW)
    count = whole.shape[0] // 4
    for i in range(2):
        kept[i * count : (i + 1) * count, :] = whole[group_rows(me, i, count), :]
        sent[i * count : (i + 1) * count, :] = whole[group_rows(me, i + 2, count), :]


def small_kernel(_, sums_one, sums_two, out):
    parts = [sums_one[i] for i in range(3)] + [sums_two[i] for i in range(3)]
    for i, part in enumerate(parts):
        out[i : i + 1, :] = jnp.sum(part, axis=0, keepdims=True)
    out[6:8, :] = jnp.zeros((2, out.shape[1]), WIDE)


def grad_uo_kernel(
    me, own, peer, units, eb_own, eb_peer, o, small, small_peer, sum_u, kept, sent, turned, whole
):
    turn((own, peer), turned)
    hidden = units.shape[1]
    for c in range(0, hidden, 256):
        whole[:, c : c + 256] = nn(turned[...], units[:, c : c + 256]).astype(LOW)
    turn((eb_own, eb_peer), turned)
    whole[:, hidden:] = nn(turned[...], o[...]).astype(LOW)
    count = whole.shape[0] // 4
    for j in range(2):
        kept[j * count : (j + 1) * count, :] = whole[group_rows(me, j, count), :]
        sent[j * count : (j + 1) * count, :] = whole[group_rows(me, j + 2, count), :]
    high, low = split_sum(small[...] + small_peer[...])
    units_high, units_low = split_sum(jnp.sum(sum_u[...], axis=0, keepdims=True))
    for out in (kept, sent):
        ride = out.at[2 * count : 2 * count + RIDE, :]
        ride[...] = jnp.zeros((RIDE, out.shape[1]), LOW)
        ride[0:8, 0:768] = high
        ride[8:16, 0:768] = low
        ride[6:7, 0:1536] = units_high
        ride[14:15, 0:1536] = units_low


def fold_d_kernel(_, kept, got, left, sent):
    count = left.shape[0]
    left[...] = (kept[:count].astype(WIDE) + got[:count].astype(WIDE)).astype(LOW)
    sent[...] = (kept[count:].astype(WIDE) + got[count:].astype(WIDE)).astype(LOW)


def fold_uo_kernel(_, kept, got, left, sent):
    count = left.shape[0] - RIDE
    left[:count] = (kept[:count].astype(WIDE) + got[:count].astype(WIDE)).astype(LOW)
    sent[:count] = (
        kept[count : 2 * count].astype(WIDE) + got[count : 2 * count].astype(WIDE)
    ).astype(LOW)
    high, low = split_sum(ride_of(kept[2 * count :]) + ride_of(got[2 * count :]))
    for out in (left, sent):
        out[count : count + RIDE // 2] = high
        out[count + RIDE // 2 :] = low


def by_quarter(flag, kept, sent, write):
    for ql in range(2):
        for out, other in ((kept, False), (sent, True)):
            @pl.when((flag == ql) != other)
            def _():
                write(out, ql)


def merge_d_kernel(spot, left, got, kept, sent):
    count = left.shape[0] // 2
    total = (left[...].astype(WIDE) + got[...].astype(WIDE)).astype(LOW)

    def write(out, ql):
        for row in range(2):
            out[row] = total[row * count : (row + 1) * count, ql * 768 : ql * 768 + 768]

    by_quarter(spot[1], kept, sent, write)


def fold_z_d_kernel(spot, kept, got, *outs):
    for row in range(2):
        total = (kept[row].astype(WIDE) + got[row].astype(WIDE)).astype(LOW)
        for a, out in enumerate(outs):
            @pl.when((spot[2] ^ a) == row)
            def _():
                out[...] = total


def merge_uo_kernel(spot, left, got, kept, sent):
    count = left.shape[0] // 2 - RIDE // 2
    total = (left[: 2 * count].astype(WIDE) + got[: 2 * count].astype(WIDE)).astype(LOW)
    high, low = split_sum(ride_of(left[2 * count :]) + ride_of(got[2 * count :]))

    def write(out, ql):
        for row in range(2):
            rows = slice(row * count, (row + 1) * count)
            out[row, :count, 0:768] = total[rows, ql * 768 : ql * 768 + 768]
            out[row, :count, 768:1024] = total[rows, 1536 + ql * 256 : 1792 + ql * 256]
            out[row, count : count + 8, 0:768] = high[:, 0:768]
            out[row, count : count + 8, 768:1024] = jnp.zeros((8, 256), LOW)
            out[row, count + 6 : count + 7, 0:768] = high[6:7, ql * 768 : ql * 768 + 768]
            out[row, count + 8 : count + 16, 0:768] = low[:, 0:768]
            out[row, count + 8 : count + 16, 768:1024] = jnp.zeros((8, 256), LOW)
            out[row, count + 14 : count + 15, 0:768] = low[6:7, ql * 768 : ql * 768 + 768]

    by_quarter(spot[1], kept, sent, write)


def merge_a_kernel(spot, *refs):
    parts, (kept, sent) = refs[:4], refs[4:6]
    count = kept.shape[1] - RIDE
    total = parts[0][...].astype(WIDE)
    ride = ride_of(parts[0][2 * count :])
    for part in parts[1:]:
        total = total + part[...].astype(WIDE)
        ride = ride + ride_of(part[2 * count :])
    total = total.astype(LOW)
    high, low = split_sum(ride)

    def write(out, ql):
        columns = slice(ql * 640, ql * 640 + 640)
        for row in range(2):
            out[row, :count, :] = total[row * count : (row + 1) * count, columns]
            out[row, count : count + 8, :] = high[:, columns]
            out[row, count + 8 : count + 16, :] = low[:, columns]

    by_quarter(spot[1], kept, sent, write)


def fold_z_kernel(spot, kept, got, *outs):
    count = kept.shape[1] - RIDE
    for row in range(2):
        total = (kept[row, :count].astype(WIDE) + got[row, :count].astype(WIDE)).astype(LOW)
        high, low = split_sum(ride_of(kept[row, count:]) + ride_of(got[row, count:]))
        for a, out in enumerate(outs):
            @pl.when((spot[2] ^ a) == row)
            def _():
                out[:count] = total
                out[count : count + 8] = high
                out[count + 8 :] = low


def shard_uo_kernel(_, d_one, d_two, one, two, down, up, output, shared):
    count = up.shape[0]
    down[...] = d_one[...].astype(WIDE) + d_two[...].astype(WIDE)
    total = one[:count].astype(WIDE) + two[:count].astype(WIDE)
    up[...] = total[:, 0:768]
    output[...] = total[:, 768 + DH : 1024].T
    ride = ride_of(one[count:]) + ride_of(two[count:])
    shared[...] = ride[:, 0:768]


def shard_a_kernel(_, one, two, key, value, query, sums):
    count, n = key.shape
    total = one[:count].astype(WIDE) + two[:count].astype(WIDE)
    key[...] = total[:, 0:n]
    value[...] = total[:, n : 2 * n]
    query[...] = total[:, 2 * n : 3 * n]
    sums[...] = ride_of(one[count:]) + ride_of(two[count:])


def pair_kernel(_, one, two, out):
    out[0] = one[...]
    out[1] = two[...]


def line_kernel(where, one, two, out):
    for i, ref in enumerate((one, two)):
        for j in range(2):
            out[i + 2 * j] = ref[j]


def output_kernel(where, mine, got, out):
    for a in range(2):
        out[where[2 * a], where[4]] = mine[a]
        out[where[2 * a], where[5]] = got[a]


def grad_qkv_kernel(
    me, a, b, c, d, own, peer, dkv_a, dkv_b, dkv_cd, dq, sum_q, sum_a, sum_b, sum_cd, *refs
):
    outs, turned, whole = refs[:4], refs[4], refs[5]
    rows = a.shape[0]
    turn((a, b.at[:rows], c, d, own, peer), turned)
    for ql in range(2):
        base = ql * 640
        kv = slice(ql * 384, ql * 384 + 384)
        whole[:, base : base + 384] = (
            nn(turned[:, :rows], dkv_a[:, kv])
            + nn(turned[:, rows : 2 * rows], dkv_b[:, kv])
            + nn(turned[:, 2 * rows : 4 * rows], dkv_cd[:, kv])
        ).astype(LOW)
        whole[:, base + 384 : base + 640] = nn(
            turned[:, 4 * rows :], dq[:, ql * 256 : ql * 256 + 256]
        ).astype(LOW)
    count = whole.shape[0] // 4
    of_q = jnp.sum(sum_q[...], axis=0, keepdims=True)
    of_kv = jnp.sum(sum_a[...] + sum_b[...] + sum_cd[...], axis=0, keepdims=True)
    sums = jnp.concatenate(
        [
            part
            for ql in range(2)
            for part in (of_kv[:, ql * 384 : ql * 384 + 384], of_q[:, ql * 256 : ql * 256 + 256])
        ],
        axis=1,
    )
    high, low = split_sum(sums)
    for i, out in enumerate(outs):
        out[:count, :] = whole[group_rows(me, i, count), :]
        out[count:, :] = jnp.zeros((RIDE, out.shape[1]), LOW)
        out[count : count + 1, :] = high
        out[count + 8 : count + 9, :] = low


def place_kernel(where, *refs):
    out = refs[-1]
    for i, piece in enumerate(refs[:-1]):
        out[where[2 * i], where[2 * i + 1]] = piece[...]


def sum_kernel(spot, near, got_b, got_c, kept, sent):
    total = near[...] + got_b[...].astype(WIDE) + got_c[...].astype(WIDE)
    half = kept.shape[0]
    lower = spot[1] == 0
    kept[...] = jnp.where(lower, total[:half], total[half:])
    sent[...] = jnp.where(lower, total[half:], total[:half]).astype(LOW)


def add_kernel(_, left, right, out):
    out[...] = (left[...].astype(WIDE) + right[...].astype(WIDE)).astype(out.dtype)


FLIP = [(0, 1), (1, 0)]


def flip(value, axis):
    return lax.ppermute(value, axis, FLIP)


def move(value, target):
    pairs = []
    for c in range(2):
        for h in range(2):
            for low in range(2):
                a, b, d = target(c, h, low)
                pairs.append((c * 4 + h * 2 + low, a * 4 + b * 2 + d))
    return lax.ppermute(value, ("cc", "th", "tl"), pairs)


BITS = ((0, 0), (0, 1), (1, 0), (1, 1))


def body(
    fsdp_size,
    inputs,
    segment_ids,
    query_weight,
    query_bias,
    key_weight,
    value_weight,
    value_bias,
    output_weight,
    output_bias,
    first_gain,
    first_shift,
    up_weight,
    up_bias,
    down_weight,
    down_bias,
    second_gain,
    second_shift,
    cotangent,
):
    f, x = lax.axis_index("fsdp"), lax.axis_index("cx")
    k, h, l = lax.axis_index("cc"), lax.axis_index("th"), lax.axis_index("tl")
    rows, width = inputs.shape[1], inputs.shape[2]
    half = rows // 2
    shard = query_weight.shape[0]
    quarter = query_bias.shape[0]
    hidden = up_bias.shape[0]
    square = fsdp_size == 2
    eighth = width // 8
    plane = ("fsdp", "cx")

    def at(*indices):
        return jnp.stack([jnp.asarray(i, jnp.int32) for i in indices])

    spot = at(k, l, h, 0)
    if square:
        me = at(f * 2 + x, k)
        groups = at(*[(f ^ df) * 2 + (x ^ dx) for df, dx in BITS], k, h, l)
    else:
        me, groups = at(0, k), at(0, 1, 2, 3, k, h, l)

    def exchange(values):
        near, side, far = values
        return [
            flip(near, "cx"),
            flip(side, "fsdp"),
            lax.ppermute(far, plane, [(i, i ^ 3) for i in range(4)]),
        ]

    def around(mine):
        if square:
            return [mine] + exchange([mine] * 3)
        full = lax.all_gather(mine, plane, axis=0).transpose(2, 0, 1, 3, 4)
        full = full.reshape(2, 4, 2, eighth, -1)
        return [full[:, i].transpose(1, 0, 2, 3) for i in range(4)]

    call = Order()

    docs = lax.dynamic_index_in_dim(segment_ids, h, 0, keepdims=False)

    def docs_at(start, size):
        return lax.dynamic_slice_in_dim(docs, start, size, 0)

    docs_k = jnp.concatenate(
        [
            docs_at((2 * x + k) * rows, rows),
            docs_at((2 * x + 1 - k) * rows, rows),
            docs_at((2 * (1 - x) + k) * rows, rows),
            docs_at((2 * (1 - x) + 1 - k) * rows, rows),
        ]
    )
    start = (2 * x + l) * rows
    docs_q = jnp.concatenate(
        [docs_at(start + k * half, half), docs_at(start + (1 - k) * half, half)]
    )
    tiles_q, tiles_k = docs_q.reshape(-1, TILE), docs_k.reshape(-1, TILE)
    active = (
        (tiles_k[None, :, 0] <= tiles_q[:, None, -1])
        & (tiles_k[None, :, -1] >= tiles_q[:, None, 0])
    ).astype(jnp.int32)
    flags = jnp.concatenate([spot, active.reshape(-1)])
    docs_row, docs_col = docs_q[None, :], docs_k[:, None]
    docs_a, docs_b, docs_cd = docs_col[:rows], docs_col[rows : 2 * rows], docs_col[2 * rows :]
    params = jnp.stack(
        [output_bias, first_gain, first_shift, down_bias, second_gain, second_shift]
    )

    biases = jnp.concatenate([query_bias, value_bias, up_bias])
    bias_high = lax.reduce_precision(biases, 8, 7)
    bias_middle = lax.reduce_precision(biases - bias_high, 8, 7)
    bias_low = biases - bias_high - bias_middle
    bias_rows = jnp.concatenate(
        [bias_high, bias_middle, bias_low, jnp.zeros((16 * 640 - 3 * biases.shape[0],), WIDE)]
    ).reshape(16, 640)
    uo_width = hidden + 256
    own_a, own_d = call(
        pack_kernel, "pack", spot,
        [key_weight, value_weight, query_weight, bias_rows, down_weight.T],
        [((16 + shard, 640), LOW), ((shard, hidden), LOW)],
        far=(True, False),
    )
    pieces = [move(own_a, lambda c, hh, ll, a=a: (hh, c ^ a, ll)) for a in range(2)]
    tall = rows + half
    block_a, beside_a, cot_kept = call(
        pick_kernel, "pick", spot, [inputs, cotangent],
        [((rows, width), LOW), ((tall, width), LOW), ((half, width), LOW)],
        [pltpu.SemaphoreType.DMA((3,))], hbm=True,
    )
    block_c = flip(block_a, "cx")
    pair_a = call(pair_kernel, "pair_a", spot, pieces, [((2, 16 + shard, 640), LOW)])[0]
    got_pair = flip(pair_a, "tl")
    own_uo = call(
        pack_uo_kernel, "pack_uo", spot, [up_weight, output_weight],
        [((shard, uo_width + 384), LOW)], far=(True, False),
    )[0]
    uo = lax.all_gather(own_uo, ("th", "tl"), axis=0)
    if square:
        pair_d = call(
            pair_kernel, "pair_d", spot, [own_d, flip(own_d, "fsdp")], [((2, shard, hidden), LOW)]
        )[0]
    got_ab = flip(beside_a, "cc")
    tokens_own, tokens_peer, grad_out = call(
        own_kernel, "own", spot, [block_a, got_ab, cot_kept], [((half, width), LOW)] * 3
    )
    if square:
        rows_d = call(
            line_kernel, "line_d", spot, [pair_d, flip(pair_d, "cx")],
            [((4, shard, hidden), LOW)],
        )[0]
    else:
        rows_d = lax.all_gather(own_d, plane, axis=0)
    all_d = lax.all_gather(rows_d, ("th", "tl"), axis=0)
    kept_c = call(
        copy_kernel, "keep", spot, [block_c], [((rows, width), LOW)],
        after=(params, docs_row, docs_col, docs_a, docs_b, docs_cd, flags),
    )[0]
    mine_a, bias_full = call(
        spread_kernel, "spread", spot, [pair_a, got_pair],
        [((2, 2, shard, 640), LOW), ((2, 16, 640), LOW)],
    )
    block_d = flip(kept_c, "cc")
    plane_a = around(mine_a)
    spots_a = at(*[i for a, b in BITS for i in (h ^ a, l ^ b)])
    bias_full = bias_full.reshape(2, -1).astype(WIDE)
    count = biases.shape[0]
    bias_parts = (
        bias_full[:, :count] + bias_full[:, count : 2 * count]
    ) + bias_full[:, 2 * count : 3 * count]
    given = call(give_kernel, "give", spot, [uo], [((2, shard, uo_width), LOW)])[0]
    uo_got = flip(given, "cc")

    zeros = jnp.zeros((quarter,), WIDE)
    kv_bias = jnp.concatenate(
        [zeros, bias_parts[0][quarter : 2 * quarter], zeros, bias_parts[1][quarter : 2 * quarter]]
    )[None, :]
    q_bias = jnp.concatenate(
        [bias_parts[0][:quarter], zeros[:DH], bias_parts[1][:quarter], zeros[:DH]]
    )[None, :]
    u_bias = bias_parts[:, 2 * quarter :].reshape(1, -1)

    def rows_kernel(spot, gathered, got, out):
        k = spot[0]
        for ql in range(2):
            out[k, ql] = gathered[2 * k + ql, :, :uo_width]
            out[1 - k, ql] = got[ql]

    mine_uo = call(
        rows_kernel, "rows", spot, [uo, uo_got], [((2, 2, shard, uo_width), LOW)],
        after=tuple(plane_a),
    )[0]
    plane_uo = around(mine_uo)
    kv, q, wkv, wq, kv_a, kv_b, kv_cd, q_far = call(
        project_kernel, "project", groups,
        plane_a + [block_a, got_ab, kept_c, block_d, tokens_own, tokens_peer, kv_bias, q_bias],
        [
            ((4 * rows, 768), LOW), ((rows, 512), LOW),
            ((4, 2, eighth, 768), LOW), ((4, 2, eighth, 512), LOW),
            ((rows, 768), LOW), ((rows, 768), LOW), ((2 * rows, 768), LOW), ((rows, 512), LOW),
        ], (), 14, far=(False, (False,) * 2 + (True,) * 6), after=(grad_out, u_bias),
    )
    wkv, wq = wkv.reshape(width, 768), wq.reshape(width, 512)
    o, lse = attention_forward(call, flags, q, kv, docs_row, docs_col)

    def core(value):
        return flip(value, "cc")

    if square:
        given_d = call(
            give_groups_kernel, "give_d", spot, [all_d], [((2, 4, shard, hidden), LOW)]
        )[0]
        got_d = core(given_d)

    own_peer = [((half, width), WIDE), ((half, width), LOW)]
    wu, wo, part_own, part_peer = call(
        branch_kernel, "branch", groups, plane_uo + [o],
        [((4, 2, eighth, 2 * hidden), LOW), ((4, 2, eighth, 512), LOW)] + own_peer,
    )
    wu, wo = wu.reshape(width, 2 * hidden), wo.reshape(width, 512)
    first_own, normed_one, inverse_one = call(
        norm_one_kernel, "norm_one", spot, [part_own, core(part_peer), tokens_own, params],
        [((half, width), LOW), ((half, width), WIDE), ((half, 1), WIDE)],
    )
    first_peer = core(first_own)
    act, slope = call(
        up_kernel, "up", spot, [first_own, first_peer, wu, u_bias],
        [((rows, 2 * hidden), LOW), ((rows, 2 * hidden), WIDE)],
    )
    if square:
        wd, part_own, part_peer = call(
            down_join_kernel, "down", groups, [all_d, got_d, act],
            [((4, 2, eighth, 2 * hidden), LOW)] + own_peer,
        )
        wd = wd.reshape(width, 2 * hidden)
    else:
        kept_d = lax.dynamic_slice_in_dim(all_d, 2 * k, 2, 0)
        got_d = core(lax.dynamic_slice_in_dim(all_d, 2 * (1 - k), 2, 0))
        both_d = jnp.stack([jnp.where(k == 0, kept_d, got_d), jnp.where(k == 0, got_d, kept_d)])
        wd = both_d.transpose(2, 0, 3, 1, 4).reshape(width, 2 * hidden)
        part_own, part_peer = call(down_kernel, "down", spot, [wd, act], own_peer)
    grad_outs = [
        ((half, width), WIDE), ((half, width), LOW), ((3, 8, width), WIDE)
    ]
    out_own, grad_two, e_own, sums_two = call(
        norm_two_kernel, "norm_two", spot,
        [part_own, core(part_peer), normed_one, params, grad_out],
        [((half, width), LOW)] + grad_outs,
    )
    out_own = move(out_own, lambda c, hh, ll: (ll, hh, c))

    e_peer = core(e_own)
    kept_d, sent_d = call(
        grad_d_kernel, "grad_d", me, [e_own, e_peer, act],
        [((4 * eighth, 2 * hidden), LOW)] * 2,
        [VMEM((width, rows), LOW), VMEM((width, 2 * hidden), LOW)], 8,
    )
    units, part_own, part_peer, sum_u = call(
        units_kernel, "units", spot, [e_own, e_peer, wd, wu, slope],
        [((rows, 2 * hidden), LOW)] + own_peer + [((8, 2 * hidden), WIDE)],
    )
    grad_one, eb_own, sums_one = call(
        norm_one_back_kernel, "norm_one_back", spot,
        [part_own, core(part_peer), grad_two, normed_one, inverse_one, params], grad_outs,
    )
    eb_peer = core(eb_own)
    small = call(small_kernel, "small", spot, [sums_one, sums_two], [((8, width), WIDE)])[0]
    out_own = call(copy_kernel, "keep", spot, [out_own], [((half, width), LOW)])[0]
    out_far = flip(out_own, "th")
    go = call(mixed_grad_kernel, "mixed_grad", spot, [eb_own, eb_peer, wo], [((rows, 512), LOW)])[0]
    uo_columns = 2 * hidden + 512
    kept_uo, sent_uo = call(
        grad_uo_kernel, "grad_uo", me,
        [first_own, first_peer, units, eb_own, eb_peer, o, small, core(small), sum_u],
        [((4 * eighth + RIDE, uo_columns), LOW)] * 2,
        [VMEM((width, rows), LOW), VMEM((width, uo_columns), LOW)], 8,
    )

    if square:
        got_d, got_uo = flip(sent_d, "fsdp"), flip(sent_uo, "fsdp")
    dq_part, dkv_cd, part_c, part_d, sum_cd = attention_backward(
        call, 0, flags, [q_far, kv_cd, docs_row, docs_cd, o, go, lse, wkv], []
    )
    sum_c = call(add_kernel, "add", spot, [part_c, core(part_d)], [((rows, width), LOW)])[0]
    got_c = flip(sum_c, "cx")
    dq_part, dkv_a, part_a, sum_a = attention_backward(
        call, 1, flags, [q_far, kv_a, docs_row, docs_a, o, go, lse, wkv], [dq_part]
    )
    if square:
        left_d, next_d = call(
            fold_d_kernel, "fold_d", spot, [kept_d, got_d], [((2 * eighth, 2 * hidden), LOW)] * 2
        )
        got_d = flip(next_d, "cx")
    out_pair = call(pair_kernel, "pair", spot, [out_own, out_far], [((2, half, width), LOW)])[0]
    out_got = flip(out_pair, "tl")
    dq, dkv_b, part_a, part_b, sum_b, sum_q = attention_backward(
        call, 2, flags, [q_far, kv_b, docs_row, docs_b, o, go, lse, wkv],
        [dq_part, wq, grad_one, part_a],
    )
    got_b = core(part_b)
    out_spots = at(h, h, 1 - h, 1 - h, l, 1 - l)
    layer_output = call(
        output_kernel, "output", out_spots, [out_pair, out_got], [((2, 2, half, width), LOW)],
        far=(False, True),
    )[0].reshape(2, rows, width)
    if square:
        kept_zd, sent_zd = call(
            merge_d_kernel, "merge_d", spot, [left_d, got_d], [((2, shard, hidden), LOW)] * 2
        )
        got_zd = flip(sent_zd, "tl")
        left_uo, next_uo = call(
            fold_uo_kernel, "fold_uo", spot, [kept_uo, got_uo],
            [((2 * eighth + RIDE, uo_columns), LOW)] * 2,
        )
        got_uo = flip(next_uo, "cx")
    kept, sent = call(
        sum_kernel, "sum", spot, [part_a, got_b, got_c],
        [((half, width), WIDE), ((half, width), LOW)],
    )
    parts_a = call(
        grad_qkv_kernel, "grad_qkv", me,
        [
            block_a, got_ab, kept_c, block_d, tokens_own, tokens_peer, dkv_a, dkv_b, dkv_cd, dq,
            sum_q, sum_a, sum_b, sum_cd,
        ],
        [((2 * eighth + RIDE, 1280), LOW)] * 4,
        [VMEM((width, 5 * rows), LOW), VMEM((width, 1280), LOW)], 10,
    )
    if square:
        sent_a = exchange(parts_a[1:])
    sent = flip(sent, "tl")
    n = quarter

    def to_owner(pieces):
        return [
            move(piece, lambda c, hh, ll, a=a: (hh ^ a, c, ll)) for a, piece in enumerate(pieces)
        ]

    def over_z(kept, got):
        pieces = call(fold_z_kernel, "fold_z", spot, [kept, got], [(kept.shape[1:], LOW)] * 2)
        return to_owner(pieces)

    if square:
        moved_d = to_owner(
            call(
                fold_z_d_kernel, "fold_zd", spot, [kept_zd, got_zd], [((shard, hidden), LOW)] * 2
            )
        )
    final = call(add_kernel, "final", spot, [kept, sent], [((half, width), LOW)])[0]
    across, beside = flip(final, "th"), flip(final, "tl")
    if square:
        kept_z, sent_z = call(
            merge_uo_kernel, "merge_uo", spot, [left_uo, got_uo],
            [((2, shard + RIDE, 1024), LOW)] * 2,
        )
        got_z = flip(sent_z, "tl")
        kept_za, sent_za = call(
            merge_a_kernel, "merge_a", spot, [parts_a[0]] + sent_a,
            [((2, shard + RIDE, 640), LOW)] * 2,
        )
        got_za = flip(sent_za, "tl")
    across = call(copy_kernel, "keep", spot, [across], [((half, width), LOW)])[0]
    beyond = flip(across, "tl")
    if square:
        moved_uo = over_z(kept_z, got_z)
        moved_a = over_z(kept_za, got_za)
    else:

        def plane_sum(full, columns):
            grouped = full.reshape(fsdp_size * 2, 2, shard, 2, columns)
            rest = lax.psum_scatter(grouped, plane, scatter_dimension=0, tiled=False)
            kept = lax.dynamic_index_in_dim(rest, k, 0, keepdims=False).transpose(1, 0, 2)
            given = lax.dynamic_index_in_dim(rest, 1 - k, 0, keepdims=False).transpose(1, 0, 2)
            got = core(given)
            quarters = jnp.concatenate(
                [jnp.where(k == 0, kept, got), jnp.where(k == 0, got, kept)], axis=0
            )
            flat = quarters.reshape(-1, quarters.shape[-1])
            return lax.psum_scatter(flat, ("th", "tl"), scatter_dimension=0, tiled=True)

        def ride_sum(block):
            return lax.psum(ride_of(block), plane + ("th", "tl"))

        count = 2 * eighth
        shard_a = plane_sum(jnp.concatenate([p[:count] for p in parts_a]), 640).astype(WIDE)
        grad_key, grad_value, grad_query = [shard_a[:, i * n : (i + 1) * n] for i in range(3)]
        halves_d, halves_uo = (kept_d, sent_d), (kept_uo, sent_uo)
        full_d = jnp.concatenate(halves_d)
        full = jnp.concatenate(
            [block[j * count : (j + 1) * count] for block in halves_uo for j in range(2)]
        )
        grad_up = plane_sum(full[:, : 2 * hidden], hidden).astype(WIDE)
        grad_output = plane_sum(full[:, 2 * hidden :], 256).astype(WIDE)[:, DH:].T
        grad_down = plane_sum(full_d, hidden).astype(WIDE).T
        ride = ride_sum(kept_uo[2 * count :])
        shared = ride[:, :width]
        other = core(ride)
        units_sum = jnp.where(k == h, ride, other)[6, : 2 * hidden].reshape(2, hidden)
        units_sum = lax.dynamic_index_in_dim(units_sum, l, 0, keepdims=False)
        ride = ride_sum(parts_a[0][count:])
        both = jnp.where(k == h, ride, core(ride))[0].reshape(2, 640)
        sums_a = lax.dynamic_index_in_dim(both, l, 0, keepdims=True)
    grad_inputs = call(
        place_kernel, "place", spots_a, [final, beside, across, beyond],
        [((2, 2, half, width), LOW)], far=(False, True),
    )[0].reshape(2, rows, width)
    if square:
        grad_down, grad_up, grad_output, shared = call(
            shard_uo_kernel, "shard_uo", spot, moved_d + moved_uo,
            [
                ((shard, hidden), WIDE), ((shard, hidden), WIDE), ((n, shard), WIDE),
                ((8, width), WIDE),
            ], far=(False, True),
        )
        units_sum = shared[6]
        grad_key, grad_value, grad_query, sums_a = call(
            shard_a_kernel, "shard_a", spot, moved_a,
            [((shard, n), WIDE)] * 3 + [((8, 640), WIDE)], far=(False, True),
        )
    if square:
        grad_down = grad_down.T
    q_sum, v_sum = sums_a[0, 2 * n : 3 * n], sums_a[0, n : 2 * n]
    units_sum = units_sum.reshape(-1)

    return (
        layer_output,
        grad_inputs,
        grad_query,
        q_sum,
        grad_key,
        grad_value,
        v_sum,
        grad_output,
        shared[0],
        shared[1],
        shared[2],
        grad_up,
        units_sum,
        grad_down,
        shared[3],
        shared[4],
        shared[5],
    )


def solution(mesh):
    fsdp = mesh.shape["fsdp"]
    if mesh.shape["ctx"] != 4 or mesh.shape["tp"] != 4:
        raise ValueError("mesh")
    fine = Mesh(mesh.devices.reshape(fsdp, 2, 2, 2, 2), ("fsdp", "cx", "cc", "th", "tl"))
    ctx, tp = ("cx", "cc"), ("th", "tl")
    both = ("fsdp",) + ctx
    tokens, rows, columns = P("fsdp", ctx, None), P(both, tp), P(tp, both)
    in_specs = (
        tokens, P("fsdp", None), rows, P(tp), rows, rows, P(tp), columns, P(), P(), P(),
        rows, P(tp), columns, P(), P(), P(), tokens,
    )
    out_specs = (
        tokens, tokens, rows, P(tp), rows, rows, P(tp), columns, P(), P(), P(),
        rows, P(tp), columns, P(), P(), P(),
    )
    return jax.shard_map(
        functools.partial(body, fsdp),
        mesh=fine,
        in_specs=in_specs,
        out_specs=out_specs,
        check_vma=False,
    )
```

time: 1010 us -> 335 us (0.33)
  waiting for transfers between devices: 729 us -> 102 us
  Pallas kernels: 0 us -> 107 us
  matrix products: 103 us -> 0 us
  starting transfers between devices: 1.05 us -> 69.9 us
  blocking collectives: 62 us -> 0 us
  other arithmetic: 59 us -> 1.18 us
    psum x4 -> x0, waiting for transfers between devices: 454 us -> none  [head_total(): return lax.psum(partial_value, 'tp')]
    reduce_scatter x4 -> x0, waiting for transfers between devices: 138 us -> none  [the longest x1 46.8 us: body(): lax.psum_scatter(grad_up_weight, ('fsdp', 'ctx'), scatter_dimension=0, ti...]
    unnamed x20 -> x2, waiting for transfers between devices: 127 us -> 0.03 us
    pallas_call x0 -> x47, Pallas kernels: none -> 107 us  [__call__(): pl.pallas_call(run, out_shape=tuple((jax.ShapeDtypeStruct(shape, kind) fo...]
    dot_general x31 -> x0, matrix products: 101 us -> none  [the longest x4 29.7 us: scores_of(): jnp.einsum('hqd,hkd->hqk', query_seq, key_seq, preferred_element_type=jnp...]
    ppermute x0 -> x49, waiting for transfers between devices: none -> 99.9 us  [the longest x37 64.1 us: flip(): return lax.ppermute(value, axis, FLIP)]
    ppermute x0 -> x49, starting transfers between devices: none -> 69.8 us  [the longest x37 41.7 us: flip(): return lax.ppermute(value, axis, FLIP)]
    all_gather x4 -> x0, blocking collectives: 39.4 us -> none  [the longest x1 10.9 us: body(): lax.all_gather(lowered[1], ('fsdp', 'ctx'), axis=0, tiled=True)]
  transfers between devices with their start and end apart: 16 -> 51, of which waited for: 13 -> 19; matrix products, arithmetic and copies ran while one was open for 6% -> 3% of each run, Pallas kernels for 0% -> 28%
where the time goes in v1:
time: 335 us; the launch traced here: 330 us
  Pallas kernels  107 us (32%)
  waiting for transfers between devices  102 us (30%)
  starting transfers between devices  69.9 us (21%)
  local copies, waits for them, and re-layouts  34.7 us (10%)
  between operations  15.3 us (5%)
    pallas_call x47, Pallas kernels, __call__(): pl.pallas_call(run, out_shape=tuple((jax.ShapeDtypeStruct(shape, kind) fo...  107 us
    ppermute x37, waiting for transfers between devices, flip(): return lax.ppermute(value, axis, FLIP)  64.1 us
    ppermute x37, starting transfers between devices, flip(): return lax.ppermute(value, axis, FLIP)  41.7 us
    ppermute x9, waiting for transfers between devices, move(): return lax.ppermute(value, ('cc', 'th', 'tl'), pairs)  27.6 us
    unnamed x127, local copies, waits for them, and re-layouts  25.4 us
    ppermute x9, starting transfers between devices, move(): return lax.ppermute(value, ('cc', 'th', 'tl'), pairs)  22.8 us
    ppermute x3, waiting for transfers between devices, exchange(): lax.ppermute(far, plane, [(i, i ^ 3) for i in range(4)])  8.3 us
  transfers between devices with their start and end apart: 51, of which 19 were waited for; matrix products, arithmetic and copies ran while one was open for 3% of the time, Pallas kernels for 28%

profile of v1, /device:TPU:1, one launch (start us, length us, event | category | flops | bytes accessed | tf_op | source)
XLA Modules:
  0.0 329.8 jit_solution(11301749392479533487)
XLA Ops:
  8.8 1.8 pack.1
  10.7 5.6 %collective-permute-start.1 = (bf16[112,640]{1,0:T(8,128)(2,1)S(1)}, bf16[112,640]{1,0:T(8,128)(2,1)S(1)}, u32[]{:S(2)}, u32[]{:S(2)}) collective-permute-start(bf16[112,640]{1,0:T(8,128)(2,1)S(1)} %get-tuple-element.110.refs_3_), channel_id=1, source_target_pairs={{0,0},{1,1},{2,4},{3,5},{4,2},{5,3},{6,6},{7,7},{8,8},{9,9},{10,12... | collective-permute-start | bytes 430088 | tf_op jit(solution)/shard_map/ppermute | solution.py:841
  16.3 2.0 pick.1
  19.3 1.6 collective-permute-done.1.refs_1_
  22.2 2.4 pack_uo.1.refs_3_
  26.1 3.6 %collective-permute-done.refs_2_ = bf16[96,768]{1,0:T(8,128)(2,1)S(1)} collective-permute-done((bf16[96,768]{1,0:T(8,128)(2,1)S(1)}, bf16[96,768]{1,0:T(8,128)(2,1)S(1)}, u32[]{:S(2)}, u32[]{:S(2)}) %collective-permute-start) | collective-permute-done | bytes 147488 | tf_op jit(solution)/shard_map/ppermute | solution.py:831
  33.9 3.7 %collective-permute-done.3.refs_2_ = bf16[2,96,768]{2,1,0:T(8,128)(2,1)S(1)} collective-permute-done((bf16[2,96,768]{2,1,0:T(8,128)(2,1)S(1)}, bf16[2,96,768]{2,1,0:T(8,128)(2,1)S(1)}, u32[]{:S(2)}, u32[]{:S(2)}) %collective-permute-start.3) | collective-permute-done | bytes 294944 | tf_op jit(solution)/shard_map/ppermute | solution.py:831
  43.0 2.3 collective-permute-start.5
  50.1 6.7 %collective-permute-done.6.refs_1_ = bf16[512,768]{1,0:T(8,128)(2,1)} collective-permute-done((bf16[512,768]{1,0:T(8,128)(2,1)S(1)}, bf16[512,768]{1,0:T(8,128)(2,1)}, u32[]{:S(2)}, u32[]{:S(2)}) %collective-permute-start.6) | collective-permute-done | bytes 786464 | tf_op jit(solution)/shard_map/ppermute | solution.py:831
  62.9 2.3 collective-permute-start.9
  65.6 4.0 %collective-permute-start.10 = (bf16[512,768]{1,0:T(8,128)(2,1)S(1)}, bf16[512,768]{1,0:T(8,128)(2,1)}, u32[]{:S(2)}, u32[]{:S(2)}) collective-permute-start(bf16[512,768]{1,0:T(8,128)(2,1)S(1)} %keep.3.refs_3_.refs_7_), channel_id=1, source_target_pairs={{0,4},{4,0},{1,5},{5,1},{2,6},{6,2},{3,7},{7,3},{8,12},{12,8},{9,1... | collective-permute-start | bytes 2359304 | tf_op jit(solution)/shard_map/ppermute | solution.py:831
  74.4 13.2 %collective-permute-done.8.refs_6_.refs_3_ = bf16[2,2,96,640]{3,2,1,0:T(8,128)(2,1)} collective-permute-done((bf16[2,2,96,640]{3,2,1,0:T(8,128)(2,1)S(1)}, bf16[2,2,96,640]{3,2,1,0:T(8,128)(2,1)}, u32[]{:S(2)}, u32[]{:S(2)}) %collective-permute-start.8) | collective-permute-done | bytes 491552 | tf_op jit(solution)/shard_map/ppermute | solution.py:831
  89.7 1.9 collective-permute-start.14
  92.0 5.5 %project.1 = (bf16[2048,768]{1,0:T(8,128)(2,1)S(1)}, bf16[512,512]{1,0:T(8,128)(2,1)S(1)}, bf16[4,2,96,768]{3,2,1,0:T(8,128)(2,1)S(1)}, bf16[4,2,96,512]{3,2,1,0...) custom-call(s32[7]{0:T(128)S(1)} %copy-done.52, ...), custom_call_target="tpu_custom_call" | custom-call | flops 1 | bytes 1 | tf_op jit(solution)/shard_map/project/pallas_call | solution.py:273
  103.2 7.5 %attend.1 = (bf16[512,512]{1,0:T(8,128)(2,1)S(1)}, f32[8,512]{1,0:T(8,128)S(1)}) custom-call(s32[20]{0:T(128)S(1)} %copy-done.50, bf16[512,512]{1,0:T(8,128)(2,1)S(1)} %get-tuple-element.119.refs_1_.refs_5_, bf16[2048,768]{1,0:T(8,128)(2,1)S(1)} %get-tuple-element.120.refs_2_, s32[1,512]{1,0:T(1,128)S(1)} %bitcast.62, s32[2048,1]{1,0:T(8,128)S(1)} %copy.51.refs_5_.refs_4_, ...), custom_call_target="tpu_custom_call" | custom-call | flops 1 | bytes 1 | tf_op jit(solution)/shard_map/attend/pallas_call | solution.py:273
  111.4 1.9 all-gather.5.cloned.1.call-done
  113.2 1.7 copy-done.1
  117.0 9.6 %collective-permute-done.14.refs_3_ = bf16[2,2,96,1024]{3,2,1,0:T(8,128)(2,1)} collective-permute-done((bf16[2,2,96,1024]{3,2,1,0:T(8,128)(2,1)}, bf16[2,2,96,1024]{3,2,1,0:T(8,128)(2,1)}, u32[]{:S(2)}, u32[]{:S(2)}) %collective-permute-start.14) | collective-permute-done | bytes 786464 | tf_op jit(solution)/shard_map/ppermute | solution.py:831
  126.6 2.7 branch.1
  134.2 2.7 up.1
  136.9 2.1 down.1
  144.0 2.1 grad_d.1
  146.1 3.4 %units.1 = (bf16[512,1536]{1,0:T(8,128)(2,1)S(1)}, f32[256,768]{1,0:T(8,128)S(1)}, bf16[256,768]{1,0:T(8,128)(2,1)S(1)}, f32[8,1536]{1,0:T(8,128)S(1)}) custom-call(s32[4]{0:T(128)S(1)} %pad_add_fusion.4.refs_0_, bf16[256,768]{1,0:T(8,128)(2,1)S(1)} %get-tuple-element.133.refs_1_, bf16[256,768]{1,0:T(8,128)(2,1)S(1)} %collective-permute-done.20.refs_2_, ...), custom_call_target="tpu_custom_call" | custom-call | flops 1 | bytes 1 | tf_op jit(solution)/shard_map/units/pallas_call | solution.py:273
  149.9 4.9 %collective-permute-start.19 = (bf16[256,768]{1,0:T(8,128)(2,1)S(1)}, bf16[256,768]{1,0:T(8,128)(2,1)S(1)}, u32[]{:S(2)}, u32[]{:S(2)}) collective-permute-start(bf16[256,768]{1,0:T(8,128)(2,1)S(1)} %get-tuple-element.132), channel_id=1, source_target_pairs={{0,0},{1,4},{2,2},{3,6},{4,1},{5,5},{6,3},{7,7},{8,8},{9,12},{10,1... | collective-permute-start | bytes 1179656 | tf_op jit(solution)/shard_map/ppermute | solution.py:841
  158.5 1.6 collective-permute-done.19.refs_1_
  161.8 3.8 %grad_uo.1 = (bf16[400,2048]{1,0:T(8,128)(2,1)S(1)}, bf16[400,2048]{1,0:T(8,128)(2,1)}) custom-call(s32[2]{0:T(128)S(1)} %pad_add_fusion.5.refs_0_, bf16[256,768]{1,0:T(8,128)(2,1)S(1)} %get-tuple-element.125.refs_1_, bf16[256,768]{1,0:T(8,128)(2,1)S(1)} %collective-permute-done.17.refs_2_, bf16[512,1536]{1,0:T(8,128)(2,1)S(1)} %get-tuple-element.150.refs_3_, ...), custom_call_target="tpu_custom_call" | custom-call | flops 1 | bytes 1 | tf_op jit(solution)/shard_map/grad_uo/pallas_call | solution.py:273
  166.7 8.9 %attend_cd.1 = (f32[384,512]{1,0:T(8,128)S(1)}, bf16[1024,768]{1,0:T(8,128)(2,1)S(1)}, f32[512,768]{1,0:T(8,128)S(1)}, bf16[512,768]{1,0:T(8,128)(2,1)S(1)}, f32[8,768]{1,0:T(8,128)S(1)}) custom-call(s32[20]{0:T(128)S(1)} %copy-done.51, bf16[512,512]{1,0:T(8,128)(2,1)} %copy-done.15, bf16[1024,768]{1,0:T(8,128)(2,1)} %copy-done.29, s32[1,512]{1,0:T(1,128)S(1)} %bitcast.63, ...), custom_call_target="tpu_custom_call" | custom-call | flops 1 | bytes 1 | tf_op jit(solution)/shard_map/attend_cd/pallas_call | solution.py:273
  179.5 7.4 %attend_a.1 = (f32[384,512]{1,0:T(8,128)S(1)}, bf16[512,768]{1,0:T(8,128)(2,1)S(1)}, f32[512,768]{1,0:T(8,128)S(1)}, f32[8,768]{1,0:T(8,128)S(1)}) custom-call(s32[20]{0:T(128)S(1)} %copy-done.51, bf16[512,512]{1,0:T(8,128)(2,1)} %copy-done.15, bf16[512,768]{1,0:T(8,128)(2,1)} %copy-done.39, s32[1,512]{1,0:T(1,128)S(1)} %bitcast.64, ...), custom_call_target="tpu_custom_call" | custom-call | flops 1 | bytes 1 | tf_op jit(solution)/shard_map/attend_a/pallas_call | solution.py:273
  186.9 1.6 fold_d.1
  189.4 13.2 %collective-permute-start.27 = (bf16[2,256,768]{2,1,0:T(8,128)(2,1)S(1)}, bf16[2,256,768]{2,1,0:T(8,128)(2,1)}, u32[]{:S(2)}, u32[]{:S(2)}) collective-permute-start(bf16[2,256,768]{2,1,0:T(8,128)(2,1)S(1)} %pair.1.refs_13_.refs_1_), channel_id=1, source_target_pairs={{0,1},{1,0},{2,3},{3,2},{4,5},{5,4},{6,7},{7,6},{8,9},{9,8},{10,11... | collective-permute-start | bytes 2359304 | tf_op jit(solution)/shard_map/ppermute | solution.py:831
  204.0 12.7 %attend_b.1 = (bf16[512,512]{1,0:T(8,128)(2,1)S(1)}, bf16[512,768]{1,0:T(8,128)(2,1)S(1)}, f32[512,768]{1,0:T(8,128)S(1)}, bf16[512,768]{1,0:T(8,128)(2,1)}, f32[8,768]{1,0:T(8,128)S(1)}, /*index=5*/f32[8,512]{1,0:T(8,128)S(1)}) custom-call(s32[20]{0:T(128)S(1)} %copy-done.51, bf16[512,512]{1,0:T(8,128)(2,1)} %copy-done.15, bf16[512,768]{1,0:T(8,128)(2,1)} %copy-done.34, ...), custom_call_target="tpu_custom_call" | custom-call | flops 1 | bytes 1 | tf_op jit(solution)/shard_map/attend_b/pallas_call | solution.py:273
  219.7 2.5 output.1.refs_3_
  225.2 2.1 fold_uo.1
  228.0 6.8 %collective-permute-done.29.refs_3_ = bf16[512,768]{1,0:T(8,128)(2,1)} collective-permute-done((bf16[512,768]{1,0:T(8,128)(2,1)}, bf16[512,768]{1,0:T(8,128)(2,1)}, u32[]{:S(2)}, u32[]{:S(2)}) %collective-permute-start.29) | collective-permute-done | bytes 786464 | tf_op jit(solution)/shard_map/ppermute | solution.py:831
  234.9 1.9 sum.1
  237.4 5.1 %grad_qkv.1 = (bf16[208,1280]{1,0:T(8,128)(2,1)S(1)}, bf16[208,1280]{1,0:T(8,128)(2,1)S(1)}, bf16[208,1280]{1,0:T(8,128)(2,1)S(1)}, bf16[208,1280]{1,0:T(8,128)(2,1)S(1)}) custom-call(s32[2]{0:T(128)S(1)} %pad_add_fusion.5.refs_0_, bf16[512,768]{1,0:T(8,128)(2,1)S(1)} %copy-done.5, bf16[768,768]{1,0:T(8,128)(2,1)S(1)} %collective-permute-done.4.refs_2_.refs_6_, ...), custom_call_target="tpu_custom_call" | custom-call | flops 1 | bytes 1 | tf_op jit(solution)/shard_map/grad_qkv/pallas_call | solution.py:273
  242.8 2.5 collective-permute-start.38
  246.6 2.7 collective-permute-start.35
  249.2 3.8 %collective-permute-done.39.refs_2_ = bf16[208,2048]{1,0:T(8,128)(2,1)S(1)} collective-permute-done((bf16[208,2048]{1,0:T(8,128)(2,1)S(1)}, bf16[208,2048]{1,0:T(8,128)(2,1)S(1)}, u32[]{:S(2)}, u32[]{:S(2)}) %collective-permute-start.39) | collective-permute-done | bytes 852000 | tf_op jit(solution)/shard_map/ppermute | solution.py:831
  254.3 10.2 %collective-permute-done.36.refs_2_ = bf16[208,1280]{1,0:T(8,128)(2,1)S(1)} collective-permute-done((bf16[208,1280]{1,0:T(8,128)(2,1)S(1)}, bf16[208,1280]{1,0:T(8,128)(2,1)S(1)}, u32[]{:S(2)}, u32[]{:S(2)}) %collective-permute-start.36) | collective-permute-done | bytes 532512 | tf_op jit(solution)/shard_map/ppermute | solution.py:831
  264.5 8.3 %collective-permute-done.38.refs_4_ = bf16[208,1280]{1,0:T(8,128)(2,1)S(1)} collective-permute-done((bf16[208,1280]{1,0:T(8,128)(2,1)S(1)}, bf16[208,1280]{1,0:T(8,128)(2,1)S(1)}, u32[]{:S(2)}, u32[]{:S(2)}) %collective-permute-start.38) | collective-permute-done | bytes 532512 | tf_op jit(solution)/shard_map/ppermute | solution.py:894
  276.6 2.5 collective-permute-start.46
  281.2 18.4 %collective-permute-done.46.refs_2_ = bf16[96,768]{1,0:T(8,128)(2,1)S(1)} collective-permute-done((bf16[96,768]{1,0:T(8,128)(2,1)S(1)}, bf16[96,768]{1,0:T(8,128)(2,1)S(1)}, u32[]{:S(2)}, u32[]{:S(2)}) %collective-permute-start.46) | collective-permute-done | bytes 147488 | tf_op jit(solution)/shard_map/ppermute | solution.py:841
  299.6 1.9 collective-permute-start.47
  301.6 4.5 %collective-permute-start.45 = (bf16[96,768]{1,0:T(8,128)(2,1)S(1)}, bf16[96,768]{1,0:T(8,128)(2,1)S(1)}, u32[]{:S(2)}, u32[]{:S(2)}) collective-permute-start(bf16[96,768]{1,0:T(8,128)(2,1)S(1)} %get-tuple-element.179.refs_3_), channel_id=1, source_target_pairs={{0,0},{1,1},{2,4},{3,5},{4,2},{5,3},{6,6},{7,7},{8,8},{9,9},{10,12... | collective-permute-start | bytes 442376 | tf_op jit(solution)/shard_map/ppermute | solution.py:841
  307.4 1.9 collective-permute-start.43
  309.5 1.8 place.1.refs_5_
  311.3 5.9 %collective-permute-done.45.refs_1_ = bf16[96,768]{1,0:T(8,128)(2,1)S(1)} collective-permute-done((bf16[96,768]{1,0:T(8,128)(2,1)S(1)}, bf16[96,768]{1,0:T(8,128)(2,1)S(1)}, u32[]{:S(2)}, u32[]{:S(2)}) %collective-permute-start.45) | collective-permute-done | bytes 147488 | tf_op jit(solution)/shard_map/ppermute | solution.py:841
  (278 shorter events, 87.3 us)
Async XLA Ops:
  7.2 63.6 %all-gather.7.cloned.1.call-start = ((), (), s32[]{:S(2)}) async-start(), calls=%async_computation.1 | async-start | bytes 1351680 | tf_op jit(solution)/shard_map/all_gather | solution.py:963
  10.6 8.7 %collective-permute-start.2 = (bf16[112,640]{1,0:T(8,128)(2,1)S(1)}, bf16[112,640]{1,0:T(8,128)(2,1)S(1)}, u32[]{:S(2)}, u32[]{:S(2)}) collective-permute-start(bf16[112,640]{1,0:T(8,128)(2,1)S(1)} %get-tuple-element.110.refs_3_), channel_id=1, source_target_pairs={{0,2},{1,3},{2,6},{3,7},{4,0},{5,1},{6,4},{7,5},{8,10},{9,11},{10,... | collective-permute-start | bytes 430088 | tf_op jit(solution)/shard_map/ppermute | solution.py:841
  10.7 10.2 %collective-permute-start.1 = (bf16[112,640]{1,0:T(8,128)(2,1)S(1)}, bf16[112,640]{1,0:T(8,128)(2,1)S(1)}, u32[]{:S(2)}, u32[]{:S(2)}) collective-permute-start(bf16[112,640]{1,0:T(8,128)(2,1)S(1)} %get-tuple-element.110.refs_3_), channel_id=1, source_target_pairs={{0,0},{1,1},{2,4},{3,5},{4,2},{5,3},{6,6},{7,7},{8,8},{9,9},{10,12... | collective-permute-start | bytes 430088 | tf_op jit(solution)/shard_map/ppermute | solution.py:841
  24.6 88.6 %all-gather.5.cloned.1.call-start = ((), (), s32[]{:S(2)}) async-start(), calls=%async_computation | async-start | bytes 2949120 | tf_op jit(solution)/shard_map/all_gather | solution.py:979
  24.7 7.1 %collective-permute-start.4 = (bf16[768,768]{1,0:T(8,128)(2,1)}, bf16[768,768]{1,0:T(8,128)(2,1)S(1)}, u32[]{:S(2)}, u32[]{:S(2)}) collective-permute-start(bf16[768,768]{1,0:T(8,128)(2,1)} %copy-done.54), channel_id=1, source_target_pairs={{0,4},{4,0},{1,5},{5,1},{2,6},{6,2},{3,7},{7,3},{8,12},{12,8},{9,1... | collective-permute-start | bytes 3538952 | tf_op jit(solution)/shard_map/ppermute | solution.py:831
  24.7 5.1 %collective-permute-start = (bf16[96,768]{1,0:T(8,128)(2,1)S(1)}, bf16[96,768]{1,0:T(8,128)(2,1)S(1)}, u32[]{:S(2)}, u32[]{:S(2)}) collective-permute-start(bf16[96,768]{1,0:T(8,128)(2,1)S(1)} %get-tuple-element.109.refs_1_), channel_id=1, source_target_pairs={{0,16},{16,0},{1,17},{17,1},{2,18},{18,2},{3,19},{19,3},{4,20},{20... | collective-permute-start | bytes 442376 | tf_op jit(solution)/shard_map/ppermute | solution.py:831
  30.4 7.3 %collective-permute-start.3 = (bf16[2,96,768]{2,1,0:T(8,128)(2,1)S(1)}, bf16[2,96,768]{2,1,0:T(8,128)(2,1)S(1)}, u32[]{:S(2)}, u32[]{:S(2)}) collective-permute-start(bf16[2,96,768]{2,1,0:T(8,128)(2,1)S(1)} %pair_d.1.refs_4_.refs_1_), channel_id=1, source_target_pairs={{0,8},{8,0},{1,9},{9,1},{2,10},{10,2},{3,11},{11,3},{4,12},{12,4},... | collective-permute-start | bytes 884744 | tf_op jit(solution)/shard_map/ppermute | solution.py:831
  39.8 17.0 %collective-permute-start.6 = (bf16[512,768]{1,0:T(8,128)(2,1)S(1)}, bf16[512,768]{1,0:T(8,128)(2,1)}, u32[]{:S(2)}, u32[]{:S(2)}) collective-permute-start(bf16[512,768]{1,0:T(8,128)(2,1)S(1)} %get-tuple-element.112.refs_1_.refs_5_), channel_id=1, source_target_pairs={{0,8},{8,0},{1,9},{9,1},{2,10},{10,2},{3,11},{11,3},{4,12},{12,4},... | collective-permute-start | bytes 2359304 | tf_op jit(solution)/shard_map/ppermute | solution.py:831
  43.0 18.7 %collective-permute-start.5 = (bf16[2,112,640]{2,1,0:T(8,128)(2,1)}, bf16[2,112,640]{2,1,0:T(8,128)(2,1)}, u32[]{:S(2)}, u32[]{:S(2)}) collective-permute-start(bf16[2,112,640]{2,1,0:T(8,128)(2,1)} %pair_a.1.refs_3_.refs_1_), channel_id=1, source_target_pairs={{0,1},{1,0},{2,3},{3,2},{4,5},{5,4},{6,7},{7,6},{8,9},{9,8},{10,11... | collective-permute-start | bytes 860168 | tf_op jit(solution)/shard_map/ppermute | solution.py:831
  62.9 11.5 %collective-permute-start.9 = (bf16[2,2,96,640]{3,2,1,0:T(8,128)(2,1)S(1)}, bf16[2,2,96,640]{3,2,1,0:T(8,128)(2,1)}, u32[]{:S(2)}, u32[]{:S(2)}) collective-permute-start(bf16[2,2,96,640]{3,2,1,0:T(8,128)(2,1)S(1)} %get-tuple-element.115.refs_4_.refs_1_), channel_id=1, source_target_pairs={{0,24},{8,16},{16,8},{24,0},{1,25},{9,17},{17,9},{25,1},{2,26},{10... | collective-permute-start | bytes 1474568 | tf_op jit(solution)/shard_map/ppermute | solution.py:894
  65.2 22.4 %collective-permute-start.8 = (bf16[2,2,96,640]{3,2,1,0:T(8,128)(2,1)S(1)}, bf16[2,2,96,640]{3,2,1,0:T(8,128)(2,1)}, u32[]{:S(2)}, u32[]{:S(2)}) collective-permute-start(bf16[2,2,96,640]{3,2,1,0:T(8,128)(2,1)S(1)} %get-tuple-element.115.refs_4_.refs_1_), channel_id=1, source_target_pairs={{0,16},{16,0},{1,17},{17,1},{2,18},{18,2},{3,19},{19,3},{4,20},{20... | collective-permute-start | bytes 1474568 | tf_op jit(solution)/shard_map/ppermute | solution.py:831
  65.4 22.2 %collective-permute-start.7 = (bf16[2,2,96,640]{3,2,1,0:T(8,128)(2,1)S(1)}, bf16[2,2,96,640]{3,2,1,0:T(8,128)(2,1)}, u32[]{:S(2)}, u32[]{:S(2)}) collective-permute-start(bf16[2,2,96,640]{3,2,1,0:T(8,128)(2,1)S(1)} %get-tuple-element.115.refs_4_.refs_1_), channel_id=1, source_target_pairs={{0,8},{8,0},{1,9},{9,1},{2,10},{10,2},{3,11},{11,3},{4,12},{12,4},... | collective-permute-start | bytes 1474568 | tf_op jit(solution)/shard_map/ppermute | solution.py:831
  65.6 26.4 %collective-permute-start.10 = (bf16[512,768]{1,0:T(8,128)(2,1)S(1)}, bf16[512,768]{1,0:T(8,128)(2,1)}, u32[]{:S(2)}, u32[]{:S(2)}) collective-permute-start(bf16[512,768]{1,0:T(8,128)(2,1)S(1)} %keep.3.refs_3_.refs_7_), channel_id=1, source_target_pairs={{0,4},{4,0},{1,5},{5,1},{2,6},{6,2},{3,7},{7,3},{8,12},{12,8},{9,1... | collective-permute-start | bytes 2359304 | tf_op jit(solution)/shard_map/ppermute | solution.py:831
  73.5 14.2 %collective-permute-start.11 = (bf16[2,96,1024]{2,1,0:T(8,128)(2,1)S(1)}, bf16[2,96,1024]{2,1,0:T(8,128)(2,1)S(1)}, u32[]{:S(2)}, u32[]{:S(2)}) collective-permute-start(bf16[2,96,1024]{2,1,0:T(8,128)(2,1)S(1)} %give.1.refs_3_), channel_id=1, source_target_pairs={{0,4},{4,0},{1,5},{5,1},{2,6},{6,2},{3,7},{7,3},{8,12},{12,8},{9,1... | collective-permute-start | bytes 1179656 | tf_op jit(solution)/shard_map/ppermute | solution.py:831
  89.1 27.9 %collective-permute-start.15 = (bf16[2,2,96,1024]{3,2,1,0:T(8,128)(2,1)}, bf16[2,2,96,1024]{3,2,1,0:T(8,128)(2,1)}, u32[]{:S(2)}, u32[]{:S(2)}) collective-permute-start(bf16[2,2,96,1024]{3,2,1,0:T(8,128)(2,1)} %rows.1.refs_13_.refs_1_), channel_id=1, source_target_pairs={{0,24},{8,16},{16,8},{24,0},{1,25},{9,17},{17,9},{25,1},{2,26},{10... | collective-permute-start | bytes 2359304 | tf_op jit(solution)/shard_map/ppermute | solution.py:894
  89.7 36.9 %collective-permute-start.14 = (bf16[2,2,96,1024]{3,2,1,0:T(8,128)(2,1)}, bf16[2,2,96,1024]{3,2,1,0:T(8,128)(2,1)}, u32[]{:S(2)}, u32[]{:S(2)}) collective-permute-start(bf16[2,2,96,1024]{3,2,1,0:T(8,128)(2,1)} %rows.1.refs_13_.refs_1_), channel_id=1, source_target_pairs={{0,16},{16,0},{1,17},{17,1},{2,18},{18,2},{3,19},{19,3},{4,20},{20... | collective-permute-start | bytes 2359304 | tf_op jit(solution)/shard_map/ppermute | solution.py:831
  91.6 35.0 %collective-permute-start.13 = (bf16[2,2,96,1024]{3,2,1,0:T(8,128)(2,1)}, bf16[2,2,96,1024]{3,2,1,0:T(8,128)(2,1)}, u32[]{:S(2)}, u32[]{:S(2)}) collective-permute-start(bf16[2,2,96,1024]{3,2,1,0:T(8,128)(2,1)} %rows.1.refs_13_.refs_1_), channel_id=1, source_target_pairs={{0,8},{8,0},{1,9},{9,1},{2,10},{10,2},{3,11},{11,3},{4,12},{12,4},... | collective-permute-start | bytes 2359304 | tf_op jit(solution)/shard_map/ppermute | solution.py:831
  116.2 20.6 %collective-permute-start.12 = (bf16[2,4,96,768]{3,2,1,0:T(8,128)(2,1)S(1)}, bf16[2,4,96,768]{3,2,1,0:T(8,128)(2,1)S(1)}, u32[]{:S(2)}, u32[]{:S(2)}) collective-permute-start(bf16[2,4,96,768]{3,2,1,0:T(8,128)(2,1)S(1)} %give_d.1.refs_6_), channel_id=1, source_target_pairs={{0,4},{4,0},{1,5},{5,1},{2,6},{6,2},{3,7},{7,3},{8,12},{12,8},{9,1... | collective-permute-start | bytes 3538952 | tf_op jit(solution)/shard_map/ppermute | solution.py:831
  129.4 2.1 collective-permute-start.16
  149.5 5.3 %collective-permute-start.21 = (bf16[256,768]{1,0:T(8,128)(2,1)S(1)}, bf16[256,768]{1,0:T(8,128)(2,1)S(1)}, u32[]{:S(2)}, u32[]{:S(2)}) collective-permute-start(bf16[256,768]{1,0:T(8,128)(2,1)S(1)} %get-tuple-element.139), channel_id=1, source_target_pairs={{0,4},{4,0},{1,5},{5,1},{2,6},{6,2},{3,7},{7,3},{8,12},{12,8},{9,1... | collective-permute-start | bytes 1179656 | tf_op jit(solution)/shard_map/ppermute | solution.py:831
  149.9 10.2 %collective-permute-start.19 = (bf16[256,768]{1,0:T(8,128)(2,1)S(1)}, bf16[256,768]{1,0:T(8,128)(2,1)S(1)}, u32[]{:S(2)}, u32[]{:S(2)}) collective-permute-start(bf16[256,768]{1,0:T(8,128)(2,1)S(1)} %get-tuple-element.132), channel_id=1, source_target_pairs={{0,0},{1,4},{2,2},{3,6},{4,1},{5,5},{6,3},{7,7},{8,8},{9,12},{10,1... | collective-permute-start | bytes 1179656 | tf_op jit(solution)/shard_map/ppermute | solution.py:841
  156.0 4.7 %collective-permute-start.24 = (bf16[256,768]{1,0:T(8,128)(2,1)S(1)}, bf16[256,768]{1,0:T(8,128)(2,1)S(1)}, u32[]{:S(2)}, u32[]{:S(2)}) collective-permute-start(bf16[256,768]{1,0:T(8,128)(2,1)S(1)} %get-tuple-element.146.refs_1_.refs_4_), channel_id=1, source_target_pairs={{0,4},{4,0},{1,5},{5,1},{2,6},{6,2},{3,7},{7,3},{8,12},{12,8},{9,1... | collective-permute-start | bytes 1179656 | tf_op jit(solution)/shard_map/ppermute | solution.py:831
  156.0 30.9 %collective-permute-start.23 = (bf16[384,1536]{1,0:T(8,128)(2,1)S(1)}, bf16[384,1536]{1,0:T(8,128)(2,1)S(1)}, u32[]{:S(2)}, u32[]{:S(2)}) collective-permute-start(bf16[384,1536]{1,0:T(8,128)(2,1)S(1)} %get-tuple-element.143), channel_id=1, source_target_pairs={{0,16},{16,0},{1,17},{17,1},{2,18},{18,2},{3,19},{19,3},{4,20},{20... | collective-permute-start | bytes 3538952 | tf_op jit(solution)/shard_map/ppermute | solution.py:831
  157.7 4.1 %collective-permute-start.25 = (f32[8,768]{1,0:T(8,128)S(1)}, f32[8,768]{1,0:T(8,128)S(1)}, u32[]{:S(2)}, u32[]{:S(2)}) collective-permute-start(f32[8,768]{1,0:T(8,128)S(1)} %small.1.refs_2_.refs_7_), channel_id=1, source_target_pairs={{0,4},{4,0},{1,5},{5,1},{2,6},{6,2},{3,7},{7,3},{8,12},{12,8},{9,1... | collective-permute-start | bytes 73736 | tf_op jit(solution)/shard_map/ppermute | solution.py:831
  165.6 59.5 %collective-permute-start.30 = (bf16[400,2048]{1,0:T(8,128)(2,1)}, bf16[400,2048]{1,0:T(8,128)(2,1)}, u32[]{:S(2)}, u32[]{:S(2)}) collective-permute-start(bf16[400,2048]{1,0:T(8,128)(2,1)} %get-tuple-element.166), channel_id=1, source_target_pairs={{0,16},{16,0},{1,17},{17,1},{2,18},{18,2},{3,19},{19,3},{4,20},{20... | collective-permute-start | bytes 4915208 | tf_op jit(solution)/shard_map/ppermute | solution.py:831
  175.6 2.4 collective-permute-start.26
  175.7 12.9 %collective-permute-start.22 = (bf16[256,768]{1,0:T(8,128)(2,1)S(1)}, bf16[256,768]{1,0:T(8,128)(2,1)S(1)}, u32[]{:S(2)}, u32[]{:S(2)}) collective-permute-start(bf16[256,768]{1,0:T(8,128)(2,1)S(1)} %keep.4.refs_4_.refs_1_), channel_id=1, source_target_pairs={{0,2},{2,0},{1,3},{3,1},{4,6},{6,4},{5,7},{7,5},{8,10},{10,8},{9,1... | collective-permute-start | bytes 1179656 | tf_op jit(solution)/shard_map/ppermute | solution.py:831
  189.4 30.3 %collective-permute-start.27 = (bf16[2,256,768]{2,1,0:T(8,128)(2,1)S(1)}, bf16[2,256,768]{2,1,0:T(8,128)(2,1)}, u32[]{:S(2)}, u32[]{:S(2)}) collective-permute-start(bf16[2,256,768]{2,1,0:T(8,128)(2,1)S(1)} %pair.1.refs_13_.refs_1_), channel_id=1, source_target_pairs={{0,1},{1,0},{2,3},{3,2},{4,5},{5,4},{6,7},{7,6},{8,9},{9,8},{10,11... | collective-permute-start | bytes 2359304 | tf_op jit(solution)/shard_map/ppermute | solution.py:831
  202.6 19.6 %collective-permute-start.31 = (bf16[192,1536]{1,0:T(8,128)(2,1)}, bf16[192,1536]{1,0:T(8,128)(2,1)}, u32[]{:S(2)}, u32[]{:S(2)}) collective-permute-start(bf16[192,1536]{1,0:T(8,128)(2,1)} %get-tuple-element.167), channel_id=1, source_target_pairs={{0,8},{8,0},{1,9},{9,1},{2,10},{10,2},{3,11},{11,3},{4,12},{12,4},... | collective-permute-start | bytes 1769480 | tf_op jit(solution)/shard_map/ppermute | solution.py:831
  202.6 32.2 %collective-permute-start.29 = (bf16[512,768]{1,0:T(8,128)(2,1)}, bf16[512,768]{1,0:T(8,128)(2,1)}, u32[]{:S(2)}, u32[]{:S(2)}) collective-permute-start(bf16[512,768]{1,0:T(8,128)(2,1)} %add.150.refs_10_), channel_id=1, source_target_pairs={{0,8},{8,0},{1,9},{9,1},{2,10},{10,2},{3,11},{11,3},{4,12},{12,4},... | collective-permute-start | bytes 2359304 | tf_op jit(solution)/shard_map/ppermute | solution.py:831
  219.6 15.2 %collective-permute-start.28 = (bf16[512,768]{1,0:T(8,128)(2,1)}, bf16[512,768]{1,0:T(8,128)(2,1)}, u32[]{:S(2)}, u32[]{:S(2)}) collective-permute-start(bf16[512,768]{1,0:T(8,128)(2,1)} %get-tuple-element.165), channel_id=1, source_target_pairs={{0,4},{4,0},{1,5},{5,1},{2,6},{6,2},{3,7},{7,3},{8,12},{12,8},{9,1... | collective-permute-start | bytes 2359304 | tf_op jit(solution)/shard_map/ppermute | solution.py:831
  227.3 25.8 %collective-permute-start.39 = (bf16[208,2048]{1,0:T(8,128)(2,1)S(1)}, bf16[208,2048]{1,0:T(8,128)(2,1)S(1)}, u32[]{:S(2)}, u32[]{:S(2)}) collective-permute-start(bf16[208,2048]{1,0:T(8,128)(2,1)S(1)} %get-tuple-element.183), channel_id=1, source_target_pairs={{0,8},{8,0},{1,9},{9,1},{2,10},{10,2},{3,11},{11,3},{4,12},{12,4},... | collective-permute-start | bytes 2555912 | tf_op jit(solution)/shard_map/ppermute | solution.py:831
  227.4 15.4 %collective-permute-start.33 = (bf16[2,96,768]{2,1,0:T(8,128)(2,1)S(1)}, bf16[2,96,768]{2,1,0:T(8,128)(2,1)S(1)}, u32[]{:S(2)}, u32[]{:S(2)}) collective-permute-start(bf16[2,96,768]{2,1,0:T(8,128)(2,1)S(1)} %get-tuple-element.172), channel_id=1, source_target_pairs={{0,1},{1,0},{2,3},{3,2},{4,5},{5,4},{6,7},{7,6},{8,9},{9,8},{10,11... | collective-permute-start | bytes 884744 | tf_op jit(solution)/shard_map/ppermute | solution.py:831
  236.8 9.2 %collective-permute-start.32 = (bf16[256,768]{1,0:T(8,128)(2,1)S(1)}, bf16[256,768]{1,0:T(8,128)(2,1)S(1)}, u32[]{:S(2)}, u32[]{:S(2)}) collective-permute-start(bf16[256,768]{1,0:T(8,128)(2,1)S(1)} %get-tuple-element.171.refs_15_), channel_id=1, source_target_pairs={{0,1},{1,0},{2,3},{3,2},{4,5},{5,4},{6,7},{7,6},{8,9},{9,8},{10,11... | collective-permute-start | bytes 1179656 | tf_op jit(solution)/shard_map/ppermute | solution.py:831
  242.5 21.9 %collective-permute-start.36 = (bf16[208,1280]{1,0:T(8,128)(2,1)S(1)}, bf16[208,1280]{1,0:T(8,128)(2,1)S(1)}, u32[]{:S(2)}, u32[]{:S(2)}) collective-permute-start(bf16[208,1280]{1,0:T(8,128)(2,1)S(1)} %get-tuple-element.180), channel_id=1, source_target_pairs={{0,8},{8,0},{1,9},{9,1},{2,10},{10,2},{3,11},{11,3},{4,12},{12,4},... | collective-permute-start | bytes 1597448 | tf_op jit(solution)/shard_map/ppermute | solution.py:831
  242.8 21.7 %collective-permute-start.37 = (bf16[208,1280]{1,0:T(8,128)(2,1)S(1)}, bf16[208,1280]{1,0:T(8,128)(2,1)S(1)}, u32[]{:S(2)}, u32[]{:S(2)}) collective-permute-start(bf16[208,1280]{1,0:T(8,128)(2,1)S(1)} %get-tuple-element.181), channel_id=1, source_target_pairs={{0,16},{16,0},{1,17},{17,1},{2,18},{18,2},{3,19},{19,3},{4,20},{20... | collective-permute-start | bytes 1597448 | tf_op jit(solution)/shard_map/ppermute | solution.py:831
  242.8 30.0 %collective-permute-start.38 = (bf16[208,1280]{1,0:T(8,128)(2,1)S(1)}, bf16[208,1280]{1,0:T(8,128)(2,1)S(1)}, u32[]{:S(2)}, u32[]{:S(2)}) collective-permute-start(bf16[208,1280]{1,0:T(8,128)(2,1)S(1)} %get-tuple-element.182), channel_id=1, source_target_pairs={{0,24},{8,16},{16,8},{24,0},{1,25},{9,17},{17,9},{25,1},{2,26},{10... | collective-permute-start | bytes 1597448 | tf_op jit(solution)/shard_map/ppermute | solution.py:894
  246.6 28.8 %collective-permute-start.35 = (bf16[256,768]{1,0:T(8,128)(2,1)S(1)}, bf16[256,768]{1,0:T(8,128)(2,1)S(1)}, u32[]{:S(2)}, u32[]{:S(2)}) collective-permute-start(bf16[256,768]{1,0:T(8,128)(2,1)S(1)} %final.1.refs_3_.refs_1_), channel_id=1, source_target_pairs={{0,2},{2,0},{1,3},{3,1},{4,6},{6,4},{5,7},{7,5},{8,10},{10,8},{9,1... | collective-permute-start | bytes 1179656 | tf_op jit(solution)/shard_map/ppermute | solution.py:831
  254.1 25.0 %collective-permute-start.42 = (bf16[2,112,1024]{2,1,0:T(8,128)(2,1)S(1)}, bf16[2,112,1024]{2,1,0:T(8,128)(2,1)S(1)}, u32[]{:S(2)}, u32[]{:S(2)}) collective-permute-start(bf16[2,112,1024]{2,1,0:T(8,128)(2,1)S(1)} %get-tuple-element.187), channel_id=1, source_target_pairs={{0,1},{1,0},{2,3},{3,2},{4,5},{5,4},{6,7},{7,6},{8,9},{9,8},{10,11... | collective-permute-start | bytes 1376264 | tf_op jit(solution)/shard_map/ppermute | solution.py:831
  273.9 27.7 %collective-permute-start.41 = (bf16[2,112,640]{2,1,0:T(8,128)(2,1)S(1)}, bf16[2,112,640]{2,1,0:T(8,128)(2,1)S(1)}, u32[]{:S(2)}, u32[]{:S(2)}) collective-permute-start(bf16[2,112,640]{2,1,0:T(8,128)(2,1)S(1)} %get-tuple-element.186), channel_id=1, source_target_pairs={{0,1},{1,0},{2,3},{3,2},{4,5},{5,4},{6,7},{7,6},{8,9},{9,8},{10,11... | collective-permute-start | bytes 860168 | tf_op jit(solution)/shard_map/ppermute | solution.py:831
  274.5 32.9 %collective-permute-start.34 = (bf16[256,768]{1,0:T(8,128)(2,1)S(1)}, bf16[256,768]{1,0:T(8,128)(2,1)S(1)}, u32[]{:S(2)}, u32[]{:S(2)}) collective-permute-start(bf16[256,768]{1,0:T(8,128)(2,1)S(1)} %final.1.refs_3_.refs_1_), channel_id=1, source_target_pairs={{0,1},{1,0},{2,3},{3,2},{4,5},{5,4},{6,7},{7,6},{8,9},{9,8},{10,11... | collective-permute-start | bytes 1179656 | tf_op jit(solution)/shard_map/ppermute | solution.py:831
  276.0 31.5 %collective-permute-start.40 = (bf16[256,768]{1,0:T(8,128)(2,1)S(1)}, bf16[256,768]{1,0:T(8,128)(2,1)S(1)}, u32[]{:S(2)}, u32[]{:S(2)}) collective-permute-start(bf16[256,768]{1,0:T(8,128)(2,1)S(1)} %keep.5.refs_3_), channel_id=1, source_target_pairs={{0,1},{1,0},{2,3},{3,2},{4,5},{5,4},{6,7},{7,6},{8,9},{9,8},{10,11... | collective-permute-start | bytes 1179656 | tf_op jit(solution)/shard_map/ppermute | solution.py:831
  276.6 23.0 %collective-permute-start.46 = (bf16[96,768]{1,0:T(8,128)(2,1)S(1)}, bf16[96,768]{1,0:T(8,128)(2,1)S(1)}, u32[]{:S(2)}, u32[]{:S(2)}) collective-permute-start(bf16[96,768]{1,0:T(8,128)(2,1)S(1)} %get-tuple-element.191), channel_id=1, source_target_pairs={{0,4},{1,5},{2,0},{3,1},{4,6},{5,7},{6,2},{7,3},{8,12},{9,13},{10,... | collective-permute-start | bytes 442376 | tf_op jit(solution)/shard_map/ppermute | solution.py:841
  279.8 37.4 %collective-permute-start.48 = (bf16[112,1024]{1,0:T(8,128)(2,1)S(1)}, bf16[112,1024]{1,0:T(8,128)(2,1)S(1)}, u32[]{:S(2)}, u32[]{:S(2)}) collective-permute-start(bf16[112,1024]{1,0:T(8,128)(2,1)S(1)} %get-tuple-element.192), channel_id=1, source_target_pairs={{0,4},{1,5},{2,0},{3,1},{4,6},{5,7},{6,2},{7,3},{8,12},{9,13},{10,... | collective-permute-start | bytes 688136 | tf_op jit(solution)/shard_map/ppermute | solution.py:841
  299.6 17.5 %collective-permute-start.47 = (bf16[112,1024]{1,0:T(8,128)(2,1)S(1)}, bf16[112,1024]{1,0:T(8,128)(2,1)S(1)}, u32[]{:S(2)}, u32[]{:S(2)}) collective-permute-start(bf16[112,1024]{1,0:T(8,128)(2,1)S(1)} %get-tuple-element.188.refs_3_), channel_id=1, source_target_pairs={{0,0},{1,1},{2,4},{3,5},{4,2},{5,3},{6,6},{7,7},{8,8},{9,9},{10,12... | collective-permute-start | bytes 688136 | tf_op jit(solution)/shard_map/ppermute | solution.py:841
  301.6 15.6 %collective-permute-start.45 = (bf16[96,768]{1,0:T(8,128)(2,1)S(1)}, bf16[96,768]{1,0:T(8,128)(2,1)S(1)}, u32[]{:S(2)}, u32[]{:S(2)}) collective-permute-start(bf16[96,768]{1,0:T(8,128)(2,1)S(1)} %get-tuple-element.179.refs_3_), channel_id=1, source_target_pairs={{0,0},{1,1},{2,4},{3,5},{4,2},{5,3},{6,6},{7,7},{8,8},{9,9},{10,12... | collective-permute-start | bytes 442376 | tf_op jit(solution)/shard_map/ppermute | solution.py:841
  307.4 13.4 %collective-permute-start.44 = (bf16[112,640]{1,0:T(8,128)(2,1)}, bf16[112,640]{1,0:T(8,128)(2,1)S(1)}, u32[]{:S(2)}, u32[]{:S(2)}) collective-permute-start(bf16[112,640]{1,0:T(8,128)(2,1)} %get-tuple-element.190), channel_id=1, source_target_pairs={{0,4},{1,5},{2,0},{3,1},{4,6},{5,7},{6,2},{7,3},{8,12},{9,13},{10,... | collective-permute-start | bytes 430088 | tf_op jit(solution)/shard_map/ppermute | solution.py:841
  307.4 13.4 %collective-permute-start.43 = (bf16[112,640]{1,0:T(8,128)(2,1)S(1)}, bf16[112,640]{1,0:T(8,128)(2,1)S(1)}, u32[]{:S(2)}, u32[]{:S(2)}) collective-permute-start(bf16[112,640]{1,0:T(8,128)(2,1)S(1)} %get-tuple-element.189.refs_5_), channel_id=1, source_target_pairs={{0,0},{1,1},{2,4},{3,5},{4,2},{5,3},{6,6},{7,7},{8,8},{9,9},{10,12... | collective-permute-start | bytes 430088 | tf_op jit(solution)/shard_map/ppermute | solution.py:841
  (65 other events, 361.2 us)
Sparse Core Ops, SparseCore 0:
  24.7 33.5 all-gather.6
  59.8 53.3 all-gather.4

commit v2 on v1

--- a/solution.py
+++ b/solution.py
@@ -34,6 +34,10 @@
 
 def tn(left, right):
     return lax.dot_general(left, right, (((0,), (0,)), ((), ())), preferred_element_type=WIDE)
+
+
+def group_of(spot, i):
+    return (spot[5] ^ (i >> 1)) * 2 + (spot[4] ^ (i & 1))
 
 
 def lanes(group):
@@ -238,8 +242,13 @@
         if held:
             held.append(pltpu.SemaphoreType.DMA((len(held),)))
 
+        scalars = scalars if isinstance(scalars, tuple) else (scalars,)
+        few = len(scalars)
+
         def run(*refs):
-            scalar, ins = refs[0], list(refs[1 : 1 + count])
+            scalar = refs[0] if few == 1 else refs[:few]
+            refs = refs[few - 1 :]
+            ins = list(refs[1 : 1 + count])
             results = list(refs[1 + count + untouched : 1 + count + untouched + len(outs)])
             rest = list(refs[1 + count + untouched + len(outs) :])
             extra = rest[len(rest) - len(held) :] if held else []
@@ -272,8 +281,11 @@
         ]
         results = pl.pallas_call(
             run,
-            out_shape=tuple(jax.ShapeDtypeStruct(shape, kind) for shape, kind in outs),
-            in_specs=[pl.BlockSpec(memory_space=pltpu.SMEM)]
+            out_shape=tuple(
+                pltpu.HBM(shape, kind) if out else jax.ShapeDtypeStruct(shape, kind)
+                for (shape, kind), out in zip(outs, far_out)
+            ),
+            in_specs=[pl.BlockSpec(memory_space=pltpu.SMEM)] * few
             + [outside if out or hbm else whole for out in far_in]
             + [pl.BlockSpec(memory_space=pl.ANY)] * untouched,
             out_specs=tuple(outside if out else whole for out in far_out),
@@ -281,7 +293,7 @@
             compiler_params=pltpu.CompilerParams(vmem_limit_bytes=limit << 20),
             cost_estimate=pl.CostEstimate(flops=1, bytes_accessed=1, transcendentals=0),
             name=name,
-        )(scalars, *arrays, *waits)
+        )(*scalars, *arrays, *waits)
         self.last = (min(results, key=lambda r: r.size * r.dtype.itemsize),)
         return results
 
@@ -312,7 +324,7 @@
     outs += [((8, 512), WIDE)] if stage == 2 else []
 
     def kernel(flags, *refs):
-        backward_kernel(stage, Active(flags), flags, *refs)
+        backward_kernel(stage, Active(flags), flags[0], *refs)
 
     return call(
         kernel, ("attend_cd", "attend_a", "attend_b")[stage], flags, list(arrays) + list(more),
@@ -334,12 +346,53 @@
 
 
 class Active:
-    def __init__(self, flags):
-        self.flags = flags
+    def __init__(self, scalars):
+        self.spot, self.docs = scalars
+
+    def ends(self, start):
+        return self.docs[self.spot[2], start], self.docs[self.spot[2], start + TILE - 1]
 
     def __getitem__(self, where):
         tile, number = where
-        return self.flags[4 + tile * 8 + number]
+        k, l, x = self.spot[0], self.spot[1], self.spot[3]
+        first, last = self.ends(((2 * x + l) * 2 + (k if tile == 0 else 1 - k)) * TILE)
+        block = number // 2
+        far, side = block // 2, block % 2
+        own = 2 * (x + far - 2 * x * far) + (k + side - 2 * k * side)
+        low, high = self.ends((own * 2 + number % 2) * TILE)
+        return jnp.where((low <= last) & (high >= first), 1, 0)
+
+
+def column_of(row):
+    return jnp.broadcast_to(row, (8, row.shape[1])).T[:, 0:1]
+
+
+def docs_kernel(spot, segments, one, two, three, four, five, six, *outs):
+    docs_q, docs_col, docs_a, docs_b, docs_cd, params = outs
+    k, l, x = spot[0], spot[1], spot[3]
+    rows = docs_q.shape[1]
+    half = rows // 2
+    line = jnp.where(spot[2] == 0, segments[0:1, :], segments[1:2, :]).astype(WIDE)
+    pieces = [line[:, i * half : (i + 1) * half] for i in range(8)]
+
+    def pick(index):
+        out = pieces[0]
+        for i in range(1, 8):
+            out = jnp.where(index == i, pieces[i], out)
+        return out
+
+    start = (2 * x + l) * 2
+    docs_q[:, :half] = pick(start + k).astype(jnp.int32)
+    docs_q[:, half:] = pick(start + 1 - k).astype(jnp.int32)
+    blocks = (2 * x + k, 2 * x + 1 - k, 2 * (1 - x) + k, 2 * (1 - x) + 1 - k)
+    targets = ((docs_a, 0), (docs_b, 0), (docs_cd, 0), (docs_cd, rows))
+    for i, (block, (out, first)) in enumerate(zip(blocks, targets)):
+        for j in range(2):
+            column = column_of(pick(2 * block + j)).astype(jnp.int32)
+            out[first + j * half : first + (j + 1) * half, :] = column
+            docs_col[i * rows + j * half : i * rows + (j + 1) * half, :] = column
+    for i, value in enumerate((one, two, three, four, five, six)):
+        params[i : i + 1, :] = value[...].reshape(1, -1)
 
 
 def pick_kernel(spot, inputs, cotangent, block, beside, kept, sem):
@@ -359,7 +412,9 @@
     beside[:rows] = block[...]
 
 
-def own_kernel(spot, block, got, kept, own, peer, grad):
+def settle_kernel(
+    spot, block, got, kept, one, two, own_d, got_d, up, output, own, peer, grad, pair_a, pair_d, own_uo
+):
     k = spot[0]
     rows, half = block.shape[0], own.shape[0]
     mine = pl.ds(pl.multiple_of(k * half, half), half)
@@ -377,66 +432,103 @@
         peer[...] = got[other, :]
         grad[...] = got[rows:, :]
 
-
-def pack_kernel(_, key, value, query, bias, down, own_a, own_d):
-    count = key.shape[0]
-    own_a[0:16, :] = bias[...].astype(LOW)
-    body = jnp.concatenate(
-        [key[...], value[...], query[...], jnp.zeros((count, DH), WIDE)], axis=1
-    )
-    own_a[16 : 16 + count, :] = body.astype(LOW)
-    own_d[...] = down[...].astype(LOW)
-
-
-def pack_uo_kernel(_, up, output, own_uo):
+    pair_a[0] = one[...]
+    pair_a[1] = two[...]
+    pair_d[0] = own_d[...]
+    pair_d[1] = got_d[...]
     count, hidden = up.shape
     own_uo[:, :hidden] = up[...].astype(LOW)
     turned = jnp.concatenate([jnp.zeros((count, DH), WIDE), output[...].T], axis=1)
-    own_uo[:, hidden : hidden + 256] = turned.astype(LOW)
-    own_uo[:, hidden + 256 :] = jnp.zeros((count, own_uo.shape[1] - hidden - 256), LOW)
-
-
-def spread_kernel(spot, mine, got, out, bias):
+    own_uo[:, hidden:] = turned.astype(LOW)
+
+
+def in_three(value):
+    high = value.astype(LOW)
+    rest = value - high.astype(WIDE)
+    middle = rest.astype(LOW)
+    return high, middle, (rest - middle.astype(WIDE)).astype(LOW)
+
+
+def pack_kernel(_, key, value, query, down, query_bias, value_bias, up_bias, own_a, own_d):
+    count, quarter = key.shape
+    gap = jnp.zeros((1, quarter), WIDE)
+    line = jnp.concatenate(
+        [gap, value_bias[...].reshape(1, -1), query_bias[...].reshape(1, -1), gap[:, :DH]], axis=1
+    )
+    units = up_bias[...].reshape(1, -1)
+    own_a[0:16, :] = jnp.zeros((16, 640), LOW)
+    for i, part in enumerate(in_three(line)):
+        own_a[i : i + 1, :] = part
+    for i, part in enumerate(in_three(units)):
+        own_a[3 + 2 * i : 4 + 2 * i, :] = part[:, :640]
+        own_a[4 + 2 * i : 5 + 2 * i, 0:128] = part[:, 640:]
+    body = jnp.concatenate(
+        [key[...], value[...], query[...], jnp.zeros((count, DH), WIDE)], axis=1
+    )
+    own_a[16 : 16 + count, :] = body.astype(LOW)
+    own_d[...] = down[...].astype(LOW)
+
+
+def spread_kernel(
+    spot, mine, got, block, one, two, pair_d, got_d, out, kept, pair_uo, rows_d, kv_bias, q_bias, u_bias
+):
     count = out.shape[2]
     l, h = spot[1], spot[2]
     for part, ql in ((mine, l), (got, 1 - l)):
         for a in range(2):
             out[h ^ a, ql] = part[a, 16 : 16 + count, :]
-        bias[ql] = part[0, 0:16, :]
-
-
-def project_kernel(where, *refs):
-    parts, (a, b, c, d, own, peer, kv_bias, q_bias) = refs[:4], refs[4:12]
-    kv, q, wkv, wq, far_a, far_b, far_cd, far_q = refs[12:20]
+    kept[...] = block[...]
+    pair_uo[0] = one[...]
+    pair_uo[1] = two[...]
+    for i, ref in enumerate((pair_d, got_d)):
+        for j in range(2):
+            rows_d[i + 2 * j] = ref[j]
+    lower = l == 0
+    first, second = mine[0, 0:16, :].astype(WIDE), got[0, 0:16, :].astype(WIDE)
+    for ql, block in enumerate(
+        (jnp.where(lower, first, second), jnp.where(lower, second, first))
+    ):
+        line = (block[0:1] + block[1:2]) + block[2:3]
+        kv_bias[:, ql * 384 : ql * 384 + 384] = line[:, 0:384]
+        q_bias[:, ql * 256 : ql * 256 + 256] = line[:, 384:640]
+        for j, (start, size) in enumerate(((0, 640), (640, 128))):
+            part = (block[3 + j : 4 + j] + block[5 + j : 6 + j]) + block[7 + j : 8 + j]
+            base = ql * 768 + start
+            u_bias[:, base : base + size] = part[:, :size]
+
+
+def join_kernel(where, *refs):
+    parts, (mine, got), (wkv, wq, mine_uo) = refs[:4], refs[4:6], refs[6:9]
     for i, part in enumerate(parts):
         for row in range(2):
             for ql in range(2):
                 at_kv, at_q = slice(ql * 384, ql * 384 + 384), slice(ql * 256, ql * 256 + 256)
-                wkv[where[i], row, :, at_kv] = part[row, ql, :, 0:384]
-                wq[where[i], row, :, at_q] = part[row, ql, :, 384:640]
-    width = 8 * wkv.shape[2]
-    of_kv, of_q = wkv[...].reshape(width, 768), wq[...].reshape(width, 512)
+                wkv[group_of(where, i), row, :, at_kv] = part[row, ql, :, 0:384]
+                wq[group_of(where, i), row, :, at_q] = part[row, ql, :, 384:640]
+    h, l = where[2], where[1]
+    for a in range(2):
+        mine_uo[h ^ a, l] = mine[a]
+        mine_uo[h ^ a, 1 - l] = got[a]
+
+
+def project_kernel(_, wkv, wq, a, b, c, d, own, peer, kv_bias, q_bias, kv, q, *far):
+    far_a, far_b, far_cd, far_q = far
     rows = a.shape[0]
     for i, block in enumerate((a, b, c, d)):
-        part = (nn(block[:rows, :], of_kv) + kv_bias[...]).astype(LOW)
+        part = (nn(block[:rows, :], wkv[...]) + kv_bias[...]).astype(LOW)
         kv[i * rows : (i + 1) * rows, :] = part
         target = (far_a, far_b, far_cd, far_cd)[i]
         start = rows if i == 3 else 0
         target[start : start + rows, :] = part
     half, scale = rows // 2, jnp.asarray(1.0 / DH**0.5, LOW)
     for i, block in enumerate((own, peer)):
-        part = (nn(block[...], of_q) + q_bias[...]).astype(LOW) * scale
+        part = (nn(block[...], wq[...]) + q_bias[...]).astype(LOW) * scale
         q[i * half : (i + 1) * half, :] = part
         far_q[i * half : (i + 1) * half, :] = part
 
 
 def copy_kernel(_, source, out):
     out[...] = source[...]
-
-
-def give_kernel(spot, gathered, out):
-    for i in range(2):
-        out[i] = gathered[2 * (1 - spot[0]) + i, :, : out.shape[2]]
 
 
 def give_groups_kernel(spot, gathered, out):
@@ -456,8 +548,8 @@
         for row in range(2):
             for ql in range(2):
                 at_u, at_o = slice(ql * 768, ql * 768 + 768), slice(ql * 256, ql * 256 + 256)
-                wu[where[i], row, :, at_u] = part[row, ql, :, 0:768]
-                wo[where[i], row, :, at_o] = part[row, ql, :, 768:1024]
+                wu[group_of(where, i), row, :, at_u] = part[row, ql, :, 0:768]
+                wo[group_of(where, i), row, :, at_o] = part[row, ql, :, 768:1024]
     two_halves(nt(o[...], wo[...].reshape(8 * wo.shape[2], 512)), own, peer)
 
 
@@ -508,12 +600,12 @@
 
 
 def down_join_kernel(where, gathered, got, act, wd, own, peer):
-    k = where[4]
+    k = where[0]
     for i in range(4):
         for ql in range(2):
             columns = slice(ql * 768, ql * 768 + 768)
-            wd[where[i], k, :, columns] = gathered[2 * k + ql, i]
-            wd[where[i], 1 - k, :, columns] = got[ql, i]
+            wd[group_of(where, i), k, :, columns] = gathered[2 * k + ql, i]
+            wd[group_of(where, i), 1 - k, :, columns] = got[ql, i]
     two_halves(nt(act[...], wd[...].reshape(8 * wd.shape[2], wd.shape[3])), own, peer)
 
 
@@ -590,7 +682,7 @@
 
 
 def group_rows(me, i, count):
-    return pl.ds(pl.multiple_of((me[0] ^ i) * count, 64), count)
+    return pl.ds(pl.multiple_of(group_of(me, i) * count, 64), count)
 
 
 def grad_d_kernel(me, own, peer, act, kept, sent, turned, whole):
@@ -734,23 +826,26 @@
                 out[count + 8 :] = low
 
 
-def shard_uo_kernel(_, d_one, d_two, one, two, down, up, output, shared):
+def shard_uo_kernel(_, d_one, d_two, one, two, down, up, output, *sums):
     count = up.shape[0]
     down[...] = d_one[...].astype(WIDE) + d_two[...].astype(WIDE)
     total = one[:count].astype(WIDE) + two[:count].astype(WIDE)
     up[...] = total[:, 0:768]
     output[...] = total[:, 768 + DH : 1024].T
     ride = ride_of(one[count:]) + ride_of(two[count:])
-    shared[...] = ride[:, 0:768]
-
-
-def shard_a_kernel(_, one, two, key, value, query, sums):
+    for i, out in enumerate(sums):
+        out[...] = ride[i : i + 1, 0:768].reshape(768)
+
+
+def shard_a_kernel(_, one, two, key, value, query, q_sum, v_sum):
     count, n = key.shape
     total = one[:count].astype(WIDE) + two[:count].astype(WIDE)
     key[...] = total[:, 0:n]
     value[...] = total[:, n : 2 * n]
     query[...] = total[:, 2 * n : 3 * n]
-    sums[...] = ride_of(one[count:]) + ride_of(two[count:])
+    line = (ride_of(one[count:]) + ride_of(two[count:]))[0:1, :]
+    v_sum[...] = line[:, n : 2 * n].reshape(n)
+    q_sum[...] = line[:, 2 * n : 3 * n].reshape(n)
 
 
 def pair_kernel(_, one, two, out):
@@ -758,16 +853,11 @@
     out[1] = two[...]
 
 
-def line_kernel(where, one, two, out):
-    for i, ref in enumerate((one, two)):
-        for j in range(2):
-            out[i + 2 * j] = ref[j]
-
-
-def output_kernel(where, mine, got, out):
+def output_kernel(spot, mine, got, out):
+    l, h = spot[1], spot[2]
     for a in range(2):
-        out[where[2 * a], where[4]] = mine[a]
-        out[where[2 * a], where[5]] = got[a]
+        out[h ^ a, l] = mine[a]
+        out[h ^ a, 1 - l] = got[a]
 
 
 def grad_qkv_kernel(
@@ -806,10 +896,9 @@
         out[count + 8 : count + 9, :] = low
 
 
-def place_kernel(where, *refs):
-    out = refs[-1]
-    for i, piece in enumerate(refs[:-1]):
-        out[where[2 * i], where[2 * i + 1]] = piece[...]
+def place_kernel(spot, *refs):
+    for (a, b), piece in zip(BITS, refs[:4]):
+        refs[4][spot[2] ^ a, spot[1] ^ b] = piece[...]
 
 
 def sum_kernel(spot, near, got_b, got_c, kept, sent):
@@ -879,12 +968,7 @@
     def at(*indices):
         return jnp.stack([jnp.asarray(i, jnp.int32) for i in indices])
 
-    spot = at(k, l, h, 0)
-    if square:
-        me = at(f * 2 + x, k)
-        groups = at(*[(f ^ df) * 2 + (x ^ dx) for df, dx in BITS], k, h, l)
-    else:
-        me, groups = at(0, k), at(0, 1, 2, 3, k, h, l)
+    spot = at(k, l, h, x, *((x, f) if square else (0, 0)))
 
     def exchange(values):
         near, side, far = values
@@ -903,48 +987,12 @@
 
     call = Order()
 
-    docs = lax.dynamic_index_in_dim(segment_ids, h, 0, keepdims=False)
-
-    def docs_at(start, size):
-        return lax.dynamic_slice_in_dim(docs, start, size, 0)
-
-    docs_k = jnp.concatenate(
-        [
-            docs_at((2 * x + k) * rows, rows),
-            docs_at((2 * x + 1 - k) * rows, rows),
-            docs_at((2 * (1 - x) + k) * rows, rows),
-            docs_at((2 * (1 - x) + 1 - k) * rows, rows),
-        ]
-    )
-    start = (2 * x + l) * rows
-    docs_q = jnp.concatenate(
-        [docs_at(start + k * half, half), docs_at(start + (1 - k) * half, half)]
-    )
-    tiles_q, tiles_k = docs_q.reshape(-1, TILE), docs_k.reshape(-1, TILE)
-    active = (
-        (tiles_k[None, :, 0] <= tiles_q[:, None, -1])
-        & (tiles_k[None, :, -1] >= tiles_q[:, None, 0])
-    ).astype(jnp.int32)
-    flags = jnp.concatenate([spot, active.reshape(-1)])
-    docs_row, docs_col = docs_q[None, :], docs_k[:, None]
-    docs_a, docs_b, docs_cd = docs_col[:rows], docs_col[rows : 2 * rows], docs_col[2 * rows :]
-    params = jnp.stack(
-        [output_bias, first_gain, first_shift, down_bias, second_gain, second_shift]
-    )
-
-    biases = jnp.concatenate([query_bias, value_bias, up_bias])
-    bias_high = lax.reduce_precision(biases, 8, 7)
-    bias_middle = lax.reduce_precision(biases - bias_high, 8, 7)
-    bias_low = biases - bias_high - bias_middle
-    bias_rows = jnp.concatenate(
-        [bias_high, bias_middle, bias_low, jnp.zeros((16 * 640 - 3 * biases.shape[0],), WIDE)]
-    ).reshape(16, 640)
     uo_width = hidden + 256
     own_a, own_d = call(
         pack_kernel, "pack", spot,
-        [key_weight, value_weight, query_weight, bias_rows, down_weight.T],
+        [key_weight, value_weight, query_weight, down_weight.T, query_bias, value_bias, up_bias],
         [((16 + shard, 640), LOW), ((shard, hidden), LOW)],
-        far=(True, False),
+        far=((True,) * 4 + (False,) * 3, False),
     )
     pieces = [move(own_a, lambda c, hh, ll, a=a: (hh, c ^ a, ll)) for a in range(2)]
     tall = rows + half
@@ -954,78 +1002,63 @@
         [pltpu.SemaphoreType.DMA((3,))], hbm=True,
     )
     block_c = flip(block_a, "cx")
-    pair_a = call(pair_kernel, "pair_a", spot, pieces, [((2, 16 + shard, 640), LOW)])[0]
+    docs_row, docs_col, docs_a, docs_b, docs_cd, params = call(
+        docs_kernel, "docs", spot,
+        [
+            segment_ids, output_bias, first_gain, first_shift, down_bias, second_gain,
+            second_shift,
+        ],
+        [
+            ((1, rows), jnp.int32), ((4 * rows, 1), jnp.int32), ((rows, 1), jnp.int32),
+            ((rows, 1), jnp.int32), ((2 * rows, 1), jnp.int32), ((6, width), WIDE),
+        ],
+    )
+    flags = (spot, segment_ids)
+    got_ab = flip(beside_a, "cc")
+    near_d = flip(own_d, "fsdp") if square else own_d
+    tokens_own, tokens_peer, grad_out, pair_a, pair_d, own_uo = call(
+        settle_kernel, "settle", spot,
+        [block_a, got_ab, cot_kept] + pieces + [own_d, near_d, up_weight, output_weight],
+        [((half, width), LOW)] * 3
+        + [
+            ((2, 16 + shard, 640), LOW), ((2, shard, hidden), LOW),
+            ((shard, uo_width), LOW),
+        ], far=((False,) * 7 + (True,) * 2, False),
+    )
     got_pair = flip(pair_a, "tl")
-    own_uo = call(
-        pack_uo_kernel, "pack_uo", spot, [up_weight, output_weight],
-        [((shard, uo_width + 384), LOW)], far=(True, False),
-    )[0]
-    uo = lax.all_gather(own_uo, ("th", "tl"), axis=0)
-    if square:
-        pair_d = call(
-            pair_kernel, "pair_d", spot, [own_d, flip(own_d, "fsdp")], [((2, shard, hidden), LOW)]
-        )[0]
-    got_ab = flip(beside_a, "cc")
-    tokens_own, tokens_peer, grad_out = call(
-        own_kernel, "own", spot, [block_a, got_ab, cot_kept], [((half, width), LOW)] * 3
-    )
-    if square:
-        rows_d = call(
-            line_kernel, "line_d", spot, [pair_d, flip(pair_d, "cx")],
-            [((4, shard, hidden), LOW)],
-        )[0]
-    else:
+    next_d = flip(pair_d, "cx") if square else pair_d
+    pieces_uo = [move(own_uo, lambda c, hh, ll, a=a: (hh, c ^ a, ll)) for a in range(2)]
+    mine_a, kept_c, pair_uo, rows_d, kv_bias, q_bias, u_bias = call(
+        spread_kernel, "spread", spot,
+        [pair_a, got_pair, block_c] + pieces_uo + [pair_d, next_d],
+        [
+            ((2, 2, shard, 640), LOW), ((rows, width), LOW), ((2, shard, uo_width), LOW),
+            ((4, shard, hidden), LOW), ((1, 768), WIDE), ((1, 512), WIDE), ((1, 1536), WIDE),
+        ],
+    )
+    if not square:
         rows_d = lax.all_gather(own_d, plane, axis=0)
     all_d = lax.all_gather(rows_d, ("th", "tl"), axis=0)
-    kept_c = call(
-        copy_kernel, "keep", spot, [block_c], [((rows, width), LOW)],
-        after=(params, docs_row, docs_col, docs_a, docs_b, docs_cd, flags),
-    )[0]
-    mine_a, bias_full = call(
-        spread_kernel, "spread", spot, [pair_a, got_pair],
-        [((2, 2, shard, 640), LOW), ((2, 16, 640), LOW)],
-    )
+    got_uo = flip(pair_uo, "tl")
     block_d = flip(kept_c, "cc")
     plane_a = around(mine_a)
-    spots_a = at(*[i for a, b in BITS for i in (h ^ a, l ^ b)])
-    bias_full = bias_full.reshape(2, -1).astype(WIDE)
-    count = biases.shape[0]
-    bias_parts = (
-        bias_full[:, :count] + bias_full[:, count : 2 * count]
-    ) + bias_full[:, 2 * count : 3 * count]
-    given = call(give_kernel, "give", spot, [uo], [((2, shard, uo_width), LOW)])[0]
-    uo_got = flip(given, "cc")
-
-    zeros = jnp.zeros((quarter,), WIDE)
-    kv_bias = jnp.concatenate(
-        [zeros, bias_parts[0][quarter : 2 * quarter], zeros, bias_parts[1][quarter : 2 * quarter]]
-    )[None, :]
-    q_bias = jnp.concatenate(
-        [bias_parts[0][:quarter], zeros[:DH], bias_parts[1][:quarter], zeros[:DH]]
-    )[None, :]
-    u_bias = bias_parts[:, 2 * quarter :].reshape(1, -1)
-
-    def rows_kernel(spot, gathered, got, out):
-        k = spot[0]
-        for ql in range(2):
-            out[k, ql] = gathered[2 * k + ql, :, :uo_width]
-            out[1 - k, ql] = got[ql]
-
-    mine_uo = call(
-        rows_kernel, "rows", spot, [uo, uo_got], [((2, 2, shard, uo_width), LOW)],
-        after=tuple(plane_a),
-    )[0]
+    wkv, wq, mine_uo = call(
+        join_kernel, "join", spot, plane_a + [pair_uo, got_uo],
+        [
+            ((4, 2, eighth, 768), LOW), ((4, 2, eighth, 512), LOW),
+            ((2, 2, shard, uo_width), LOW),
+        ], far=(False, (True, True, False)),
+    )
+    wkv, wq = wkv.reshape(width, 768), wq.reshape(width, 512)
     plane_uo = around(mine_uo)
-    kv, q, wkv, wq, kv_a, kv_b, kv_cd, q_far = call(
-        project_kernel, "project", groups,
-        plane_a + [block_a, got_ab, kept_c, block_d, tokens_own, tokens_peer, kv_bias, q_bias],
+    kv, q, kv_a, kv_b, kv_cd, q_far = call(
+        project_kernel, "project", spot,
+        [wkv, wq, block_a, got_ab, kept_c, block_d, tokens_own, tokens_peer, kv_bias, q_bias],
         [
             ((4 * rows, 768), LOW), ((rows, 512), LOW),
-            ((4, 2, eighth, 768), LOW), ((4, 2, eighth, 512), LOW),
             ((rows, 768), LOW), ((rows, 768), LOW), ((2 * rows, 768), LOW), ((rows, 512), LOW),
-        ], (), 14, far=(False, (False,) * 2 + (True,) * 6), after=(grad_out, u_bias),
-    )
-    wkv, wq = wkv.reshape(width, 768), wq.reshape(width, 512)
+        ], (), 14, far=((True, True) + (False,) * 8, (False,) * 2 + (True,) * 4),
+    )
     o, lse = attention_forward(call, flags, q, kv, docs_row, docs_col)
 
     def core(value):
@@ -1039,7 +1072,7 @@
 
     own_peer = [((half, width), WIDE), ((half, width), LOW)]
     wu, wo, part_own, part_peer = call(
-        branch_kernel, "branch", groups, plane_uo + [o],
+        branch_kernel, "branch", spot, plane_uo + [o],
         [((4, 2, eighth, 2 * hidden), LOW), ((4, 2, eighth, 512), LOW)] + own_peer,
     )
     wu, wo = wu.reshape(width, 2 * hidden), wo.reshape(width, 512)
@@ -1054,7 +1087,7 @@
     )
     if square:
         wd, part_own, part_peer = call(
-            down_join_kernel, "down", groups, [all_d, got_d, act],
+            down_join_kernel, "down", spot, [all_d, got_d, act],
             [((4, 2, eighth, 2 * hidden), LOW)] + own_peer,
         )
         wd = wd.reshape(width, 2 * hidden)
@@ -1076,7 +1109,7 @@
 
     e_peer = core(e_own)
     kept_d, sent_d = call(
-        grad_d_kernel, "grad_d", me, [e_own, e_peer, act],
+        grad_d_kernel, "grad_d", spot, [e_own, e_peer, act],
         [((4 * eighth, 2 * hidden), LOW)] * 2,
         [VMEM((width, rows), LOW), VMEM((width, 2 * hidden), LOW)], 8,
     )
@@ -1095,7 +1128,7 @@
     go = call(mixed_grad_kernel, "mixed_grad", spot, [eb_own, eb_peer, wo], [((rows, 512), LOW)])[0]
     uo_columns = 2 * hidden + 512
     kept_uo, sent_uo = call(
-        grad_uo_kernel, "grad_uo", me,
+        grad_uo_kernel, "grad_uo", spot,
         [first_own, first_peer, units, eb_own, eb_peer, o, small, core(small), sum_u],
         [((4 * eighth + RIDE, uo_columns), LOW)] * 2,
         [VMEM((width, rows), LOW), VMEM((width, uo_columns), LOW)], 8,
@@ -1122,12 +1155,18 @@
         call, 2, flags, [q_far, kv_b, docs_row, docs_b, o, go, lse, wkv],
         [dq_part, wq, grad_one, part_a],
     )
+    parts_a = call(
+        grad_qkv_kernel, "grad_qkv", spot,
+        [
+            block_a, got_ab, kept_c, block_d, tokens_own, tokens_peer, dkv_a, dkv_b, dkv_cd, dq,
+            sum_q, sum_a, sum_b, sum_cd,
+        ],
+        [((2 * eighth + RIDE, 1280), LOW)] * 4,
+        [VMEM((width, 5 * rows), LOW), VMEM((width, 1280), LOW)], 10,
+    )
+    if square:
+        sent_a = exchange(parts_a[1:])
     got_b = core(part_b)
-    out_spots = at(h, h, 1 - h, 1 - h, l, 1 - l)
-    layer_output = call(
-        output_kernel, "output", out_spots, [out_pair, out_got], [((2, 2, half, width), LOW)],
-        far=(False, True),
-    )[0].reshape(2, rows, width)
     if square:
         kept_zd, sent_zd = call(
             merge_d_kernel, "merge_d", spot, [left_d, got_d], [((2, shard, hidden), LOW)] * 2
@@ -1142,18 +1181,11 @@
         sum_kernel, "sum", spot, [part_a, got_b, got_c],
         [((half, width), WIDE), ((half, width), LOW)],
     )
-    parts_a = call(
-        grad_qkv_kernel, "grad_qkv", me,
-        [
-            block_a, got_ab, kept_c, block_d, tokens_own, tokens_peer, dkv_a, dkv_b, dkv_cd, dq,
-            sum_q, sum_a, sum_b, sum_cd,
-        ],
-        [((2 * eighth + RIDE, 1280), LOW)] * 4,
-        [VMEM((width, 5 * rows), LOW), VMEM((width, 1280), LOW)], 10,
-    )
-    if square:
-        sent_a = exchange(parts_a[1:])
     sent = flip(sent, "tl")
+    layer_output = call(
+        output_kernel, "output", spot, [out_pair, out_got], [((2, 2, half, width), LOW)],
+        far=(False, True),
+    )[0].reshape(2, rows, width)
     n = quarter
 
     def to_owner(pieces):
@@ -1226,25 +1258,26 @@
         both = jnp.where(k == h, ride, core(ride))[0].reshape(2, 640)
         sums_a = lax.dynamic_index_in_dim(both, l, 0, keepdims=True)
     grad_inputs = call(
-        place_kernel, "place", spots_a, [final, beside, across, beyond],
+        place_kernel, "place", spot, [final, beside, across, beyond],
         [((2, 2, half, width), LOW)], far=(False, True),
     )[0].reshape(2, rows, width)
     if square:
-        grad_down, grad_up, grad_output, shared = call(
+        grad_down, grad_up, grad_output, *shared = call(
             shard_uo_kernel, "shard_uo", spot, moved_d + moved_uo,
             [
                 ((shard, hidden), WIDE), ((shard, hidden), WIDE), ((n, shard), WIDE),
-                ((8, width), WIDE),
-            ], far=(False, True),
+            ]
+            + [((width,), WIDE)] * 7,
         )
         units_sum = shared[6]
-        grad_key, grad_value, grad_query, sums_a = call(
+        grad_key, grad_value, grad_query, q_sum, v_sum = call(
             shard_a_kernel, "shard_a", spot, moved_a,
-            [((shard, n), WIDE)] * 3 + [((8, 640), WIDE)], far=(False, True),
+            [((shard, n), WIDE)] * 3 + [((n,), WIDE)] * 2,
         )
     if square:
         grad_down = grad_down.T
-    q_sum, v_sum = sums_a[0, 2 * n : 3 * n], sums_a[0, n : 2 * n]
+    else:
+        q_sum, v_sum = sums_a[0, 2 * n : 3 * n], sums_a[0, n : 2 * n]
     units_sum = units_sum.reshape(-1)
 
     return (

time: 335 us -> 307 us (0.916)
  local copies, waits for them, and re-layouts: 34.7 us -> 16.9 us
  Pallas kernels: 107 us -> 90 us
  waiting for transfers between devices: 102 us -> 110 us
    pallas_call x47 -> x42, Pallas kernels: 107 us -> 90 us  [__call__(): pl.pallas_call(run, out_shape=tuple((pltpu.HBM(shape, kind) if out else j...]
    unnamed x127 -> x74, local copies, waits for them, and re-layouts: 25.4 us -> 16.8 us
    all_gather x1, waiting for transfers between devices: 1.87 us -> 7.01 us  [body(): all_d = lax.all_gather(rows_d, ('th', 'tl'), axis=0)]
    slice x8 -> x0, local copies, waits for them, and re-layouts: 4.48 us -> none  [the longest x1 1.05 us: body(): docs_col[2 * rows:]]
    ppermute x9 -> x11, waiting for transfers between devices: 27.6 us -> 29.4 us  [move(): return lax.ppermute(value, ('cc', 'th', 'tl'), pairs)]
    ppermute x9 -> x11, starting transfers between devices: 22.8 us -> 22.9 us  [move(): return lax.ppermute(value, ('cc', 'th', 'tl'), pairs)]
  transfers between devices with their start and end apart: 51 -> 52, of which waited for: 19 -> 21; matrix products, arithmetic and copies ran while one was open for 3% -> 0% of each run, Pallas kernels for 28% -> 25%
where the time goes in v2:
time: 307 us; the launch traced here: 301 us
  waiting for transfers between devices  110 us (36%)
  Pallas kernels  90 us (29%)
  starting transfers between devices  67.9 us (22%)
  local copies, waits for them, and re-layouts  16.9 us (6%)
  between operations  15.3 us (5%)
    pallas_call x42, Pallas kernels, __call__(): pl.pallas_call(run, out_shape=tuple((pltpu.HBM(shape, kind) if out else j...  90 us
    ppermute x37, waiting for transfers between devices, flip(): return lax.ppermute(value, axis, FLIP)  63.7 us
    ppermute x37, starting transfers between devices, flip(): return lax.ppermute(value, axis, FLIP)  42.5 us
    ppermute x11, waiting for transfers between devices, move(): return lax.ppermute(value, ('cc', 'th', 'tl'), pairs)  29.4 us
    ppermute x11, starting transfers between devices, move(): return lax.ppermute(value, ('cc', 'th', 'tl'), pairs)  22.9 us
    unnamed x74, local copies, waits for them, and re-layouts  16.8 us
    ppermute x3, waiting for transfers between devices, exchange(): lax.ppermute(far, plane, [(i, i ^ 3) for i in range(4)])  10.3 us
    all_gather x1, waiting for transfers between devices, body(): all_d = lax.all_gather(rows_d, ('th', 'tl'), axis=0)  7.01 us
  transfers between devices with their start and end apart: 52, of which 21 were waited for; matrix products, arithmetic and copies ran while one was open for 0% of the time, Pallas kernels for 25%

profile of v2, /device:TPU:1, one launch (start us, length us, event | category | flops | bytes accessed | tf_op | source)
XLA Modules:
  0.0 300.5 jit_solution(18172459647617248486)
XLA Ops:
  9.4 1.8 pack.1
  11.3 2.0 pick.1
  13.4 2.7 collective-permute-start.5
  17.9 4.1 %collective-permute-start.1 = (bf16[112,640]{1,0:T(8,128)(2,1)S(1)}, bf16[112,640]{1,0:T(8,128)(2,1)S(1)}, u32[]{:S(2)}, u32[]{:S(2)}) collective-permute-start(bf16[112,640]{1,0:T(8,128)(2,1)S(1)} %get-tuple-element.131.refs_3_), channel_id=1, source_target_pairs={{0,0},{1,1},{2,4},{3,5},{4,2},{5,3},{6,6},{7,7},{8,8},{9,9},{10,12... | collective-permute-start | bytes 430088 | tf_op jit(solution)/shard_map/ppermute | solution.py:930
  26.9 1.8 settle.1
  29.7 1.7 collective-permute-start.4
  32.2 5.0 %collective-permute-start.6 = (bf16[96,1024]{1,0:T(8,128)(2,1)S(1)}, bf16[96,1024]{1,0:T(8,128)(2,1)S(1)}, u32[]{:S(2)}, u32[]{:S(2)}) collective-permute-start(bf16[96,1024]{1,0:T(8,128)(2,1)S(1)} %get-tuple-element.138.refs_8_), channel_id=1, source_target_pairs={{0,0},{1,1},{2,4},{3,5},{4,2},{5,3},{6,6},{7,7},{8,8},{9,9},{10,12... | collective-permute-start | bytes 589832 | tf_op jit(solution)/shard_map/ppermute | solution.py:930
  37.2 1.8 collective-permute-done.7.refs_5_
  39.0 3.9 %collective-permute-done.6.refs_4_ = bf16[96,1024]{1,0:T(8,128)(2,1)S(1)} collective-permute-done((bf16[96,1024]{1,0:T(8,128)(2,1)S(1)}, bf16[96,1024]{1,0:T(8,128)(2,1)S(1)}, u32[]{:S(2)}, u32[]{:S(2)}) %collective-permute-start.6) | collective-permute-done | bytes 196640 | tf_op jit(solution)/shard_map/ppermute | solution.py:930
  49.4 1.6 collective-permute-start.12
  51.0 11.9 %collective-permute-done.12.refs_6_ = bf16[2,96,1024]{2,1,0:T(8,128)(2,1)S(1)} collective-permute-done((bf16[2,96,1024]{2,1,0:T(8,128)(2,1)}, bf16[2,96,1024]{2,1,0:T(8,128)(2,1)S(1)}, u32[]{:S(2)}, u32[]{:S(2)}) %collective-permute-start.12) | collective-permute-done | bytes 393248 | tf_op jit(solution)/shard_map/ppermute | solution.py:920
  62.9 8.7 %collective-permute-done.10.refs_3_ = bf16[2,2,96,640]{3,2,1,0:T(8,128)(2,1)S(1)} collective-permute-done((bf16[2,2,96,640]{3,2,1,0:T(8,128)(2,1)}, bf16[2,2,96,640]{3,2,1,0:T(8,128)(2,1)S(1)}, u32[]{:S(2)}, u32[]{:S(2)}) %collective-permute-start.10) | collective-permute-done | bytes 491552 | tf_op jit(solution)/shard_map/ppermute | solution.py:920
  73.7 2.9 join.1
  79.3 6.2 %project.1 = (bf16[2048,768]{1,0:T(8,128)(2,1)S(1)}, bf16[512,512]{1,0:T(8,128)(2,1)S(1)}, bf16[512,768]{1,0:T(8,128)(2,1)}, bf16[512,768]{1,0:T(8,128)(2,1)}, b...) custom-call(s32[6]{0:T(128)S(1)} %stack.24.refs_0_, bf16[768,768]{1,0:T(8,128)(2,1)} %bitcast.23, ...), custom_call_target="tpu_custom_call" | custom-call | flops 1 | bytes 1 | tf_op jit(solution)/shard_map/project/pallas_call | solution.py:282
  85.6 6.5 %attend.1 = (bf16[512,512]{1,0:T(8,128)(2,1)S(1)}, f32[8,512]{1,0:T(8,128)S(1)}) custom-call(s32[6]{0:T(128)S(1)} %stack.24.refs_0_, s32[2,2048]{1,0:T(2,128)S(1)} %copy-done.15, bf16[512,512]{1,0:T(8,128)(2,1)S(1)} %get-tuple-element.150.refs_2_.refs_6_, bf16[2048,768]{1,0:T(8,128)(2,1)S(1)} %get-tuple-element.151.refs_3_, ...), custom_call_target="tpu_custom_call" | custom-call | flops 1 | bytes 1 | tf_op jit(solution)/shard_map/attend/pallas_call | solution.py:282
  92.1 7.0 %all-gather.3.cloned.1.call-done = bf16[16,96,768]{2,1,0:T(8,128)(2,1)} async-done(((bf16[4,96,768]{2,1,0:T(8,128)(2,1)}), bf16[16,96,768]{2,1,0:T(8,128)(2,1)}) %all-gather.3.cloned.1.call-update) | async-done | bytes 2359312 | tf_op jit(solution)/shard_map/all_gather | solution.py:1041
  99.1 1.7 copy-done
  101.9 12.3 %collective-permute-done.16.refs_3_ = bf16[2,2,96,1024]{3,2,1,0:T(8,128)(2,1)} collective-permute-done((bf16[2,2,96,1024]{3,2,1,0:T(8,128)(2,1)}, bf16[2,2,96,1024]{3,2,1,0:T(8,128)(2,1)}, u32[]{:S(2)}, u32[]{:S(2)}) %collective-permute-start.16) | collective-permute-done | bytes 786464 | tf_op jit(solution)/shard_map/ppermute | solution.py:920
  114.2 2.7 branch.1
  121.5 2.7 up.1
  124.2 2.1 down.1
  131.3 2.1 grad_d.1
  133.4 3.3 %units.1 = (bf16[512,1536]{1,0:T(8,128)(2,1)S(1)}, f32[256,768]{1,0:T(8,128)S(1)}, bf16[256,768]{1,0:T(8,128)(2,1)S(1)}, f32[8,1536]{1,0:T(8,128)S(1)}) custom-call(s32[6]{0:T(128)S(1)} %stack.24.refs_0_, bf16[256,768]{1,0:T(8,128)(2,1)S(1)} %get-tuple-element.169.refs_1_, bf16[256,768]{1,0:T(8,128)(2,1)S(1)} %collective-permute-done.22.refs_2_, ...), custom_call_target="tpu_custom_call" | custom-call | flops 1 | bytes 1 | tf_op jit(solution)/shard_map/units/pallas_call | solution.py:282
  137.1 2.2 collective-permute-start.21
  143.2 3.3 %collective-permute-done.21.refs_1_ = bf16[256,768]{1,0:T(8,128)(2,1)S(1)} collective-permute-done((bf16[256,768]{1,0:T(8,128)(2,1)S(1)}, bf16[256,768]{1,0:T(8,128)(2,1)S(1)}, u32[]{:S(2)}, u32[]{:S(2)}) %collective-permute-start.21) | collective-permute-done | bytes 393248 | tf_op jit(solution)/shard_map/ppermute | solution.py:930
  148.2 2.6 grad_uo.1
  151.2 6.1 %attend_cd.1 = (f32[384,512]{1,0:T(8,128)S(1)}, bf16[1024,768]{1,0:T(8,128)(2,1)S(1)}, f32[512,768]{1,0:T(8,128)S(1)}, bf16[512,768]{1,0:T(8,128)(2,1)S(1)}, f32[8,768]{1,0:T(8,128)S(1)}) custom-call(s32[6]{0:T(128)S(1)} %stack.24.refs_0_, s32[2,2048]{1,0:T(2,128)S(1)} %copy-done.16, bf16[512,512]{1,0:T(8,128)(2,1)} %get-tuple-element.180.refs_2_, ...), custom_call_target="tpu_custom_call" | custom-call | flops 1 | bytes 1 | tf_op jit(solution)/shard_map/attend_cd/pallas_call | solution.py:282
  157.4 3.6 %collective-permute-start.24 = (bf16[256,768]{1,0:T(8,128)(2,1)S(1)}, bf16[256,768]{1,0:T(8,128)(2,1)S(1)}, u32[]{:S(2)}, u32[]{:S(2)}) collective-permute-start(bf16[256,768]{1,0:T(8,128)(2,1)S(1)} %keep.2.refs_4_.refs_1_), channel_id=1, source_target_pairs={{0,2},{2,0},{1,3},{3,1},{4,6},{6,4},{5,7},{7,5},{8,10},{10,8},{9,1... | collective-permute-start | bytes 1179656 | tf_op jit(solution)/shard_map/ppermute | solution.py:920
  161.7 6.1 %attend_a.1 = (f32[384,512]{1,0:T(8,128)S(1)}, bf16[512,768]{1,0:T(8,128)(2,1)S(1)}, f32[512,768]{1,0:T(8,128)S(1)}, f32[8,768]{1,0:T(8,128)S(1)}) custom-call(s32[6]{0:T(128)S(1)} %stack.24.refs_0_, s32[2,2048]{1,0:T(2,128)S(1)} %copy-done.16, bf16[512,512]{1,0:T(8,128)(2,1)} %get-tuple-element.180.refs_2_, bf16[512,768]{1,0:T(8,128)(2,1)} %get-tuple-element.181.refs_3_, ...), custom_call_target="tpu_custom_call" | custom-call | flops 1 | bytes 1 | tf_op jit(solution)/shard_map/attend_a/pallas_call | solution.py:282
  168.7 11.3 %collective-permute-start.33 = (bf16[192,1536]{1,0:T(8,128)(2,1)S(1)}, bf16[192,1536]{1,0:T(8,128)(2,1)S(1)}, u32[]{:S(2)}, u32[]{:S(2)}) collective-permute-start(bf16[192,1536]{1,0:T(8,128)(2,1)S(1)} %get-tuple-element.203), channel_id=1, source_target_pairs={{0,8},{8,0},{1,9},{9,1},{2,10},{10,2},{3,11},{11,3},{4,12},{12,4},... | collective-permute-start | bytes 1769480 | tf_op jit(solution)/shard_map/ppermute | solution.py:920
  180.7 12.2 %attend_b.1 = (bf16[512,512]{1,0:T(8,128)(2,1)S(1)}, bf16[512,768]{1,0:T(8,128)(2,1)S(1)}, f32[512,768]{1,0:T(8,128)S(1)}, bf16[512,768]{1,0:T(8,128)(2,1)S(1)},...) custom-call(s32[6]{0:T(128)S(1)} %stack.24.refs_0_, s32[2,2048]{1,0:T(2,128)S(1)} %copy-done.16, ...), custom_call_target="tpu_custom_call" | custom-call | flops 1 | bytes 1 | tf_op jit(solution)/shard_map/attend_b/pallas_call | solution.py:282
  193.0 4.6 %grad_qkv.1 = (bf16[208,1280]{1,0:T(8,128)(2,1)S(1)}, bf16[208,1280]{1,0:T(8,128)(2,1)S(1)}, bf16[208,1280]{1,0:T(8,128)(2,1)S(1)}, bf16[208,1280]{1,0:T(8,128)(2,1)S(1)}) custom-call(s32[6]{0:T(128)S(1)} %stack.24.refs_0_, bf16[512,768]{1,0:T(8,128)(2,1)S(1)} %get-tuple-element.132.refs_1_.refs_3_, ...), custom_call_target="tpu_custom_call" | custom-call | flops 1 | bytes 1 | tf_op jit(solution)/shard_map/grad_qkv/pallas_call | solution.py:282
  198.5 4.4 %collective-permute-done.32.refs_2_ = bf16[400,2048]{1,0:T(8,128)(2,1)S(1)} collective-permute-done((bf16[400,2048]{1,0:T(8,128)(2,1)S(1)}, bf16[400,2048]{1,0:T(8,128)(2,1)S(1)}, u32[]{:S(2)}, u32[]{:S(2)}) %collective-permute-start.32) | collective-permute-done | bytes 1638432 | tf_op jit(solution)/shard_map/ppermute | solution.py:920
  206.2 3.6 %collective-permute-done.31.refs_3_ = bf16[512,768]{1,0:T(8,128)(2,1)S(1)} collective-permute-done((bf16[512,768]{1,0:T(8,128)(2,1)S(1)}, bf16[512,768]{1,0:T(8,128)(2,1)S(1)}, u32[]{:S(2)}, u32[]{:S(2)}) %collective-permute-start.31) | collective-permute-done | bytes 786464 | tf_op jit(solution)/shard_map/ppermute | solution.py:920
  212.0 2.6 collective-permute-start.39
  214.6 3.4 %collective-permute-done.35.refs_2_ = bf16[2,96,768]{2,1,0:T(8,128)(2,1)S(1)} collective-permute-done((bf16[2,96,768]{2,1,0:T(8,128)(2,1)S(1)}, bf16[2,96,768]{2,1,0:T(8,128)(2,1)S(1)}, u32[]{:S(2)}, u32[]{:S(2)}) %collective-permute-start.35) | collective-permute-done | bytes 294944 | tf_op jit(solution)/shard_map/ppermute | solution.py:920
  218.0 1.8 output.1.refs_3_
  221.9 4.5 %collective-permute-done.34.refs_2_ = bf16[256,768]{1,0:T(8,128)(2,1)S(1)} collective-permute-done((bf16[256,768]{1,0:T(8,128)(2,1)S(1)}, bf16[256,768]{1,0:T(8,128)(2,1)S(1)}, u32[]{:S(2)}, u32[]{:S(2)}) %collective-permute-start.34) | collective-permute-done | bytes 393248 | tf_op jit(solution)/shard_map/ppermute | solution.py:920
  227.1 2.1 collective-permute-start.37
  231.6 8.0 %collective-permute-done.38.refs_2_ = bf16[208,1280]{1,0:T(8,128)(2,1)S(1)} collective-permute-done((bf16[208,1280]{1,0:T(8,128)(2,1)S(1)}, bf16[208,1280]{1,0:T(8,128)(2,1)S(1)}, u32[]{:S(2)}, u32[]{:S(2)}) %collective-permute-start.38) | collective-permute-done | bytes 532512 | tf_op jit(solution)/shard_map/ppermute | solution.py:920
  239.5 10.3 %collective-permute-done.40.refs_4_ = bf16[208,1280]{1,0:T(8,128)(2,1)S(1)} collective-permute-done((bf16[208,1280]{1,0:T(8,128)(2,1)S(1)}, bf16[208,1280]{1,0:T(8,128)(2,1)S(1)}, u32[]{:S(2)}, u32[]{:S(2)}) %collective-permute-start.40) | collective-permute-done | bytes 532512 | tf_op jit(solution)/shard_map/ppermute | solution.py:978
  255.1 17.5 %collective-permute-done.48.refs_2_ = bf16[96,768]{1,0:T(8,128)(2,1)S(1)} collective-permute-done((bf16[96,768]{1,0:T(8,128)(2,1)S(1)}, bf16[96,768]{1,0:T(8,128)(2,1)S(1)}, u32[]{:S(2)}, u32[]{:S(2)}) %collective-permute-start.48) | collective-permute-done | bytes 147488 | tf_op jit(solution)/shard_map/ppermute | solution.py:930
  272.6 1.9 collective-permute-start.49
  275.9 3.6 %collective-permute-start.47 = (bf16[96,768]{1,0:T(8,128)(2,1)S(1)}, bf16[96,768]{1,0:T(8,128)(2,1)S(1)}, u32[]{:S(2)}, u32[]{:S(2)}) collective-permute-start(bf16[96,768]{1,0:T(8,128)(2,1)S(1)} %get-tuple-element.216.refs_3_), channel_id=1, source_target_pairs={{0,0},{1,1},{2,4},{3,5},{4,2},{5,3},{6,6},{7,7},{8,8},{9,9},{10,12... | collective-permute-start | bytes 442376 | tf_op jit(solution)/shard_map/ppermute | solution.py:930
  280.3 3.4 %collective-permute-start.45 = (bf16[112,640]{1,0:T(8,128)(2,1)S(1)}, bf16[112,640]{1,0:T(8,128)(2,1)S(1)}, u32[]{:S(2)}, u32[]{:S(2)}) collective-permute-start(bf16[112,640]{1,0:T(8,128)(2,1)S(1)} %get-tuple-element.226.refs_5_), channel_id=1, source_target_pairs={{0,0},{1,1},{2,4},{3,5},{4,2},{5,3},{6,6},{7,7},{8,8},{9,9},{10,12... | collective-permute-start | bytes 430088 | tf_op jit(solution)/shard_map/ppermute | solution.py:930
  283.7 1.8 place.1.refs_5_
  288.1 1.5 shard_uo.1
  289.6 1.6 collective-permute-done.45.refs_1_
  (174 shorter events, 64.6 us)
Async XLA Ops:
  7.2 91.9 %all-gather.3.cloned.1.call-start = ((), (), s32[]{:S(2)}) async-start(), calls=%async_computation | async-start | bytes 2949120 | tf_op jit(solution)/shard_map/all_gather | solution.py:1041
  13.2 13.6 %collective-permute-start = (bf16[768,768]{1,0:T(8,128)(2,1)S(1)}, bf16[768,768]{1,0:T(8,128)(2,1)S(1)}, u32[]{:S(2)}, u32[]{:S(2)}) collective-permute-start(bf16[768,768]{1,0:T(8,128)(2,1)S(1)} %get-tuple-element.133), channel_id=1, source_target_pairs={{0,4},{4,0},{1,5},{5,1},{2,6},{6,2},{3,7},{7,3},{8,12},{12,8},{9,1... | collective-permute-start | bytes 3538952 | tf_op jit(solution)/shard_map/ppermute | solution.py:920
  13.4 23.8 %collective-permute-start.5 = (bf16[512,768]{1,0:T(8,128)(2,1)S(1)}, bf16[512,768]{1,0:T(8,128)(2,1)S(1)}, u32[]{:S(2)}, u32[]{:S(2)}) collective-permute-start(bf16[512,768]{1,0:T(8,128)(2,1)S(1)} %get-tuple-element.132.refs_1_.refs_3_), channel_id=1, source_target_pairs={{0,8},{8,0},{1,9},{9,1},{2,10},{10,2},{3,11},{11,3},{4,12},{12,4},... | collective-permute-start | bytes 2359304 | tf_op jit(solution)/shard_map/ppermute | solution.py:920
  16.0 10.8 %collective-permute-start.3 = (bf16[96,768]{1,0:T(8,128)(2,1)S(1)}, bf16[96,768]{1,0:T(8,128)(2,1)S(1)}, u32[]{:S(2)}, u32[]{:S(2)}) collective-permute-start(bf16[96,768]{1,0:T(8,128)(2,1)S(1)} %get-tuple-element.135.refs_6_), channel_id=1, source_target_pairs={{0,16},{16,0},{1,17},{17,1},{2,18},{18,2},{3,19},{19,3},{4,20},{20... | collective-permute-start | bytes 442376 | tf_op jit(solution)/shard_map/ppermute | solution.py:920
  17.3 9.6 %collective-permute-start.2 = (bf16[112,640]{1,0:T(8,128)(2,1)S(1)}, bf16[112,640]{1,0:T(8,128)(2,1)S(1)}, u32[]{:S(2)}, u32[]{:S(2)}) collective-permute-start(bf16[112,640]{1,0:T(8,128)(2,1)S(1)} %get-tuple-element.131.refs_3_), channel_id=1, source_target_pairs={{0,2},{1,3},{2,6},{3,7},{4,0},{5,1},{6,4},{7,5},{8,10},{9,11},{10,... | collective-permute-start | bytes 430088 | tf_op jit(solution)/shard_map/ppermute | solution.py:930
  17.9 8.9 %collective-permute-start.1 = (bf16[112,640]{1,0:T(8,128)(2,1)S(1)}, bf16[112,640]{1,0:T(8,128)(2,1)S(1)}, u32[]{:S(2)}, u32[]{:S(2)}) collective-permute-start(bf16[112,640]{1,0:T(8,128)(2,1)S(1)} %get-tuple-element.131.refs_3_), channel_id=1, source_target_pairs={{0,0},{1,1},{2,4},{3,5},{4,2},{5,3},{6,6},{7,7},{8,8},{9,9},{10,12... | collective-permute-start | bytes 430088 | tf_op jit(solution)/shard_map/ppermute | solution.py:930
  29.4 13.5 %collective-permute-start.8 = (bf16[2,96,768]{2,1,0:T(8,128)(2,1)S(1)}, bf16[2,96,768]{2,1,0:T(8,128)(2,1)S(1)}, u32[]{:S(2)}, u32[]{:S(2)}) collective-permute-start(bf16[2,96,768]{2,1,0:T(8,128)(2,1)S(1)} %get-tuple-element.139.refs_6_), channel_id=1, source_target_pairs={{0,8},{8,0},{1,9},{9,1},{2,10},{10,2},{3,11},{11,3},{4,12},{12,4},... | collective-permute-start | bytes 884744 | tf_op jit(solution)/shard_map/ppermute | solution.py:920
  29.7 13.3 %collective-permute-start.4 = (bf16[2,112,640]{2,1,0:T(8,128)(2,1)S(1)}, bf16[2,112,640]{2,1,0:T(8,128)(2,1)S(1)}, u32[]{:S(2)}, u32[]{:S(2)}) collective-permute-start(bf16[2,112,640]{2,1,0:T(8,128)(2,1)S(1)} %get-tuple-element.137.refs_1_), channel_id=1, source_target_pairs={{0,1},{1,0},{2,3},{3,2},{4,5},{5,4},{6,7},{7,6},{8,9},{9,8},{10,11... | collective-permute-start | bytes 860168 | tf_op jit(solution)/shard_map/ppermute | solution.py:920
  31.4 7.6 %collective-permute-start.7 = (bf16[96,1024]{1,0:T(8,128)(2,1)S(1)}, bf16[96,1024]{1,0:T(8,128)(2,1)S(1)}, u32[]{:S(2)}, u32[]{:S(2)}) collective-permute-start(bf16[96,1024]{1,0:T(8,128)(2,1)S(1)} %get-tuple-element.138.refs_8_), channel_id=1, source_target_pairs={{0,2},{1,3},{2,6},{3,7},{4,0},{5,1},{6,4},{7,5},{8,10},{9,11},{10,... | collective-permute-start | bytes 589832 | tf_op jit(solution)/shard_map/ppermute | solution.py:930
  32.2 10.7 %collective-permute-start.6 = (bf16[96,1024]{1,0:T(8,128)(2,1)S(1)}, bf16[96,1024]{1,0:T(8,128)(2,1)S(1)}, u32[]{:S(2)}, u32[]{:S(2)}) collective-permute-start(bf16[96,1024]{1,0:T(8,128)(2,1)S(1)} %get-tuple-element.138.refs_8_), channel_id=1, source_target_pairs={{0,0},{1,1},{2,4},{3,5},{4,2},{5,3},{6,6},{7,7},{8,8},{9,9},{10,12... | collective-permute-start | bytes 589832 | tf_op jit(solution)/shard_map/ppermute | solution.py:930
  46.6 16.3 %collective-permute-start.11 = (bf16[2,2,96,640]{3,2,1,0:T(8,128)(2,1)}, bf16[2,2,96,640]{3,2,1,0:T(8,128)(2,1)S(1)}, u32[]{:S(2)}, u32[]{:S(2)}) collective-permute-start(bf16[2,2,96,640]{3,2,1,0:T(8,128)(2,1)} %copy-done.12), channel_id=1, source_target_pairs={{0,24},{8,16},{16,8},{24,0},{1,25},{9,17},{17,9},{25,1},{2,26},{10... | collective-permute-start | bytes 1474568 | tf_op jit(solution)/shard_map/ppermute | solution.py:978
  47.8 23.8 %collective-permute-start.10 = (bf16[2,2,96,640]{3,2,1,0:T(8,128)(2,1)}, bf16[2,2,96,640]{3,2,1,0:T(8,128)(2,1)S(1)}, u32[]{:S(2)}, u32[]{:S(2)}) collective-permute-start(bf16[2,2,96,640]{3,2,1,0:T(8,128)(2,1)} %copy-done.12), channel_id=1, source_target_pairs={{0,16},{16,0},{1,17},{17,1},{2,18},{18,2},{3,19},{19,3},{4,20},{20... | collective-permute-start | bytes 1474568 | tf_op jit(solution)/shard_map/ppermute | solution.py:920
  49.1 22.5 %collective-permute-start.9 = (bf16[2,2,96,640]{3,2,1,0:T(8,128)(2,1)}, bf16[2,2,96,640]{3,2,1,0:T(8,128)(2,1)S(1)}, u32[]{:S(2)}, u32[]{:S(2)}) collective-permute-start(bf16[2,2,96,640]{3,2,1,0:T(8,128)(2,1)} %copy-done.12), channel_id=1, source_target_pairs={{0,8},{8,0},{1,9},{9,1},{2,10},{10,2},{3,11},{11,3},{4,12},{12,4},... | collective-permute-start | bytes 1474568 | tf_op jit(solution)/shard_map/ppermute | solution.py:920
  49.4 13.5 %collective-permute-start.12 = (bf16[2,96,1024]{2,1,0:T(8,128)(2,1)}, bf16[2,96,1024]{2,1,0:T(8,128)(2,1)S(1)}, u32[]{:S(2)}, u32[]{:S(2)}) collective-permute-start(bf16[2,96,1024]{2,1,0:T(8,128)(2,1)} %copy-done.19), channel_id=1, source_target_pairs={{0,1},{1,0},{2,3},{3,2},{4,5},{5,4},{6,7},{7,6},{8,9},{9,8},{10,11... | collective-permute-start | bytes 1179656 | tf_op jit(solution)/shard_map/ppermute | solution.py:920
  51.0 28.3 %collective-permute-start.13 = (bf16[512,768]{1,0:T(8,128)(2,1)S(1)}, bf16[512,768]{1,0:T(8,128)(2,1)S(1)}, u32[]{:S(2)}, u32[]{:S(2)}) collective-permute-start(bf16[512,768]{1,0:T(8,128)(2,1)S(1)} %get-tuple-element.146.refs_5_.refs_3_), channel_id=1, source_target_pairs={{0,4},{4,0},{1,5},{5,1},{2,6},{6,2},{3,7},{7,3},{8,12},{12,8},{9,1... | collective-permute-start | bytes 2359304 | tf_op jit(solution)/shard_map/ppermute | solution.py:920
  76.6 25.3 %collective-permute-start.17 = (bf16[2,2,96,1024]{3,2,1,0:T(8,128)(2,1)}, bf16[2,2,96,1024]{3,2,1,0:T(8,128)(2,1)}, u32[]{:S(2)}, u32[]{:S(2)}) collective-permute-start(bf16[2,2,96,1024]{3,2,1,0:T(8,128)(2,1)} %get-tuple-element.154.refs_1_), channel_id=1, source_target_pairs={{0,24},{8,16},{16,8},{24,0},{1,25},{9,17},{17,9},{25,1},{2,26},{10... | collective-permute-start | bytes 2359304 | tf_op jit(solution)/shard_map/ppermute | solution.py:978
  77.8 36.4 %collective-permute-start.16 = (bf16[2,2,96,1024]{3,2,1,0:T(8,128)(2,1)}, bf16[2,2,96,1024]{3,2,1,0:T(8,128)(2,1)}, u32[]{:S(2)}, u32[]{:S(2)}) collective-permute-start(bf16[2,2,96,1024]{3,2,1,0:T(8,128)(2,1)} %get-tuple-element.154.refs_1_), channel_id=1, source_target_pairs={{0,16},{16,0},{1,17},{17,1},{2,18},{18,2},{3,19},{19,3},{4,20},{20... | collective-permute-start | bytes 2359304 | tf_op jit(solution)/shard_map/ppermute | solution.py:920
  77.9 36.3 %collective-permute-start.15 = (bf16[2,2,96,1024]{3,2,1,0:T(8,128)(2,1)}, bf16[2,2,96,1024]{3,2,1,0:T(8,128)(2,1)}, u32[]{:S(2)}, u32[]{:S(2)}) collective-permute-start(bf16[2,2,96,1024]{3,2,1,0:T(8,128)(2,1)} %get-tuple-element.154.refs_1_), channel_id=1, source_target_pairs={{0,8},{8,0},{1,9},{9,1},{2,10},{10,2},{3,11},{11,3},{4,12},{12,4},... | collective-permute-start | bytes 2359304 | tf_op jit(solution)/shard_map/ppermute | solution.py:920
  101.4 22.8 %collective-permute-start.14 = (bf16[2,4,96,768]{3,2,1,0:T(8,128)(2,1)S(1)}, bf16[2,4,96,768]{3,2,1,0:T(8,128)(2,1)S(1)}, u32[]{:S(2)}, u32[]{:S(2)}) collective-permute-start(bf16[2,4,96,768]{3,2,1,0:T(8,128)(2,1)S(1)} %give_d.1.refs_6_), channel_id=1, source_target_pairs={{0,4},{4,0},{1,5},{5,1},{2,6},{6,2},{3,7},{7,3},{8,12},{12,8},{9,1... | collective-permute-start | bytes 3538952 | tf_op jit(solution)/shard_map/ppermute | solution.py:920
  136.7 2.7 collective-permute-start.23
  137.1 9.4 %collective-permute-start.21 = (bf16[256,768]{1,0:T(8,128)(2,1)S(1)}, bf16[256,768]{1,0:T(8,128)(2,1)S(1)}, u32[]{:S(2)}, u32[]{:S(2)}) collective-permute-start(bf16[256,768]{1,0:T(8,128)(2,1)S(1)} %get-tuple-element.168), channel_id=1, source_target_pairs={{0,0},{1,4},{2,2},{3,6},{4,1},{5,5},{6,3},{7,7},{8,8},{9,12},{10,1... | collective-permute-start | bytes 1179656 | tf_op jit(solution)/shard_map/ppermute | solution.py:930
  140.5 6.6 %collective-permute-start.26 = (bf16[256,768]{1,0:T(8,128)(2,1)S(1)}, bf16[256,768]{1,0:T(8,128)(2,1)S(1)}, u32[]{:S(2)}, u32[]{:S(2)}) collective-permute-start(bf16[256,768]{1,0:T(8,128)(2,1)S(1)} %get-tuple-element.183.refs_1_.refs_4_), channel_id=1, source_target_pairs={{0,4},{4,0},{1,5},{5,1},{2,6},{6,2},{3,7},{7,3},{8,12},{12,8},{9,1... | collective-permute-start | bytes 1179656 | tf_op jit(solution)/shard_map/ppermute | solution.py:920
  140.6 27.3 %collective-permute-start.25 = (bf16[384,1536]{1,0:T(8,128)(2,1)S(1)}, bf16[384,1536]{1,0:T(8,128)(2,1)S(1)}, u32[]{:S(2)}, u32[]{:S(2)}) collective-permute-start(bf16[384,1536]{1,0:T(8,128)(2,1)S(1)} %get-tuple-element.179), channel_id=1, source_target_pairs={{0,16},{16,0},{1,17},{17,1},{2,18},{18,2},{3,19},{19,3},{4,20},{20... | collective-permute-start | bytes 3538952 | tf_op jit(solution)/shard_map/ppermute | solution.py:920
  142.4 5.8 %collective-permute-start.27 = (f32[8,768]{1,0:T(8,128)S(1)}, f32[8,768]{1,0:T(8,128)S(1)}, u32[]{:S(2)}, u32[]{:S(2)}) collective-permute-start(f32[8,768]{1,0:T(8,128)S(1)} %small.1.refs_2_.refs_7_), channel_id=1, source_target_pairs={{0,4},{4,0},{1,5},{5,1},{2,6},{6,2},{3,7},{7,3},{8,12},{12,8},{9,1... | collective-permute-start | bytes 73736 | tf_op jit(solution)/shard_map/ppermute | solution.py:920
  150.8 52.0 %collective-permute-start.32 = (bf16[400,2048]{1,0:T(8,128)(2,1)S(1)}, bf16[400,2048]{1,0:T(8,128)(2,1)S(1)}, u32[]{:S(2)}, u32[]{:S(2)}) collective-permute-start(bf16[400,2048]{1,0:T(8,128)(2,1)S(1)} %get-tuple-element.202), channel_id=1, source_target_pairs={{0,16},{16,0},{1,17},{17,1},{2,18},{18,2},{3,19},{19,3},{4,20},{20... | collective-permute-start | bytes 4915208 | tf_op jit(solution)/shard_map/ppermute | solution.py:920
  157.3 3.7 %collective-permute-start.28 = (bf16[512,768]{1,0:T(8,128)(2,1)S(1)}, bf16[512,768]{1,0:T(8,128)(2,1)S(1)}, u32[]{:S(2)}, u32[]{:S(2)}) collective-permute-start(bf16[512,768]{1,0:T(8,128)(2,1)S(1)} %get-tuple-element.191), channel_id=1, source_target_pairs={{0,4},{4,0},{1,5},{5,1},{2,6},{6,2},{3,7},{7,3},{8,12},{12,8},{9,1... | collective-permute-start | bytes 2359304 | tf_op jit(solution)/shard_map/ppermute | solution.py:920
  157.4 22.6 %collective-permute-start.24 = (bf16[256,768]{1,0:T(8,128)(2,1)S(1)}, bf16[256,768]{1,0:T(8,128)(2,1)S(1)}, u32[]{:S(2)}, u32[]{:S(2)}) collective-permute-start(bf16[256,768]{1,0:T(8,128)(2,1)S(1)} %keep.2.refs_4_.refs_1_), channel_id=1, source_target_pairs={{0,2},{2,0},{1,3},{3,1},{4,6},{6,4},{5,7},{7,5},{8,10},{10,8},{9,1... | collective-permute-start | bytes 1179656 | tf_op jit(solution)/shard_map/ppermute | solution.py:920
  168.7 28.9 %collective-permute-start.33 = (bf16[192,1536]{1,0:T(8,128)(2,1)S(1)}, bf16[192,1536]{1,0:T(8,128)(2,1)S(1)}, u32[]{:S(2)}, u32[]{:S(2)}) collective-permute-start(bf16[192,1536]{1,0:T(8,128)(2,1)S(1)} %get-tuple-element.203), channel_id=1, source_target_pairs={{0,8},{8,0},{1,9},{9,1},{2,10},{10,2},{3,11},{11,3},{4,12},{12,4},... | collective-permute-start | bytes 1769480 | tf_op jit(solution)/shard_map/ppermute | solution.py:920
  180.0 29.9 %collective-permute-start.31 = (bf16[512,768]{1,0:T(8,128)(2,1)S(1)}, bf16[512,768]{1,0:T(8,128)(2,1)S(1)}, u32[]{:S(2)}, u32[]{:S(2)}) collective-permute-start(bf16[512,768]{1,0:T(8,128)(2,1)S(1)} %add.1.refs_11_), channel_id=1, source_target_pairs={{0,8},{8,0},{1,9},{9,1},{2,10},{10,2},{3,11},{11,3},{4,12},{12,4},... | collective-permute-start | bytes 2359304 | tf_op jit(solution)/shard_map/ppermute | solution.py:920
  192.9 17.0 %collective-permute-start.30 = (bf16[512,768]{1,0:T(8,128)(2,1)S(1)}, bf16[512,768]{1,0:T(8,128)(2,1)S(1)}, u32[]{:S(2)}, u32[]{:S(2)}) collective-permute-start(bf16[512,768]{1,0:T(8,128)(2,1)S(1)} %get-tuple-element.201), channel_id=1, source_target_pairs={{0,4},{4,0},{1,5},{5,1},{2,6},{6,2},{3,7},{7,3},{8,12},{12,8},{9,1... | collective-permute-start | bytes 2359304 | tf_op jit(solution)/shard_map/ppermute | solution.py:920
  192.9 19.0 %collective-permute-start.29 = (bf16[2,256,768]{2,1,0:T(8,128)(2,1)S(1)}, bf16[2,256,768]{2,1,0:T(8,128)(2,1)S(1)}, u32[]{:S(2)}, u32[]{:S(2)}) collective-permute-start(bf16[2,256,768]{2,1,0:T(8,128)(2,1)S(1)} %pair.1.refs_14_.refs_1_), channel_id=1, source_target_pairs={{0,1},{1,0},{2,3},{3,2},{4,5},{5,4},{6,7},{7,6},{8,9},{9,8},{10,11... | collective-permute-start | bytes 2359304 | tf_op jit(solution)/shard_map/ppermute | solution.py:920
  203.8 25.4 %collective-permute-start.41 = (bf16[208,2048]{1,0:T(8,128)(2,1)S(1)}, bf16[208,2048]{1,0:T(8,128)(2,1)S(1)}, u32[]{:S(2)}, u32[]{:S(2)}) collective-permute-start(bf16[208,2048]{1,0:T(8,128)(2,1)S(1)} %get-tuple-element.220), channel_id=1, source_target_pairs={{0,8},{8,0},{1,9},{9,1},{2,10},{10,2},{3,11},{11,3},{4,12},{12,4},... | collective-permute-start | bytes 2555912 | tf_op jit(solution)/shard_map/ppermute | solution.py:920
  205.1 12.9 %collective-permute-start.35 = (bf16[2,96,768]{2,1,0:T(8,128)(2,1)S(1)}, bf16[2,96,768]{2,1,0:T(8,128)(2,1)S(1)}, u32[]{:S(2)}, u32[]{:S(2)}) collective-permute-start(bf16[2,96,768]{2,1,0:T(8,128)(2,1)S(1)} %get-tuple-element.215), channel_id=1, source_target_pairs={{0,1},{1,0},{2,3},{3,2},{4,5},{5,4},{6,7},{7,6},{8,9},{9,8},{10,11... | collective-permute-start | bytes 884744 | tf_op jit(solution)/shard_map/ppermute | solution.py:920
  210.7 15.8 %collective-permute-start.34 = (bf16[256,768]{1,0:T(8,128)(2,1)S(1)}, bf16[256,768]{1,0:T(8,128)(2,1)S(1)}, u32[]{:S(2)}, u32[]{:S(2)}) collective-permute-start(bf16[256,768]{1,0:T(8,128)(2,1)S(1)} %get-tuple-element.213.refs_3_), channel_id=1, source_target_pairs={{0,1},{1,0},{2,3},{3,2},{4,5},{5,4},{6,7},{7,6},{8,9},{9,8},{10,11... | collective-permute-start | bytes 1179656 | tf_op jit(solution)/shard_map/ppermute | solution.py:920
  210.8 28.7 %collective-permute-start.38 = (bf16[208,1280]{1,0:T(8,128)(2,1)S(1)}, bf16[208,1280]{1,0:T(8,128)(2,1)S(1)}, u32[]{:S(2)}, u32[]{:S(2)}) collective-permute-start(bf16[208,1280]{1,0:T(8,128)(2,1)S(1)} %get-tuple-element.217), channel_id=1, source_target_pairs={{0,8},{8,0},{1,9},{9,1},{2,10},{10,2},{3,11},{11,3},{4,12},{12,4},... | collective-permute-start | bytes 1597448 | tf_op jit(solution)/shard_map/ppermute | solution.py:920
  212.0 27.5 %collective-permute-start.39 = (bf16[208,1280]{1,0:T(8,128)(2,1)S(1)}, bf16[208,1280]{1,0:T(8,128)(2,1)S(1)}, u32[]{:S(2)}, u32[]{:S(2)}) collective-permute-start(bf16[208,1280]{1,0:T(8,128)(2,1)S(1)} %get-tuple-element.218), channel_id=1, source_target_pairs={{0,16},{16,0},{1,17},{17,1},{2,18},{18,2},{3,19},{19,3},{4,20},{20... | collective-permute-start | bytes 1597448 | tf_op jit(solution)/shard_map/ppermute | solution.py:920
  218.0 31.8 %collective-permute-start.40 = (bf16[208,1280]{1,0:T(8,128)(2,1)S(1)}, bf16[208,1280]{1,0:T(8,128)(2,1)S(1)}, u32[]{:S(2)}, u32[]{:S(2)}) collective-permute-start(bf16[208,1280]{1,0:T(8,128)(2,1)S(1)} %get-tuple-element.219), channel_id=1, source_target_pairs={{0,24},{8,16},{16,8},{24,0},{1,25},{9,17},{17,9},{25,1},{2,26},{10... | collective-permute-start | bytes 1597448 | tf_op jit(solution)/shard_map/ppermute | solution.py:978
  227.1 23.9 %collective-permute-start.37 = (bf16[256,768]{1,0:T(8,128)(2,1)S(1)}, bf16[256,768]{1,0:T(8,128)(2,1)S(1)}, u32[]{:S(2)}, u32[]{:S(2)}) collective-permute-start(bf16[256,768]{1,0:T(8,128)(2,1)S(1)} %final.1.refs_3_.refs_1_), channel_id=1, source_target_pairs={{0,2},{2,0},{1,3},{3,1},{4,6},{6,4},{5,7},{7,5},{8,10},{10,8},{9,1... | collective-permute-start | bytes 1179656 | tf_op jit(solution)/shard_map/ppermute | solution.py:920
  230.2 22.8 %collective-permute-start.44 = (bf16[2,112,1024]{2,1,0:T(8,128)(2,1)S(1)}, bf16[2,112,1024]{2,1,0:T(8,128)(2,1)S(1)}, u32[]{:S(2)}, u32[]{:S(2)}) collective-permute-start(bf16[2,112,1024]{2,1,0:T(8,128)(2,1)S(1)} %get-tuple-element.224), channel_id=1, source_target_pairs={{0,1},{1,0},{2,3},{3,2},{4,5},{5,4},{6,7},{7,6},{8,9},{9,8},{10,11... | collective-permute-start | bytes 1376264 | tf_op jit(solution)/shard_map/ppermute | solution.py:920
  239.5 40.7 %collective-permute-start.36 = (bf16[256,768]{1,0:T(8,128)(2,1)S(1)}, bf16[256,768]{1,0:T(8,128)(2,1)S(1)}, u32[]{:S(2)}, u32[]{:S(2)}) collective-permute-start(bf16[256,768]{1,0:T(8,128)(2,1)S(1)} %final.1.refs_3_.refs_1_), channel_id=1, source_target_pairs={{0,1},{1,0},{2,3},{3,2},{4,5},{5,4},{6,7},{7,6},{8,9},{9,8},{10,11... | collective-permute-start | bytes 1179656 | tf_op jit(solution)/shard_map/ppermute | solution.py:920
  251.5 28.8 %collective-permute-start.42 = (bf16[256,768]{1,0:T(8,128)(2,1)S(1)}, bf16[256,768]{1,0:T(8,128)(2,1)S(1)}, u32[]{:S(2)}, u32[]{:S(2)}) collective-permute-start(bf16[256,768]{1,0:T(8,128)(2,1)S(1)} %keep.3.refs_3_), channel_id=1, source_target_pairs={{0,1},{1,0},{2,3},{3,2},{4,5},{5,4},{6,7},{7,6},{8,9},{9,8},{10,11... | collective-permute-start | bytes 1179656 | tf_op jit(solution)/shard_map/ppermute | solution.py:920
  252.2 23.7 %collective-permute-start.43 = (bf16[2,112,640]{2,1,0:T(8,128)(2,1)S(1)}, bf16[2,112,640]{2,1,0:T(8,128)(2,1)S(1)}, u32[]{:S(2)}, u32[]{:S(2)}) collective-permute-start(bf16[2,112,640]{2,1,0:T(8,128)(2,1)S(1)} %get-tuple-element.223), channel_id=1, source_target_pairs={{0,1},{1,0},{2,3},{3,2},{4,5},{5,4},{6,7},{7,6},{8,9},{9,8},{10,11... | collective-permute-start | bytes 860168 | tf_op jit(solution)/shard_map/ppermute | solution.py:920
  253.0 19.6 %collective-permute-start.48 = (bf16[96,768]{1,0:T(8,128)(2,1)S(1)}, bf16[96,768]{1,0:T(8,128)(2,1)S(1)}, u32[]{:S(2)}, u32[]{:S(2)}) collective-permute-start(bf16[96,768]{1,0:T(8,128)(2,1)S(1)} %get-tuple-element.228), channel_id=1, source_target_pairs={{0,4},{1,5},{2,0},{3,1},{4,6},{5,7},{6,2},{7,3},{8,12},{9,13},{10,... | collective-permute-start | bytes 442376 | tf_op jit(solution)/shard_map/ppermute | solution.py:930
  253.8 32.8 %collective-permute-start.50 = (bf16[112,1024]{1,0:T(8,128)(2,1)S(1)}, bf16[112,1024]{1,0:T(8,128)(2,1)S(1)}, u32[]{:S(2)}, u32[]{:S(2)}) collective-permute-start(bf16[112,1024]{1,0:T(8,128)(2,1)S(1)} %get-tuple-element.229), channel_id=1, source_target_pairs={{0,4},{1,5},{2,0},{3,1},{4,6},{5,7},{6,2},{7,3},{8,12},{9,13},{10,... | collective-permute-start | bytes 688136 | tf_op jit(solution)/shard_map/ppermute | solution.py:930
  272.6 14.0 %collective-permute-start.49 = (bf16[112,1024]{1,0:T(8,128)(2,1)S(1)}, bf16[112,1024]{1,0:T(8,128)(2,1)S(1)}, u32[]{:S(2)}, u32[]{:S(2)}) collective-permute-start(bf16[112,1024]{1,0:T(8,128)(2,1)S(1)} %get-tuple-element.225.refs_3_), channel_id=1, source_target_pairs={{0,0},{1,1},{2,4},{3,5},{4,2},{5,3},{6,6},{7,7},{8,8},{9,9},{10,12... | collective-permute-start | bytes 688136 | tf_op jit(solution)/shard_map/ppermute | solution.py:930
  275.9 10.7 %collective-permute-start.47 = (bf16[96,768]{1,0:T(8,128)(2,1)S(1)}, bf16[96,768]{1,0:T(8,128)(2,1)S(1)}, u32[]{:S(2)}, u32[]{:S(2)}) collective-permute-start(bf16[96,768]{1,0:T(8,128)(2,1)S(1)} %get-tuple-element.216.refs_3_), channel_id=1, source_target_pairs={{0,0},{1,1},{2,4},{3,5},{4,2},{5,3},{6,6},{7,7},{8,8},{9,9},{10,12... | collective-permute-start | bytes 442376 | tf_op jit(solution)/shard_map/ppermute | solution.py:930
  280.2 9.4 %collective-permute-start.46 = (bf16[112,640]{1,0:T(8,128)(2,1)S(1)}, bf16[112,640]{1,0:T(8,128)(2,1)S(1)}, u32[]{:S(2)}, u32[]{:S(2)}) collective-permute-start(bf16[112,640]{1,0:T(8,128)(2,1)S(1)} %get-tuple-element.227), channel_id=1, source_target_pairs={{0,4},{1,5},{2,0},{3,1},{4,6},{5,7},{6,2},{7,3},{8,12},{9,13},{10,... | collective-permute-start | bytes 430088 | tf_op jit(solution)/shard_map/ppermute | solution.py:930
  280.3 10.9 %collective-permute-start.45 = (bf16[112,640]{1,0:T(8,128)(2,1)S(1)}, bf16[112,640]{1,0:T(8,128)(2,1)S(1)}, u32[]{:S(2)}, u32[]{:S(2)}) collective-permute-start(bf16[112,640]{1,0:T(8,128)(2,1)S(1)} %get-tuple-element.226.refs_5_), channel_id=1, source_target_pairs={{0,0},{1,1},{2,4},{3,5},{4,2},{5,3},{6,6},{7,7},{8,8},{9,9},{10,12... | collective-permute-start | bytes 430088 | tf_op jit(solution)/shard_map/ppermute | solution.py:930
  (41 other events, 194.9 us)
Sparse Core Ops, SparseCore 0:
  46.7 52.3 all-gather.2

commit v3 on v2

--- a/solution.py
+++ b/solution.py
@@ -62,8 +62,8 @@
         for head in range(3):
             group, upper = Q_AT[head]
             qm[part * 3 + head] = half_mask(q_ref[:, lanes(part * 2 + group)], upper)
-    for tile in range(rows // TILE):
-        across = slice(tile * TILE, (tile + 1) * TILE)
+    def one_tile(tile, carry):
+        across = pl.ds(pl.multiple_of(tile * TILE, TILE), TILE)
         top[...] = jnp.full_like(top, MASKED)
         total[...] = jnp.zeros_like(total)
         acc[...] = jnp.zeros_like(acc)
@@ -118,53 +118,56 @@
             second = jnp.concatenate([mixed[1], mixed[2]], axis=0)
             o_ref[across, lanes(part * 2)] = first.T.astype(LOW)
             o_ref[across, lanes(part * 2 + 1)] = second.T.astype(LOW)
-
-
-def backward_kernel(
-    stage, active, spot, q_ref, kv_ref, docs_q, docs_k, o_ref, go_ref, lse_ref, wkv_ref, *refs
-):
+        return carry
+
+    lax.fori_loop(0, rows // TILE, one_tile, 0)
+
+
+def backward_kernel(stage, active, spot, kv_ref, docs_q, docs_k, lse_ref, wkv_ref, *refs):
     if stage == 0:
-        dq_out, dkv_ref, near_ref, far_ref, sum_ref = refs[:5]
+        q_ref, o_ref, go_ref, dq_out, dkv_ref, near_ref, far_ref, sum_ref, qm, gm, along = refs[:11]
     elif stage == 1:
-        dq_in, dq_out, dkv_ref, near_ref, sum_ref = refs[:5]
+        qm, gm, along, dq_in, dq_out, dkv_ref, near_ref, sum_ref = refs[:8]
     else:
-        dq_in, wq_ref, extra_ref, block_a, dq_ref, dkv_ref, near_ref, far_ref, sum_ref, sum_q = (
-            refs[:10]
-        )
-    qm, gm, along, dq_acc, dkv_acc, grads_acc = refs[-6:]
+        qm, gm, along, dq_in, wq_ref, extra_ref, block_a = refs[:7]
+        dq_ref, dkv_ref, near_ref, far_ref, sum_ref, sum_q = refs[7:13]
+    dq_acc, dkv_acc, grads_acc = refs[-3:]
     sum_ref[...] = jnp.zeros_like(sum_ref)
-    rows = q_ref.shape[0]
+    rows = qm.shape[1]
     chunks = dkv_ref.shape[0] // TILE
     first_tile = (4, 0, 2)[stage]
-    for part in range(2):
-        for head in range(3):
-            at = part * 3 + head
-            group, upper = Q_AT[head]
-            qm[at] = half_mask(q_ref[:, lanes(part * 2 + group)], upper)
-            group, upper = O_AT[head]
-            gm[at] = half_mask(go_ref[:, lanes(part * 2 + group)], upper)
-        for tile in range(rows // TILE):
-            across = slice(tile * TILE, (tile + 1) * TILE)
-            for group in range(2):
-                both = (
-                    go_ref[across, lanes(part * 2 + group)].astype(WIDE)
-                    * o_ref[across, lanes(part * 2 + group)].astype(WIDE)
-                ).T
-                for head in range(3):
-                    if O_AT[head][0] == group:
-                        upper = O_AT[head][1]
-                        at = part * 3 + head
-                        along[at : at + 1, across] = jnp.sum(
-                            both[upper * DH : upper * DH + DH, :], axis=0, keepdims=True
-                        )
+    if stage == 0:
+        along[...] = jnp.zeros_like(along)
+        for part in range(2):
+            for head in range(3):
+                at = part * 3 + head
+                group, upper = Q_AT[head]
+                qm[at] = half_mask(q_ref[:, lanes(part * 2 + group)], upper)
+                group, upper = O_AT[head]
+                gm[at] = half_mask(go_ref[:, lanes(part * 2 + group)], upper)
+            for tile in range(rows // TILE):
+                across = slice(tile * TILE, (tile + 1) * TILE)
+                for group in range(2):
+                    both = (
+                        go_ref[across, lanes(part * 2 + group)].astype(WIDE)
+                        * o_ref[across, lanes(part * 2 + group)].astype(WIDE)
+                    ).T
+                    for head in range(3):
+                        if O_AT[head][0] == group:
+                            upper = O_AT[head][1]
+                            at = part * 3 + head
+                            along[at : at + 1, across] = jnp.sum(
+                                both[upper * DH : upper * DH + DH, :], axis=0, keepdims=True
+                            )
     dq_acc[...] = dq_in[...] if stage else jnp.zeros_like(dq_acc)
 
     def chunk(c, carry):
         here = down = pl.ds(pl.multiple_of(c * TILE, TILE), TILE)
         number = first_tile + c
         dkv_acc[...] = jnp.zeros_like(dkv_acc)
-        for tile in range(rows // TILE):
-            across = slice(tile * TILE, (tile + 1) * TILE)
+
+        def one_tile(tile, inner):
+            across = pl.ds(pl.multiple_of(tile * TILE, TILE), TILE)
 
             @pl.when(active[tile, number] == 1)
             def _():
@@ -187,6 +190,9 @@
                         keys = turned[group][upper * DH : upper * DH + DH, :]
                         dq_acc[at * DH : at * DH + DH, across] += nn(keys, slope)
 
+            return inner
+
+        lax.fori_loop(0, rows // TILE, one_tile, 0)
         dkv = dkv_acc[...].astype(LOW)
         dkv_ref[here, :] = dkv
         grads_acc[here, :] = nt(dkv, wkv_ref[...])
@@ -313,35 +319,31 @@
     )
 
 
-def attention_backward(call, stage, flags, arrays, more):
-    q, kv, wkv = arrays[0], arrays[1], arrays[-1]
-    rows, keys, width = q.shape[0], kv.shape[0], wkv.shape[0]
+def attention_backward(call, stage, flags, kv, docs_row, docs_k, lse, wkv, more):
+    rows, keys, width = docs_row.shape[1], kv.shape[0], wkv.shape[0]
     part, part_low = ((rows, width), WIDE), ((rows, width), LOW)
     dq_out = ((rows, 512), LOW) if stage == 2 else ((6 * DH, rows), WIDE)
     outs = [dq_out, ((keys, 768), LOW), part]
     outs += [] if stage == 1 else [part_low]
     outs += [((8, 768), WIDE)]
-    outs += [((8, 512), WIDE)] if stage == 2 else []
+    if stage == 0:
+        outs += [((6, rows, 128), LOW), ((6, rows, 128), LOW), ((8, rows), WIDE)]
+    if stage == 2:
+        outs += [((8, 512), WIDE)]
+    far = ((True, True, False), (False,) * 4, (False,) * 4 + (True, False, False))[stage]
 
     def kernel(flags, *refs):
         backward_kernel(stage, Active(flags), flags[0], *refs)
 
     return call(
-        kernel, ("attend_cd", "attend_a", "attend_b")[stage], flags, list(arrays) + list(more),
-        outs,
+        kernel, ("attend_cd", "attend_a", "attend_b")[stage], flags,
+        [kv, docs_row, docs_k, lse, wkv] + list(more), outs,
         [
-            VMEM((6, rows, 128), LOW),
-            VMEM((6, rows, 128), LOW),
-            VMEM((8, rows), WIDE),
             VMEM((6 * DH, rows), WIDE),
             VMEM((TILE, 768), WIDE),
             VMEM((keys, width), WIDE),
-        ], 18,
-        far=(
-            (True, True, False, True, False, False, False, True)
-            + tuple(i == 1 for i in range(len(more))),
-            False,
-        ),
+        ], 16,
+        far=((True, False, True, False, True) + far, False),
     )
 
 
@@ -355,7 +357,7 @@
     def __getitem__(self, where):
         tile, number = where
         k, l, x = self.spot[0], self.spot[1], self.spot[3]
-        first, last = self.ends(((2 * x + l) * 2 + (k if tile == 0 else 1 - k)) * TILE)
+        first, last = self.ends(((2 * x + l) * 2 + (k + tile - 2 * k * tile)) * TILE)
         block = number // 2
         far, side = block // 2, block % 2
         own = 2 * (x + far - 2 * x * far) + (k + side - 2 * k * side)
@@ -497,18 +499,27 @@
             u_bias[:, base : base + size] = part[:, :size]
 
 
+def rows_kernel(spot, mine, got, mine_uo):
+    h, l = spot[2], spot[1]
+    for a in range(2):
+        mine_uo[h ^ a, l] = mine[a]
+        mine_uo[h ^ a, 1 - l] = got[a]
+
+
+def line_kernel(spot, pair_d, got_d, rows_d):
+    for i, ref in enumerate((pair_d, got_d)):
+        for j in range(2):
+            rows_d[i + 2 * j] = ref[j]
+
+
 def join_kernel(where, *refs):
-    parts, (mine, got), (wkv, wq, mine_uo) = refs[:4], refs[4:6], refs[6:9]
+    parts, (wkv, wq) = refs[:4], refs[4:6]
     for i, part in enumerate(parts):
         for row in range(2):
             for ql in range(2):
                 at_kv, at_q = slice(ql * 384, ql * 384 + 384), slice(ql * 256, ql * 256 + 256)
                 wkv[group_of(where, i), row, :, at_kv] = part[row, ql, :, 0:384]
                 wq[group_of(where, i), row, :, at_q] = part[row, ql, :, 384:640]
-    h, l = where[2], where[1]
-    for a in range(2):
-        mine_uo[h ^ a, l] = mine[a]
-        mine_uo[h ^ a, 1 - l] = got[a]
 
 
 def project_kernel(_, wkv, wq, a, b, c, d, own, peer, kv_bias, q_bias, kv, q, *far):
@@ -1042,15 +1053,16 @@
     got_uo = flip(pair_uo, "tl")
     block_d = flip(kept_c, "cc")
     plane_a = around(mine_a)
-    wkv, wq, mine_uo = call(
-        join_kernel, "join", spot, plane_a + [pair_uo, got_uo],
-        [
-            ((4, 2, eighth, 768), LOW), ((4, 2, eighth, 512), LOW),
-            ((2, 2, shard, uo_width), LOW),
-        ], far=(False, (True, True, False)),
+    mine_uo = call(
+        rows_kernel, "rows", spot, [pair_uo, got_uo], [((2, 2, shard, uo_width), LOW)],
+        after=tuple(plane_a[1:4]),
+    )[0]
+    plane_uo = around(mine_uo)
+    wkv, wq = call(
+        join_kernel, "join", spot, plane_a,
+        [((4, 2, eighth, 768), LOW), ((4, 2, eighth, 512), LOW)], far=(False, True),
     )
     wkv, wq = wkv.reshape(width, 768), wq.reshape(width, 512)
-    plane_uo = around(mine_uo)
     kv, q, kv_a, kv_b, kv_cd, q_far = call(
         project_kernel, "project", spot,
         [wkv, wq, block_a, got_ab, kept_c, block_d, tokens_own, tokens_peer, kv_bias, q_bias],
@@ -1136,13 +1148,13 @@
 
     if square:
         got_d, got_uo = flip(sent_d, "fsdp"), flip(sent_uo, "fsdp")
-    dq_part, dkv_cd, part_c, part_d, sum_cd = attention_backward(
-        call, 0, flags, [q_far, kv_cd, docs_row, docs_cd, o, go, lse, wkv], []
+    dq_part, dkv_cd, part_c, part_d, sum_cd, *masks = attention_backward(
+        call, 0, flags, kv_cd, docs_row, docs_cd, lse, wkv, [q_far, o, go]
     )
     sum_c = call(add_kernel, "add", spot, [part_c, core(part_d)], [((rows, width), LOW)])[0]
     got_c = flip(sum_c, "cx")
     dq_part, dkv_a, part_a, sum_a = attention_backward(
-        call, 1, flags, [q_far, kv_a, docs_row, docs_a, o, go, lse, wkv], [dq_part]
+        call, 1, flags, kv_a, docs_row, docs_a, lse, wkv, masks + [dq_part]
     )
     if square:
         left_d, next_d = call(
@@ -1152,8 +1164,8 @@
     out_pair = call(pair_kernel, "pair", spot, [out_own, out_far], [((2, half, width), LOW)])[0]
     out_got = flip(out_pair, "tl")
     dq, dkv_b, part_a, part_b, sum_b, sum_q = attention_backward(
-        call, 2, flags, [q_far, kv_b, docs_row, docs_b, o, go, lse, wkv],
-        [dq_part, wq, grad_one, part_a],
+        call, 2, flags, kv_b, docs_row, docs_b, lse, wkv,
+        masks + [dq_part, wq, grad_one, part_a],
     )
     parts_a = call(
         grad_qkv_kernel, "grad_qkv", spot,

time: 307 us -> 298 us (0.971); the launches traced: 301 us -> 295 us
  waiting for transfers between devices: 110 us -> 98.3 us
  starting transfers between devices: 67.9 us -> 75.6 us
    ppermute x37, waiting for transfers between devices: 63.7 us -> 54 us  [flip(): return lax.ppermute(value, axis, FLIP)]
    ppermute x3, starting transfers between devices: 2.43 us -> 7.08 us  [exchange(): lax.ppermute(far, plane, [(i, i ^ 3) for i in range(4)])]
    unnamed x74 -> x80, local copies, waits for them, and re-layouts: 16.8 us -> 15.1 us
    pallas_call x42 -> x43, Pallas kernels: 90 us -> 90.9 us  [__call__(): pl.pallas_call(run, out_shape=tuple((pltpu.HBM(shape, kind) if out else j...]
  transfers between devices with their start and end apart: 52 -> 52, of which waited for: 21 -> 21; matrix products, arithmetic and copies ran while one was open for 0% -> 0% of each run, Pallas kernels for 25% -> 26%
where the time goes in v3:
time: 298 us; the launch traced here: 295 us
  waiting for transfers between devices  98.3 us (33%)
  Pallas kernels  90.9 us (31%)
  starting transfers between devices  75.6 us (25%)
  local copies, waits for them, and re-layouts  15.1 us (5%)
  between operations  14.9 us (5%)
    pallas_call x43, Pallas kernels, __call__(): pl.pallas_call(run, out_shape=tuple((pltpu.HBM(shape, kind) if out else j...  90.9 us
    ppermute x37, waiting for transfers between devices, flip(): return lax.ppermute(value, axis, FLIP)  54 us
    ppermute x37, starting transfers between devices, flip(): return lax.ppermute(value, axis, FLIP)  43.5 us
    ppermute x11, waiting for transfers between devices, move(): return lax.ppermute(value, ('cc', 'th', 'tl'), pairs)  27 us
    ppermute x11, starting transfers between devices, move(): return lax.ppermute(value, ('cc', 'th', 'tl'), pairs)  24.9 us
    unnamed x80, local copies, waits for them, and re-layouts  15.1 us
    ppermute x3, waiting for transfers between devices, exchange(): lax.ppermute(far, plane, [(i, i ^ 3) for i in range(4)])  9.97 us
    all_gather x1, waiting for transfers between devices, body(): all_d = lax.all_gather(rows_d, ('th', 'tl'), axis=0)  7.32 us
  transfers between devices with their start and end apart: 52, of which 21 were waited for; matrix products, arithmetic and copies ran while one was open for 0% of the time, Pallas kernels for 26%

profile of v3, /device:TPU:1, one launch (start us, length us, event | category | flops | bytes accessed | tf_op | source)
XLA Modules:
  0.0 294.8 jit_solution(15470819444361396562)
XLA Ops:
  9.4 1.8 pack.1
  11.3 2.0 pick.1
  13.4 2.7 collective-permute-start.5
  17.9 4.1 %collective-permute-start.1 = (bf16[112,640]{1,0:T(8,128)(2,1)S(1)}, bf16[112,640]{1,0:T(8,128)(2,1)S(1)}, u32[]{:S(2)}, u32[]{:S(2)}) collective-permute-start(bf16[112,640]{1,0:T(8,128)(2,1)S(1)} %get-tuple-element.133.refs_3_), channel_id=1, source_target_pairs={{0,0},{1,1},{2,4},{3,5},{4,2},{5,3},{6,6},{7,7},{8,8},{9,9},{10,12... | collective-permute-start | bytes 430088 | tf_op jit(solution)/shard_map/ppermute | solution.py:941
  26.7 1.8 settle.1
  29.5 1.9 collective-permute-start.4
  32.2 5.0 %collective-permute-start.6 = (bf16[96,1024]{1,0:T(8,128)(2,1)S(1)}, bf16[96,1024]{1,0:T(8,128)(2,1)S(1)}, u32[]{:S(2)}, u32[]{:S(2)}) collective-permute-start(bf16[96,1024]{1,0:T(8,128)(2,1)S(1)} %get-tuple-element.140.refs_8_), channel_id=1, source_target_pairs={{0,0},{1,1},{2,4},{3,5},{4,2},{5,3},{6,6},{7,7},{8,8},{9,9},{10,12... | collective-permute-start | bytes 589832 | tf_op jit(solution)/shard_map/ppermute | solution.py:941
  37.2 1.8 collective-permute-done.7.refs_5_
  39.0 3.9 %collective-permute-done.6.refs_4_ = bf16[96,1024]{1,0:T(8,128)(2,1)S(1)} collective-permute-done((bf16[96,1024]{1,0:T(8,128)(2,1)S(1)}, bf16[96,1024]{1,0:T(8,128)(2,1)S(1)}, u32[]{:S(2)}, u32[]{:S(2)}) %collective-permute-start.6) | collective-permute-done | bytes 196640 | tf_op jit(solution)/shard_map/ppermute | solution.py:941
  51.9 11.9 %collective-permute-done.12.refs_2_ = bf16[2,96,1024]{2,1,0:T(8,128)(2,1)S(1)} collective-permute-done((bf16[2,96,1024]{2,1,0:T(8,128)(2,1)}, bf16[2,96,1024]{2,1,0:T(8,128)(2,1)S(1)}, u32[]{:S(2)}, u32[]{:S(2)}) %collective-permute-start.12) | collective-permute-done | bytes 393248 | tf_op jit(solution)/shard_map/ppermute | solution.py:931
  63.7 8.8 %collective-permute-done.10.refs_5_.refs_3_ = bf16[2,2,96,640]{3,2,1,0:T(8,128)(2,1)S(1)} collective-permute-done((bf16[2,2,96,640]{3,2,1,0:T(8,128)(2,1)}, bf16[2,2,96,640]{3,2,1,0:T(8,128)(2,1)S(1)}, u32[]{:S(2)}, u32[]{:S(2)}) %collective-permute-start.10) | collective-permute-done | bytes 491552 | tf_op jit(solution)/shard_map/ppermute | solution.py:931
  76.9 2.0 join.1
  78.9 7.1 %project.1 = (bf16[2048,768]{1,0:T(8,128)(2,1)S(1)}, bf16[512,512]{1,0:T(8,128)(2,1)S(1)}, bf16[512,768]{1,0:T(8,128)(2,1)}, bf16[512,768]{1,0:T(8,128)(2,1)}, b...) custom-call(s32[6]{0:T(128)S(1)} %stack.24.refs_0_, bf16[768,768]{1,0:T(8,128)(2,1)} %bitcast.23, ...), custom_call_target="tpu_custom_call" | custom-call | flops 1 | bytes 1 | tf_op jit(solution)/shard_map/project/pallas_call | solution.py:288
  86.1 6.6 %attend.1 = (bf16[512,512]{1,0:T(8,128)(2,1)S(1)}, f32[8,512]{1,0:T(8,128)S(1)}) custom-call(s32[6]{0:T(128)S(1)} %stack.24.refs_0_, s32[2,2048]{1,0:T(2,128)S(1)} %copy-done.18, bf16[512,512]{1,0:T(8,128)(2,1)S(1)} %get-tuple-element.152.refs_2_.refs_6_, bf16[2048,768]{1,0:T(8,128)(2,1)S(1)} %get-tuple-element.153.refs_3_, ...), custom_call_target="tpu_custom_call" | custom-call | flops 1 | bytes 1 | tf_op jit(solution)/shard_map/attend/pallas_call | solution.py:288
  92.7 7.3 %all-gather.3.cloned.1.call-done = bf16[16,96,768]{2,1,0:T(8,128)(2,1)} async-done(((bf16[4,96,768]{2,1,0:T(8,128)(2,1)}), bf16[16,96,768]{2,1,0:T(8,128)(2,1)}) %all-gather.3.cloned.1.call-update) | async-done | bytes 2359312 | tf_op jit(solution)/shard_map/all_gather | solution.py:1052
  100.0 1.7 copy-done
  102.8 8.7 %collective-permute-done.16.refs_3_ = bf16[2,2,96,1024]{3,2,1,0:T(8,128)(2,1)} collective-permute-done((bf16[2,2,96,1024]{3,2,1,0:T(8,128)(2,1)S(1)}, bf16[2,2,96,1024]{3,2,1,0:T(8,128)(2,1)}, u32[]{:S(2)}, u32[]{:S(2)}) %collective-permute-start.16) | collective-permute-done | bytes 786464 | tf_op jit(solution)/shard_map/ppermute | solution.py:931
  111.5 2.5 branch.1
  118.7 2.7 up.1
  121.4 2.1 down.1
  128.5 2.1 grad_d.1
  130.6 3.3 %units.1 = (bf16[512,1536]{1,0:T(8,128)(2,1)S(1)}, f32[256,768]{1,0:T(8,128)S(1)}, bf16[256,768]{1,0:T(8,128)(2,1)S(1)}, f32[8,1536]{1,0:T(8,128)S(1)}) custom-call(s32[6]{0:T(128)S(1)} %stack.24.refs_0_, bf16[256,768]{1,0:T(8,128)(2,1)S(1)} %get-tuple-element.170.refs_1_, bf16[256,768]{1,0:T(8,128)(2,1)S(1)} %collective-permute-done.22.refs_2_, ...), custom_call_target="tpu_custom_call" | custom-call | flops 1 | bytes 1 | tf_op jit(solution)/shard_map/units/pallas_call | solution.py:288
  134.3 2.2 collective-permute-start.21
  140.3 3.4 %collective-permute-done.21.refs_1_ = bf16[256,768]{1,0:T(8,128)(2,1)S(1)} collective-permute-done((bf16[256,768]{1,0:T(8,128)(2,1)S(1)}, bf16[256,768]{1,0:T(8,128)(2,1)S(1)}, u32[]{:S(2)}, u32[]{:S(2)}) %collective-permute-start.21) | collective-permute-done | bytes 393248 | tf_op jit(solution)/shard_map/ppermute | solution.py:941
  145.4 2.6 grad_uo.1
  148.4 6.5 %attend_cd.1 = (f32[384,512]{1,0:T(8,128)S(1)}, bf16[1024,768]{1,0:T(8,128)(2,1)S(1)}, f32[512,768]{1,0:T(8,128)S(1)}, bf16[512,768]{1,0:T(8,128)(2,1)S(1)}, f32...) custom-call(s32[6]{0:T(128)S(1)} %stack.24.refs_0_, ...), custom_call_target="tpu_custom_call" | custom-call | flops 1 | bytes 1 | tf_op jit(solution)/shard_map/attend_cd/pallas_call | solution.py:288
  155.4 1.8 collective-permute-done.28.refs_2_
  157.9 5.4 %attend_a.1 = (f32[384,512]{1,0:T(8,128)S(1)}, bf16[512,768]{1,0:T(8,128)(2,1)S(1)}, f32[512,768]{1,0:T(8,128)S(1)}, f32[8,768]{1,0:T(8,128)S(1)}) custom-call(s32[6]{0:T(128)S(1)} %stack.24.refs_0_, s32[2,2048]{1,0:T(2,128)S(1)} %copy-done.19, bf16[512,768]{1,0:T(8,128)(2,1)} %get-tuple-element.181.refs_2_, ...), custom_call_target="tpu_custom_call" | custom-call | flops 1 | bytes 1 | tf_op jit(solution)/shard_map/attend_a/pallas_call | solution.py:288
  165.7 7.8 %collective-permute-start.33 = (bf16[192,1536]{1,0:T(8,128)(2,1)S(1)}, bf16[192,1536]{1,0:T(8,128)(2,1)S(1)}, u32[]{:S(2)}, u32[]{:S(2)}) collective-permute-start(bf16[192,1536]{1,0:T(8,128)(2,1)S(1)} %get-tuple-element.206), channel_id=1, source_target_pairs={{0,8},{8,0},{1,9},{9,1},{2,10},{10,2},{3,11},{11,3},{4,12},{12,4},... | collective-permute-start | bytes 1769480 | tf_op jit(solution)/shard_map/ppermute | solution.py:931
  174.2 11.4 %attend_b.1 = (bf16[512,512]{1,0:T(8,128)(2,1)S(1)}, bf16[512,768]{1,0:T(8,128)(2,1)S(1)}, f32[512,768]{1,0:T(8,128)S(1)}, bf16[512,768]{1,0:T(8,128)(2,1)S(1)},...) custom-call(s32[6]{0:T(128)S(1)} %stack.24.refs_0_, s32[2,2048]{1,0:T(2,128)S(1)} %copy-done.19, ...), custom_call_target="tpu_custom_call" | custom-call | flops 1 | bytes 1 | tf_op jit(solution)/shard_map/attend_b/pallas_call | solution.py:288
  185.8 5.2 %grad_qkv.1 = (bf16[208,1280]{1,0:T(8,128)(2,1)S(1)}, bf16[208,1280]{1,0:T(8,128)(2,1)S(1)}, bf16[208,1280]{1,0:T(8,128)(2,1)S(1)}, bf16[208,1280]{1,0:T(8,128)(2,1)S(1)}) custom-call(s32[6]{0:T(128)S(1)} %stack.24.refs_0_, bf16[512,768]{1,0:T(8,128)(2,1)S(1)} %get-tuple-element.134.refs_1_.refs_3_, ...), custom_call_target="tpu_custom_call" | custom-call | flops 1 | bytes 1 | tf_op jit(solution)/shard_map/grad_qkv/pallas_call | solution.py:288
  191.9 8.2 %collective-permute-done.32.refs_2_ = bf16[400,2048]{1,0:T(8,128)(2,1)S(1)} collective-permute-done((bf16[400,2048]{1,0:T(8,128)(2,1)S(1)}, bf16[400,2048]{1,0:T(8,128)(2,1)S(1)}, u32[]{:S(2)}, u32[]{:S(2)}) %collective-permute-start.32) | collective-permute-done | bytes 1638432 | tf_op jit(solution)/shard_map/ppermute | solution.py:931
  204.3 2.5 collective-permute-start.34
  207.2 4.1 %collective-permute-start.39 = (bf16[208,1280]{1,0:T(8,128)(2,1)S(1)}, bf16[208,1280]{1,0:T(8,128)(2,1)S(1)}, u32[]{:S(2)}, u32[]{:S(2)}) collective-permute-start(bf16[208,1280]{1,0:T(8,128)(2,1)S(1)} %get-tuple-element.222), channel_id=1, source_target_pairs={{0,16},{16,0},{1,17},{17,1},{2,18},{18,2},{3,19},{19,3},{4,20},{20... | collective-permute-start | bytes 1597448 | tf_op jit(solution)/shard_map/ppermute | solution.py:931
  211.4 4.7 %collective-permute-start.40 = (bf16[208,1280]{1,0:T(8,128)(2,1)S(1)}, bf16[208,1280]{1,0:T(8,128)(2,1)S(1)}, u32[]{:S(2)}, u32[]{:S(2)}) collective-permute-start(bf16[208,1280]{1,0:T(8,128)(2,1)S(1)} %get-tuple-element.223), channel_id=1, source_target_pairs={{0,24},{8,16},{16,8},{24,0},{1,25},{9,17},{17,9},{25,1},{2,26},{10... | collective-permute-start | bytes 1597448 | tf_op jit(solution)/shard_map/ppermute | solution.py:989
  216.0 1.8 output.1.refs_3_
  220.5 3.4 %collective-permute-start.37 = (bf16[256,768]{1,0:T(8,128)(2,1)S(1)}, bf16[256,768]{1,0:T(8,128)(2,1)S(1)}, u32[]{:S(2)}, u32[]{:S(2)}) collective-permute-start(bf16[256,768]{1,0:T(8,128)(2,1)S(1)} %final.1.refs_3_.refs_1_), channel_id=1, source_target_pairs={{0,2},{2,0},{1,3},{3,1},{4,6},{6,4},{5,7},{7,5},{8,10},{10,8},{9,1... | collective-permute-start | bytes 1179656 | tf_op jit(solution)/shard_map/ppermute | solution.py:931
  226.2 6.4 %collective-permute-done.38.refs_2_ = bf16[208,1280]{1,0:T(8,128)(2,1)S(1)} collective-permute-done((bf16[208,1280]{1,0:T(8,128)(2,1)S(1)}, bf16[208,1280]{1,0:T(8,128)(2,1)S(1)}, u32[]{:S(2)}, u32[]{:S(2)}) %collective-permute-start.38) | collective-permute-done | bytes 532512 | tf_op jit(solution)/shard_map/ppermute | solution.py:931
  232.7 2.0 collective-permute-start.36
  234.7 10.0 %collective-permute-done.40.refs_4_ = bf16[208,1280]{1,0:T(8,128)(2,1)S(1)} collective-permute-done((bf16[208,1280]{1,0:T(8,128)(2,1)S(1)}, bf16[208,1280]{1,0:T(8,128)(2,1)S(1)}, u32[]{:S(2)}, u32[]{:S(2)}) %collective-permute-start.40) | collective-permute-done | bytes 532512 | tf_op jit(solution)/shard_map/ppermute | solution.py:989
  246.3 2.6 collective-permute-start.42
  251.2 1.9 collective-permute-start.50
  253.1 14.2 %collective-permute-done.48.refs_2_ = bf16[96,768]{1,0:T(8,128)(2,1)S(1)} collective-permute-done((bf16[96,768]{1,0:T(8,128)(2,1)S(1)}, bf16[96,768]{1,0:T(8,128)(2,1)S(1)}, u32[]{:S(2)}, u32[]{:S(2)}) %collective-permute-start.48) | collective-permute-done | bytes 147488 | tf_op jit(solution)/shard_map/ppermute | solution.py:941
  267.3 1.9 collective-permute-start.49
  270.4 4.0 %collective-permute-start.47 = (bf16[96,768]{1,0:T(8,128)(2,1)S(1)}, bf16[96,768]{1,0:T(8,128)(2,1)S(1)}, u32[]{:S(2)}, u32[]{:S(2)}) collective-permute-start(bf16[96,768]{1,0:T(8,128)(2,1)S(1)} %get-tuple-element.220.refs_3_), channel_id=1, source_target_pairs={{0,0},{1,1},{2,4},{3,5},{4,2},{5,3},{6,6},{7,7},{8,8},{9,9},{10,12... | collective-permute-start | bytes 442376 | tf_op jit(solution)/shard_map/ppermute | solution.py:941
  275.2 2.9 collective-permute-start.45
  278.1 1.8 place.1.refs_5_
  284.3 1.6 collective-permute-done.45.refs_1_
  (181 shorter events, 68.1 us)
Async XLA Ops:
  7.2 92.8 %all-gather.3.cloned.1.call-start = ((), (), s32[]{:S(2)}) async-start(), calls=%async_computation | async-start | bytes 2949120 | tf_op jit(solution)/shard_map/all_gather | solution.py:1052
  13.2 13.5 %collective-permute-start = (bf16[768,768]{1,0:T(8,128)(2,1)S(1)}, bf16[768,768]{1,0:T(8,128)(2,1)S(1)}, u32[]{:S(2)}, u32[]{:S(2)}) collective-permute-start(bf16[768,768]{1,0:T(8,128)(2,1)S(1)} %get-tuple-element.135), channel_id=1, source_target_pairs={{0,4},{4,0},{1,5},{5,1},{2,6},{6,2},{3,7},{7,3},{8,12},{12,8},{9,1... | collective-permute-start | bytes 3538952 | tf_op jit(solution)/shard_map/ppermute | solution.py:931
  13.4 23.8 %collective-permute-start.5 = (bf16[512,768]{1,0:T(8,128)(2,1)S(1)}, bf16[512,768]{1,0:T(8,128)(2,1)S(1)}, u32[]{:S(2)}, u32[]{:S(2)}) collective-permute-start(bf16[512,768]{1,0:T(8,128)(2,1)S(1)} %get-tuple-element.134.refs_1_.refs_3_), channel_id=1, source_target_pairs={{0,8},{8,0},{1,9},{9,1},{2,10},{10,2},{3,11},{11,3},{4,12},{12,4},... | collective-permute-start | bytes 2359304 | tf_op jit(solution)/shard_map/ppermute | solution.py:931
  16.0 10.7 %collective-permute-start.3 = (bf16[96,768]{1,0:T(8,128)(2,1)S(1)}, bf16[96,768]{1,0:T(8,128)(2,1)S(1)}, u32[]{:S(2)}, u32[]{:S(2)}) collective-permute-start(bf16[96,768]{1,0:T(8,128)(2,1)S(1)} %get-tuple-element.137.refs_6_), channel_id=1, source_target_pairs={{0,16},{16,0},{1,17},{17,1},{2,18},{18,2},{3,19},{19,3},{4,20},{20... | collective-permute-start | bytes 442376 | tf_op jit(solution)/shard_map/ppermute | solution.py:931
  17.3 8.8 %collective-permute-start.2 = (bf16[112,640]{1,0:T(8,128)(2,1)S(1)}, bf16[112,640]{1,0:T(8,128)(2,1)S(1)}, u32[]{:S(2)}, u32[]{:S(2)}) collective-permute-start(bf16[112,640]{1,0:T(8,128)(2,1)S(1)} %get-tuple-element.133.refs_3_), channel_id=1, source_target_pairs={{0,2},{1,3},{2,6},{3,7},{4,0},{5,1},{6,4},{7,5},{8,10},{9,11},{10,... | collective-permute-start | bytes 430088 | tf_op jit(solution)/shard_map/ppermute | solution.py:941
  17.9 8.8 %collective-permute-start.1 = (bf16[112,640]{1,0:T(8,128)(2,1)S(1)}, bf16[112,640]{1,0:T(8,128)(2,1)S(1)}, u32[]{:S(2)}, u32[]{:S(2)}) collective-permute-start(bf16[112,640]{1,0:T(8,128)(2,1)S(1)} %get-tuple-element.133.refs_3_), channel_id=1, source_target_pairs={{0,0},{1,1},{2,4},{3,5},{4,2},{5,3},{6,6},{7,7},{8,8},{9,9},{10,12... | collective-permute-start | bytes 430088 | tf_op jit(solution)/shard_map/ppermute | solution.py:941
  29.3 13.6 %collective-permute-start.8 = (bf16[2,96,768]{2,1,0:T(8,128)(2,1)S(1)}, bf16[2,96,768]{2,1,0:T(8,128)(2,1)S(1)}, u32[]{:S(2)}, u32[]{:S(2)}) collective-permute-start(bf16[2,96,768]{2,1,0:T(8,128)(2,1)S(1)} %get-tuple-element.141.refs_6_), channel_id=1, source_target_pairs={{0,8},{8,0},{1,9},{9,1},{2,10},{10,2},{3,11},{11,3},{4,12},{12,4},... | collective-permute-start | bytes 884744 | tf_op jit(solution)/shard_map/ppermute | solution.py:931
  29.5 13.4 %collective-permute-start.4 = (bf16[2,112,640]{2,1,0:T(8,128)(2,1)S(1)}, bf16[2,112,640]{2,1,0:T(8,128)(2,1)S(1)}, u32[]{:S(2)}, u32[]{:S(2)}) collective-permute-start(bf16[2,112,640]{2,1,0:T(8,128)(2,1)S(1)} %get-tuple-element.139.refs_1_), channel_id=1, source_target_pairs={{0,1},{1,0},{2,3},{3,2},{4,5},{5,4},{6,7},{7,6},{8,9},{9,8},{10,11... | collective-permute-start | bytes 860168 | tf_op jit(solution)/shard_map/ppermute | solution.py:931
  31.4 7.6 %collective-permute-start.7 = (bf16[96,1024]{1,0:T(8,128)(2,1)S(1)}, bf16[96,1024]{1,0:T(8,128)(2,1)S(1)}, u32[]{:S(2)}, u32[]{:S(2)}) collective-permute-start(bf16[96,1024]{1,0:T(8,128)(2,1)S(1)} %get-tuple-element.140.refs_8_), channel_id=1, source_target_pairs={{0,2},{1,3},{2,6},{3,7},{4,0},{5,1},{6,4},{7,5},{8,10},{9,11},{10,... | collective-permute-start | bytes 589832 | tf_op jit(solution)/shard_map/ppermute | solution.py:941
  32.2 10.7 %collective-permute-start.6 = (bf16[96,1024]{1,0:T(8,128)(2,1)S(1)}, bf16[96,1024]{1,0:T(8,128)(2,1)S(1)}, u32[]{:S(2)}, u32[]{:S(2)}) collective-permute-start(bf16[96,1024]{1,0:T(8,128)(2,1)S(1)} %get-tuple-element.140.refs_8_), channel_id=1, source_target_pairs={{0,0},{1,1},{2,4},{3,5},{4,2},{5,3},{6,6},{7,7},{8,8},{9,9},{10,12... | collective-permute-start | bytes 589832 | tf_op jit(solution)/shard_map/ppermute | solution.py:941
  47.5 16.2 %collective-permute-start.11 = (bf16[2,2,96,640]{3,2,1,0:T(8,128)(2,1)}, bf16[2,2,96,640]{3,2,1,0:T(8,128)(2,1)S(1)}, u32[]{:S(2)}, u32[]{:S(2)}) collective-permute-start(bf16[2,2,96,640]{3,2,1,0:T(8,128)(2,1)} %copy-done.15), channel_id=1, source_target_pairs={{0,24},{8,16},{16,8},{24,0},{1,25},{9,17},{17,9},{25,1},{2,26},{10... | collective-permute-start | bytes 1474568 | tf_op jit(solution)/shard_map/ppermute | solution.py:989
  48.7 23.8 %collective-permute-start.10 = (bf16[2,2,96,640]{3,2,1,0:T(8,128)(2,1)}, bf16[2,2,96,640]{3,2,1,0:T(8,128)(2,1)S(1)}, u32[]{:S(2)}, u32[]{:S(2)}) collective-permute-start(bf16[2,2,96,640]{3,2,1,0:T(8,128)(2,1)} %copy-done.15), channel_id=1, source_target_pairs={{0,16},{16,0},{1,17},{17,1},{2,18},{18,2},{3,19},{19,3},{4,20},{20... | collective-permute-start | bytes 1474568 | tf_op jit(solution)/shard_map/ppermute | solution.py:931
  50.0 22.5 %collective-permute-start.9 = (bf16[2,2,96,640]{3,2,1,0:T(8,128)(2,1)}, bf16[2,2,96,640]{3,2,1,0:T(8,128)(2,1)S(1)}, u32[]{:S(2)}, u32[]{:S(2)}) collective-permute-start(bf16[2,2,96,640]{3,2,1,0:T(8,128)(2,1)} %copy-done.15), channel_id=1, source_target_pairs={{0,8},{8,0},{1,9},{9,1},{2,10},{10,2},{3,11},{11,3},{4,12},{12,4},... | collective-permute-start | bytes 1474568 | tf_op jit(solution)/shard_map/ppermute | solution.py:931
  50.3 13.5 %collective-permute-start.12 = (bf16[2,96,1024]{2,1,0:T(8,128)(2,1)}, bf16[2,96,1024]{2,1,0:T(8,128)(2,1)S(1)}, u32[]{:S(2)}, u32[]{:S(2)}) collective-permute-start(bf16[2,96,1024]{2,1,0:T(8,128)(2,1)} %copy-done.22), channel_id=1, source_target_pairs={{0,1},{1,0},{2,3},{3,2},{4,5},{5,4},{6,7},{7,6},{8,9},{9,8},{10,11... | collective-permute-start | bytes 1179656 | tf_op jit(solution)/shard_map/ppermute | solution.py:931
  51.9 27.0 %collective-permute-start.13 = (bf16[512,768]{1,0:T(8,128)(2,1)}, bf16[512,768]{1,0:T(8,128)(2,1)S(1)}, u32[]{:S(2)}, u32[]{:S(2)}) collective-permute-start(bf16[512,768]{1,0:T(8,128)(2,1)} %get-tuple-element.148.refs_5_.refs_3_), channel_id=1, source_target_pairs={{0,4},{4,0},{1,5},{5,1},{2,6},{6,2},{3,7},{7,3},{8,12},{12,8},{9,1... | collective-permute-start | bytes 2359304 | tf_op jit(solution)/shard_map/ppermute | solution.py:931
  74.1 28.7 %collective-permute-start.17 = (bf16[2,2,96,1024]{3,2,1,0:T(8,128)(2,1)S(1)}, bf16[2,2,96,1024]{3,2,1,0:T(8,128)(2,1)}, u32[]{:S(2)}, u32[]{:S(2)}) collective-permute-start(bf16[2,2,96,1024]{3,2,1,0:T(8,128)(2,1)S(1)} %rows.1.refs_5_.refs_1_), channel_id=1, source_target_pairs={{0,24},{8,16},{16,8},{24,0},{1,25},{9,17},{17,9},{25,1},{2,26},{10... | collective-permute-start | bytes 2359304 | tf_op jit(solution)/shard_map/ppermute | solution.py:989
  75.4 36.2 %collective-permute-start.16 = (bf16[2,2,96,1024]{3,2,1,0:T(8,128)(2,1)S(1)}, bf16[2,2,96,1024]{3,2,1,0:T(8,128)(2,1)}, u32[]{:S(2)}, u32[]{:S(2)}) collective-permute-start(bf16[2,2,96,1024]{3,2,1,0:T(8,128)(2,1)S(1)} %rows.1.refs_5_.refs_1_), channel_id=1, source_target_pairs={{0,16},{16,0},{1,17},{17,1},{2,18},{18,2},{3,19},{19,3},{4,20},{20... | collective-permute-start | bytes 2359304 | tf_op jit(solution)/shard_map/ppermute | solution.py:931
  75.5 36.0 %collective-permute-start.15 = (bf16[2,2,96,1024]{3,2,1,0:T(8,128)(2,1)S(1)}, bf16[2,2,96,1024]{3,2,1,0:T(8,128)(2,1)}, u32[]{:S(2)}, u32[]{:S(2)}) collective-permute-start(bf16[2,2,96,1024]{3,2,1,0:T(8,128)(2,1)S(1)} %rows.1.refs_5_.refs_1_), channel_id=1, source_target_pairs={{0,8},{8,0},{1,9},{9,1},{2,10},{10,2},{3,11},{11,3},{4,12},{12,4},... | collective-permute-start | bytes 2359304 | tf_op jit(solution)/shard_map/ppermute | solution.py:931
  102.3 19.1 %collective-permute-start.14 = (bf16[2,4,96,768]{3,2,1,0:T(8,128)(2,1)S(1)}, bf16[2,4,96,768]{3,2,1,0:T(8,128)(2,1)S(1)}, u32[]{:S(2)}, u32[]{:S(2)}) collective-permute-start(bf16[2,4,96,768]{3,2,1,0:T(8,128)(2,1)S(1)} %give_d.1.refs_6_), channel_id=1, source_target_pairs={{0,4},{4,0},{1,5},{5,1},{2,6},{6,2},{3,7},{7,3},{8,12},{12,8},{9,1... | collective-permute-start | bytes 3538952 | tf_op jit(solution)/shard_map/ppermute | solution.py:931
  133.9 2.7 collective-permute-start.23
  134.3 9.4 %collective-permute-start.21 = (bf16[256,768]{1,0:T(8,128)(2,1)S(1)}, bf16[256,768]{1,0:T(8,128)(2,1)S(1)}, u32[]{:S(2)}, u32[]{:S(2)}) collective-permute-start(bf16[256,768]{1,0:T(8,128)(2,1)S(1)} %get-tuple-element.169), channel_id=1, source_target_pairs={{0,0},{1,4},{2,2},{3,6},{4,1},{5,5},{6,3},{7,7},{8,8},{9,12},{10,1... | collective-permute-start | bytes 1179656 | tf_op jit(solution)/shard_map/ppermute | solution.py:941
  137.7 6.6 %collective-permute-start.26 = (bf16[256,768]{1,0:T(8,128)(2,1)S(1)}, bf16[256,768]{1,0:T(8,128)(2,1)S(1)}, u32[]{:S(2)}, u32[]{:S(2)}) collective-permute-start(bf16[256,768]{1,0:T(8,128)(2,1)S(1)} %get-tuple-element.186.refs_1_.refs_4_), channel_id=1, source_target_pairs={{0,4},{4,0},{1,5},{5,1},{2,6},{6,2},{3,7},{7,3},{8,12},{12,8},{9,1... | collective-permute-start | bytes 1179656 | tf_op jit(solution)/shard_map/ppermute | solution.py:931
  137.7 27.2 %collective-permute-start.25 = (bf16[384,1536]{1,0:T(8,128)(2,1)S(1)}, bf16[384,1536]{1,0:T(8,128)(2,1)S(1)}, u32[]{:S(2)}, u32[]{:S(2)}) collective-permute-start(bf16[384,1536]{1,0:T(8,128)(2,1)S(1)} %get-tuple-element.180), channel_id=1, source_target_pairs={{0,16},{16,0},{1,17},{17,1},{2,18},{18,2},{3,19},{19,3},{4,20},{20... | collective-permute-start | bytes 3538952 | tf_op jit(solution)/shard_map/ppermute | solution.py:931
  139.5 5.8 %collective-permute-start.27 = (f32[8,768]{1,0:T(8,128)S(1)}, f32[8,768]{1,0:T(8,128)S(1)}, u32[]{:S(2)}, u32[]{:S(2)}) collective-permute-start(f32[8,768]{1,0:T(8,128)S(1)} %small.1.refs_2_.refs_7_), channel_id=1, source_target_pairs={{0,4},{4,0},{1,5},{5,1},{2,6},{6,2},{3,7},{7,3},{8,12},{12,8},{9,1... | collective-permute-start | bytes 73736 | tf_op jit(solution)/shard_map/ppermute | solution.py:931
  148.0 52.0 %collective-permute-start.32 = (bf16[400,2048]{1,0:T(8,128)(2,1)S(1)}, bf16[400,2048]{1,0:T(8,128)(2,1)S(1)}, u32[]{:S(2)}, u32[]{:S(2)}) collective-permute-start(bf16[400,2048]{1,0:T(8,128)(2,1)S(1)} %get-tuple-element.205), channel_id=1, source_target_pairs={{0,16},{16,0},{1,17},{17,1},{2,18},{18,2},{3,19},{19,3},{4,20},{20... | collective-permute-start | bytes 4915208 | tf_op jit(solution)/shard_map/ppermute | solution.py:931
  154.9 2.4 collective-permute-start.28
  155.0 18.6 %collective-permute-start.24 = (bf16[256,768]{1,0:T(8,128)(2,1)S(1)}, bf16[256,768]{1,0:T(8,128)(2,1)S(1)}, u32[]{:S(2)}, u32[]{:S(2)}) collective-permute-start(bf16[256,768]{1,0:T(8,128)(2,1)S(1)} %keep.2.refs_4_.refs_1_), channel_id=1, source_target_pairs={{0,2},{2,0},{1,3},{3,1},{4,6},{6,4},{5,7},{7,5},{8,10},{10,8},{9,1... | collective-permute-start | bytes 1179656 | tf_op jit(solution)/shard_map/ppermute | solution.py:931
  165.7 25.3 %collective-permute-start.33 = (bf16[192,1536]{1,0:T(8,128)(2,1)S(1)}, bf16[192,1536]{1,0:T(8,128)(2,1)S(1)}, u32[]{:S(2)}, u32[]{:S(2)}) collective-permute-start(bf16[192,1536]{1,0:T(8,128)(2,1)S(1)} %get-tuple-element.206), channel_id=1, source_target_pairs={{0,8},{8,0},{1,9},{9,1},{2,10},{10,2},{3,11},{11,3},{4,12},{12,4},... | collective-permute-start | bytes 1769480 | tf_op jit(solution)/shard_map/ppermute | solution.py:931
  173.5 29.9 %collective-permute-start.31 = (bf16[512,768]{1,0:T(8,128)(2,1)S(1)}, bf16[512,768]{1,0:T(8,128)(2,1)S(1)}, u32[]{:S(2)}, u32[]{:S(2)}) collective-permute-start(bf16[512,768]{1,0:T(8,128)(2,1)S(1)} %add.1.refs_11_), channel_id=1, source_target_pairs={{0,8},{8,0},{1,9},{9,1},{2,10},{10,2},{3,11},{11,3},{4,12},{12,4},... | collective-permute-start | bytes 2359304 | tf_op jit(solution)/shard_map/ppermute | solution.py:931
  185.7 17.8 %collective-permute-start.30 = (bf16[512,768]{1,0:T(8,128)(2,1)S(1)}, bf16[512,768]{1,0:T(8,128)(2,1)S(1)}, u32[]{:S(2)}, u32[]{:S(2)}) collective-permute-start(bf16[512,768]{1,0:T(8,128)(2,1)S(1)} %get-tuple-element.204), channel_id=1, source_target_pairs={{0,4},{4,0},{1,5},{5,1},{2,6},{6,2},{3,7},{7,3},{8,12},{12,8},{9,1... | collective-permute-start | bytes 2359304 | tf_op jit(solution)/shard_map/ppermute | solution.py:931
  185.7 21.5 %collective-permute-start.29 = (bf16[2,256,768]{2,1,0:T(8,128)(2,1)S(1)}, bf16[2,256,768]{2,1,0:T(8,128)(2,1)S(1)}, u32[]{:S(2)}, u32[]{:S(2)}) collective-permute-start(bf16[2,256,768]{2,1,0:T(8,128)(2,1)S(1)} %pair.1.refs_14_.refs_1_), channel_id=1, source_target_pairs={{0,1},{1,0},{2,3},{3,2},{4,5},{5,4},{6,7},{7,6},{8,9},{9,8},{10,11... | collective-permute-start | bytes 2359304 | tf_op jit(solution)/shard_map/ppermute | solution.py:931
  201.0 22.9 %collective-permute-start.41 = (bf16[208,2048]{1,0:T(8,128)(2,1)S(1)}, bf16[208,2048]{1,0:T(8,128)(2,1)S(1)}, u32[]{:S(2)}, u32[]{:S(2)}) collective-permute-start(bf16[208,2048]{1,0:T(8,128)(2,1)S(1)} %get-tuple-element.224), channel_id=1, source_target_pairs={{0,8},{8,0},{1,9},{9,1},{2,10},{10,2},{3,11},{11,3},{4,12},{12,4},... | collective-permute-start | bytes 2555912 | tf_op jit(solution)/shard_map/ppermute | solution.py:931
  202.2 9.1 %collective-permute-start.35 = (bf16[2,96,768]{2,1,0:T(8,128)(2,1)S(1)}, bf16[2,96,768]{2,1,0:T(8,128)(2,1)S(1)}, u32[]{:S(2)}, u32[]{:S(2)}) collective-permute-start(bf16[2,96,768]{2,1,0:T(8,128)(2,1)S(1)} %get-tuple-element.219), channel_id=1, source_target_pairs={{0,1},{1,0},{2,3},{3,2},{4,5},{5,4},{6,7},{7,6},{8,9},{9,8},{10,11... | collective-permute-start | bytes 884744 | tf_op jit(solution)/shard_map/ppermute | solution.py:931
  204.3 15.6 %collective-permute-start.34 = (bf16[256,768]{1,0:T(8,128)(2,1)S(1)}, bf16[256,768]{1,0:T(8,128)(2,1)S(1)}, u32[]{:S(2)}, u32[]{:S(2)}) collective-permute-start(bf16[256,768]{1,0:T(8,128)(2,1)S(1)} %get-tuple-element.217.refs_3_), channel_id=1, source_target_pairs={{0,1},{1,0},{2,3},{3,2},{4,5},{5,4},{6,7},{7,6},{8,9},{9,8},{10,11... | collective-permute-start | bytes 1179656 | tf_op jit(solution)/shard_map/ppermute | solution.py:931
  206.8 25.9 %collective-permute-start.38 = (bf16[208,1280]{1,0:T(8,128)(2,1)S(1)}, bf16[208,1280]{1,0:T(8,128)(2,1)S(1)}, u32[]{:S(2)}, u32[]{:S(2)}) collective-permute-start(bf16[208,1280]{1,0:T(8,128)(2,1)S(1)} %get-tuple-element.221), channel_id=1, source_target_pairs={{0,8},{8,0},{1,9},{9,1},{2,10},{10,2},{3,11},{11,3},{4,12},{12,4},... | collective-permute-start | bytes 1597448 | tf_op jit(solution)/shard_map/ppermute | solution.py:931
  207.2 27.5 %collective-permute-start.39 = (bf16[208,1280]{1,0:T(8,128)(2,1)S(1)}, bf16[208,1280]{1,0:T(8,128)(2,1)S(1)}, u32[]{:S(2)}, u32[]{:S(2)}) collective-permute-start(bf16[208,1280]{1,0:T(8,128)(2,1)S(1)} %get-tuple-element.222), channel_id=1, source_target_pairs={{0,16},{16,0},{1,17},{17,1},{2,18},{18,2},{3,19},{19,3},{4,20},{20... | collective-permute-start | bytes 1597448 | tf_op jit(solution)/shard_map/ppermute | solution.py:931
  211.4 33.3 %collective-permute-start.40 = (bf16[208,1280]{1,0:T(8,128)(2,1)S(1)}, bf16[208,1280]{1,0:T(8,128)(2,1)S(1)}, u32[]{:S(2)}, u32[]{:S(2)}) collective-permute-start(bf16[208,1280]{1,0:T(8,128)(2,1)S(1)} %get-tuple-element.223), channel_id=1, source_target_pairs={{0,24},{8,16},{16,8},{24,0},{1,25},{9,17},{17,9},{25,1},{2,26},{10... | collective-permute-start | bytes 1597448 | tf_op jit(solution)/shard_map/ppermute | solution.py:989
  220.5 25.2 %collective-permute-start.37 = (bf16[256,768]{1,0:T(8,128)(2,1)S(1)}, bf16[256,768]{1,0:T(8,128)(2,1)S(1)}, u32[]{:S(2)}, u32[]{:S(2)}) collective-permute-start(bf16[256,768]{1,0:T(8,128)(2,1)S(1)} %final.1.refs_3_.refs_1_), channel_id=1, source_target_pairs={{0,2},{2,0},{1,3},{3,1},{4,6},{6,4},{5,7},{7,5},{8,10},{10,8},{9,1... | collective-permute-start | bytes 1179656 | tf_op jit(solution)/shard_map/ppermute | solution.py:931
  224.9 25.6 %collective-permute-start.44 = (bf16[2,112,1024]{2,1,0:T(8,128)(2,1)S(1)}, bf16[2,112,1024]{2,1,0:T(8,128)(2,1)S(1)}, u32[]{:S(2)}, u32[]{:S(2)}) collective-permute-start(bf16[2,112,1024]{2,1,0:T(8,128)(2,1)S(1)} %get-tuple-element.228), channel_id=1, source_target_pairs={{0,1},{1,0},{2,3},{3,2},{4,5},{5,4},{6,7},{7,6},{8,9},{9,8},{10,11... | collective-permute-start | bytes 1376264 | tf_op jit(solution)/shard_map/ppermute | solution.py:931
  232.7 42.4 %collective-permute-start.36 = (bf16[256,768]{1,0:T(8,128)(2,1)S(1)}, bf16[256,768]{1,0:T(8,128)(2,1)S(1)}, u32[]{:S(2)}, u32[]{:S(2)}) collective-permute-start(bf16[256,768]{1,0:T(8,128)(2,1)S(1)} %final.1.refs_3_.refs_1_), channel_id=1, source_target_pairs={{0,1},{1,0},{2,3},{3,2},{4,5},{5,4},{6,7},{7,6},{8,9},{9,8},{10,11... | collective-permute-start | bytes 1179656 | tf_op jit(solution)/shard_map/ppermute | solution.py:931
  246.3 28.8 %collective-permute-start.42 = (bf16[256,768]{1,0:T(8,128)(2,1)S(1)}, bf16[256,768]{1,0:T(8,128)(2,1)S(1)}, u32[]{:S(2)}, u32[]{:S(2)}) collective-permute-start(bf16[256,768]{1,0:T(8,128)(2,1)S(1)} %keep.3.refs_3_), channel_id=1, source_target_pairs={{0,1},{1,0},{2,3},{3,2},{4,5},{5,4},{6,7},{7,6},{8,9},{9,8},{10,11... | collective-permute-start | bytes 1179656 | tf_op jit(solution)/shard_map/ppermute | solution.py:931
  248.9 21.5 %collective-permute-start.43 = (bf16[2,112,640]{2,1,0:T(8,128)(2,1)S(1)}, bf16[2,112,640]{2,1,0:T(8,128)(2,1)S(1)}, u32[]{:S(2)}, u32[]{:S(2)}) collective-permute-start(bf16[2,112,640]{2,1,0:T(8,128)(2,1)S(1)} %get-tuple-element.227), channel_id=1, source_target_pairs={{0,1},{1,0},{2,3},{3,2},{4,5},{5,4},{6,7},{7,6},{8,9},{9,8},{10,11... | collective-permute-start | bytes 860168 | tf_op jit(solution)/shard_map/ppermute | solution.py:931
  249.0 18.3 %collective-permute-start.48 = (bf16[96,768]{1,0:T(8,128)(2,1)S(1)}, bf16[96,768]{1,0:T(8,128)(2,1)S(1)}, u32[]{:S(2)}, u32[]{:S(2)}) collective-permute-start(bf16[96,768]{1,0:T(8,128)(2,1)S(1)} %get-tuple-element.232), channel_id=1, source_target_pairs={{0,4},{1,5},{2,0},{3,1},{4,6},{5,7},{6,2},{7,3},{8,12},{9,13},{10,... | collective-permute-start | bytes 442376 | tf_op jit(solution)/shard_map/ppermute | solution.py:941
  251.2 30.1 %collective-permute-start.50 = (bf16[112,1024]{1,0:T(8,128)(2,1)S(1)}, bf16[112,1024]{1,0:T(8,128)(2,1)S(1)}, u32[]{:S(2)}, u32[]{:S(2)}) collective-permute-start(bf16[112,1024]{1,0:T(8,128)(2,1)S(1)} %get-tuple-element.233), channel_id=1, source_target_pairs={{0,4},{1,5},{2,0},{3,1},{4,6},{5,7},{6,2},{7,3},{8,12},{9,13},{10,... | collective-permute-start | bytes 688136 | tf_op jit(solution)/shard_map/ppermute | solution.py:941
  267.3 14.0 %collective-permute-start.49 = (bf16[112,1024]{1,0:T(8,128)(2,1)S(1)}, bf16[112,1024]{1,0:T(8,128)(2,1)S(1)}, u32[]{:S(2)}, u32[]{:S(2)}) collective-permute-start(bf16[112,1024]{1,0:T(8,128)(2,1)S(1)} %get-tuple-element.229.refs_3_), channel_id=1, source_target_pairs={{0,0},{1,1},{2,4},{3,5},{4,2},{5,3},{6,6},{7,7},{8,8},{9,9},{10,12... | collective-permute-start | bytes 688136 | tf_op jit(solution)/shard_map/ppermute | solution.py:941
  270.4 10.9 %collective-permute-start.47 = (bf16[96,768]{1,0:T(8,128)(2,1)S(1)}, bf16[96,768]{1,0:T(8,128)(2,1)S(1)}, u32[]{:S(2)}, u32[]{:S(2)}) collective-permute-start(bf16[96,768]{1,0:T(8,128)(2,1)S(1)} %get-tuple-element.220.refs_3_), channel_id=1, source_target_pairs={{0,0},{1,1},{2,4},{3,5},{4,2},{5,3},{6,6},{7,7},{8,8},{9,9},{10,12... | collective-permute-start | bytes 442376 | tf_op jit(solution)/shard_map/ppermute | solution.py:941
  275.1 9.2 %collective-permute-start.46 = (bf16[112,640]{1,0:T(8,128)(2,1)S(1)}, bf16[112,640]{1,0:T(8,128)(2,1)S(1)}, u32[]{:S(2)}, u32[]{:S(2)}) collective-permute-start(bf16[112,640]{1,0:T(8,128)(2,1)S(1)} %get-tuple-element.231), channel_id=1, source_target_pairs={{0,4},{1,5},{2,0},{3,1},{4,6},{5,7},{6,2},{7,3},{8,12},{9,13},{10,... | collective-permute-start | bytes 430088 | tf_op jit(solution)/shard_map/ppermute | solution.py:941
  275.2 10.8 %collective-permute-start.45 = (bf16[112,640]{1,0:T(8,128)(2,1)S(1)}, bf16[112,640]{1,0:T(8,128)(2,1)S(1)}, u32[]{:S(2)}, u32[]{:S(2)}) collective-permute-start(bf16[112,640]{1,0:T(8,128)(2,1)S(1)} %get-tuple-element.230.refs_5_), channel_id=1, source_target_pairs={{0,0},{1,1},{2,4},{3,5},{4,2},{5,3},{6,6},{7,7},{8,8},{9,9},{10,12... | collective-permute-start | bytes 430088 | tf_op jit(solution)/shard_map/ppermute | solution.py:941
  (44 other events, 349.6 us)
Sparse Core Ops, SparseCore 0:
  47.6 52.3 all-gather.2

commit v4 on v3

--- a/solution.py
+++ b/solution.py
@@ -713,19 +713,24 @@
     out[6:8, :] = jnp.zeros((2, out.shape[1]), WIDE)
 
 
+def grad_u_kernel(_, own, peer, units, whole, turned):
+    turn((own, peer), turned)
+    for c in range(0, units.shape[1], 256):
+        whole[:, c : c + 256] = nn(turned[...], units[:, c : c + 256]).astype(LOW)
+
+
 def grad_uo_kernel(
-    me, own, peer, units, eb_own, eb_peer, o, small, small_peer, sum_u, kept, sent, turned, whole
+    me, of_u, eb_own, eb_peer, o, small, small_peer, sum_u, kept, sent, turned, of_o
 ):
-    turn((own, peer), turned)
-    hidden = units.shape[1]
-    for c in range(0, hidden, 256):
-        whole[:, c : c + 256] = nn(turned[...], units[:, c : c + 256]).astype(LOW)
     turn((eb_own, eb_peer), turned)
-    whole[:, hidden:] = nn(turned[...], o[...]).astype(LOW)
-    count = whole.shape[0] // 4
+    of_o[...] = nn(turned[...], o[...]).astype(LOW)
+    hidden = of_u.shape[1]
+    count = of_u.shape[0] // 4
     for j in range(2):
-        kept[j * count : (j + 1) * count, :] = whole[group_rows(me, j, count), :]
-        sent[j * count : (j + 1) * count, :] = whole[group_rows(me, j + 2, count), :]
+        for i, out in ((j, kept), (j + 2, sent)):
+            target = slice(j * count, (j + 1) * count)
+            out[target, :hidden] = of_u[group_rows(me, i, count), :]
+            out[target, hidden:] = of_o[group_rows(me, i, count), :]
     high, low = split_sum(small[...] + small_peer[...])
     units_high, units_low = split_sum(jnp.sum(sum_u[...], axis=0, keepdims=True))
     for out in (kept, sent):
@@ -1120,20 +1125,24 @@
     out_own = move(out_own, lambda c, hh, ll: (ll, hh, c))
 
     e_peer = core(e_own)
+    units, part_own, part_peer, sum_u = call(
+        units_kernel, "units", spot, [e_own, e_peer, wd, wu, slope],
+        [((rows, 2 * hidden), LOW)] + own_peer + [((8, 2 * hidden), WIDE)],
+    )
     kept_d, sent_d = call(
         grad_d_kernel, "grad_d", spot, [e_own, e_peer, act],
         [((4 * eighth, 2 * hidden), LOW)] * 2,
         [VMEM((width, rows), LOW), VMEM((width, 2 * hidden), LOW)], 8,
     )
-    units, part_own, part_peer, sum_u = call(
-        units_kernel, "units", spot, [e_own, e_peer, wd, wu, slope],
-        [((rows, 2 * hidden), LOW)] + own_peer + [((8, 2 * hidden), WIDE)],
-    )
     grad_one, eb_own, sums_one = call(
         norm_one_back_kernel, "norm_one_back", spot,
         [part_own, core(part_peer), grad_two, normed_one, inverse_one, params], grad_outs,
     )
     eb_peer = core(eb_own)
+    of_u = call(
+        grad_u_kernel, "grad_u", spot, [first_own, first_peer, units],
+        [((width, 2 * hidden), LOW)], [VMEM((width, rows), LOW)], 8,
+    )[0]
     small = call(small_kernel, "small", spot, [sums_one, sums_two], [((8, width), WIDE)])[0]
     out_own = call(copy_kernel, "keep", spot, [out_own], [((half, width), LOW)])[0]
     out_far = flip(out_own, "th")
@@ -1141,9 +1150,9 @@
     uo_columns = 2 * hidden + 512
     kept_uo, sent_uo = call(
         grad_uo_kernel, "grad_uo", spot,
-        [first_own, first_peer, units, eb_own, eb_peer, o, small, core(small), sum_u],
+        [of_u, eb_own, eb_peer, o, small, core(small), sum_u],
         [((4 * eighth + RIDE, uo_columns), LOW)] * 2,
-        [VMEM((width, rows), LOW), VMEM((width, uo_columns), LOW)], 8,
+        [VMEM((width, rows), LOW), VMEM((width, 512), LOW)], 8,
     )
 
     if square:

time: 298 us -> 296 us (level)
  starting transfers between devices: 75.6 us -> 58.5 us
  Pallas kernels: 90.9 us -> 103 us
  waiting for transfers between devices: 98.3 us -> 104 us
    ppermute x37, starting transfers between devices: 43.5 us -> 28.6 us  [flip(): return lax.ppermute(value, axis, FLIP)]
    pallas_call x43 -> x44, Pallas kernels: 90.9 us -> 103 us  [__call__(): pl.pallas_call(run, out_shape=tuple((pltpu.HBM(shape, kind) if out else j...]
    ppermute x37, waiting for transfers between devices: 54 us -> 65.9 us  [flip(): return lax.ppermute(value, axis, FLIP)]
    all_gather x1, waiting for transfers between devices: 7.32 us -> 3.69 us  [body(): all_d = lax.all_gather(rows_d, ('th', 'tl'), axis=0)]
  transfers between devices with their start and end apart: 52 -> 52, of which waited for: 21 -> 23; matrix products, arithmetic and copies ran while one was open for 0% -> 0% of each run, Pallas kernels for 26% -> 30%
where the time goes in v4:
time: 296 us; the launch traced here: 295 us
  waiting for transfers between devices  104 us (35%)
  Pallas kernels  103 us (35%)
  starting transfers between devices  58.5 us (20%)
  local copies, waits for them, and re-layouts  15.1 us (5%)
  between operations  14.9 us (5%)
    pallas_call x44, Pallas kernels, __call__(): pl.pallas_call(run, out_shape=tuple((pltpu.HBM(shape, kind) if out else j...  103 us
    ppermute x37, waiting for transfers between devices, flip(): return lax.ppermute(value, axis, FLIP)  65.9 us
    ppermute x37, starting transfers between devices, flip(): return lax.ppermute(value, axis, FLIP)  28.6 us
    ppermute x11, starting transfers between devices, move(): return lax.ppermute(value, ('cc', 'th', 'tl'), pairs)  25.1 us
    ppermute x11, waiting for transfers between devices, move(): return lax.ppermute(value, ('cc', 'th', 'tl'), pairs)  24.4 us
    unnamed x80, local copies, waits for them, and re-layouts  15.1 us
    ppermute x3, waiting for transfers between devices, exchange(): lax.ppermute(far, plane, [(i, i ^ 3) for i in range(4)])  9.7 us
  transfers between devices with their start and end apart: 52, of which 23 were waited for; matrix products, arithmetic and copies ran while one was open for 0% of the time, Pallas kernels for 30%

profile of v4, /device:TPU:1, one launch (start us, length us, event | category | flops | bytes accessed | tf_op | source)
XLA Modules:
  0.0 295.1 jit_solution(2911885113089239350)
XLA Ops:
  9.4 1.8 pack.1
  11.3 2.0 pick.1
  13.4 2.7 collective-permute-start.5
  17.9 4.1 %collective-permute-start.1 = (bf16[112,640]{1,0:T(8,128)(2,1)S(1)}, bf16[112,640]{1,0:T(8,128)(2,1)S(1)}, u32[]{:S(2)}, u32[]{:S(2)}) collective-permute-start(bf16[112,640]{1,0:T(8,128)(2,1)S(1)} %get-tuple-element.133.refs_3_), channel_id=1, source_target_pairs={{0,0},{1,1},{2,4},{3,5},{4,2},{5,3},{6,6},{7,7},{8,8},{9,9},{10,12... | collective-permute-start | bytes 430088 | tf_op jit(solution)/shard_map/ppermute | solution.py:946
  26.7 1.8 settle.1
  29.5 1.9 collective-permute-start.4
  32.2 5.0 %collective-permute-start.6 = (bf16[96,1024]{1,0:T(8,128)(2,1)S(1)}, bf16[96,1024]{1,0:T(8,128)(2,1)S(1)}, u32[]{:S(2)}, u32[]{:S(2)}) collective-permute-start(bf16[96,1024]{1,0:T(8,128)(2,1)S(1)} %get-tuple-element.140.refs_8_), channel_id=1, source_target_pairs={{0,0},{1,1},{2,4},{3,5},{4,2},{5,3},{6,6},{7,7},{8,8},{9,9},{10,12... | collective-permute-start | bytes 589832 | tf_op jit(solution)/shard_map/ppermute | solution.py:946
  37.2 1.8 collective-permute-done.7.refs_5_
  39.0 3.9 %collective-permute-done.6.refs_4_ = bf16[96,1024]{1,0:T(8,128)(2,1)S(1)} collective-permute-done((bf16[96,1024]{1,0:T(8,128)(2,1)S(1)}, bf16[96,1024]{1,0:T(8,128)(2,1)S(1)}, u32[]{:S(2)}, u32[]{:S(2)}) %collective-permute-start.6) | collective-permute-done | bytes 196640 | tf_op jit(solution)/shard_map/ppermute | solution.py:946
  51.9 11.9 %collective-permute-done.12.refs_2_ = bf16[2,96,1024]{2,1,0:T(8,128)(2,1)S(1)} collective-permute-done((bf16[2,96,1024]{2,1,0:T(8,128)(2,1)}, bf16[2,96,1024]{2,1,0:T(8,128)(2,1)S(1)}, u32[]{:S(2)}, u32[]{:S(2)}) %collective-permute-start.12) | collective-permute-done | bytes 393248 | tf_op jit(solution)/shard_map/ppermute | solution.py:936
  63.7 8.8 %collective-permute-done.10.refs_5_.refs_3_ = bf16[2,2,96,640]{3,2,1,0:T(8,128)(2,1)S(1)} collective-permute-done((bf16[2,2,96,640]{3,2,1,0:T(8,128)(2,1)}, bf16[2,2,96,640]{3,2,1,0:T(8,128)(2,1)S(1)}, u32[]{:S(2)}, u32[]{:S(2)}) %collective-permute-start.10) | collective-permute-done | bytes 491552 | tf_op jit(solution)/shard_map/ppermute | solution.py:936
  76.9 2.0 join.1
  78.9 7.1 %project.1 = (bf16[2048,768]{1,0:T(8,128)(2,1)S(1)}, bf16[512,512]{1,0:T(8,128)(2,1)S(1)}, bf16[512,768]{1,0:T(8,128)(2,1)}, bf16[512,768]{1,0:T(8,128)(2,1)}, b...) custom-call(s32[6]{0:T(128)S(1)} %stack.24.refs_0_, bf16[768,768]{1,0:T(8,128)(2,1)} %bitcast.23, ...), custom_call_target="tpu_custom_call" | custom-call | flops 1 | bytes 1 | tf_op jit(solution)/shard_map/project/pallas_call | solution.py:288
  86.1 10.2 %attend.1 = (bf16[512,512]{1,0:T(8,128)(2,1)S(1)}, f32[8,512]{1,0:T(8,128)S(1)}) custom-call(s32[6]{0:T(128)S(1)} %stack.24.refs_0_, s32[2,2048]{1,0:T(2,128)S(1)} %copy-done.18, bf16[512,512]{1,0:T(8,128)(2,1)S(1)} %get-tuple-element.152.refs_2_.refs_6_, bf16[2048,768]{1,0:T(8,128)(2,1)S(1)} %get-tuple-element.153.refs_3_, ...), custom_call_target="tpu_custom_call" | custom-call | flops 1 | bytes 1 | tf_op jit(solution)/shard_map/attend/pallas_call | solution.py:288
  96.3 3.7 %all-gather.3.cloned.1.call-done = bf16[16,96,768]{2,1,0:T(8,128)(2,1)} async-done(((bf16[4,96,768]{2,1,0:T(8,128)(2,1)}), bf16[16,96,768]{2,1,0:T(8,128)(2,1)}) %all-gather.3.cloned.1.call-update) | async-done | bytes 2359312 | tf_op jit(solution)/shard_map/all_gather | solution.py:1057
  100.0 1.7 copy-done
  102.8 8.7 %collective-permute-done.16.refs_3_ = bf16[2,2,96,1024]{3,2,1,0:T(8,128)(2,1)} collective-permute-done((bf16[2,2,96,1024]{3,2,1,0:T(8,128)(2,1)S(1)}, bf16[2,2,96,1024]{3,2,1,0:T(8,128)(2,1)}, u32[]{:S(2)}, u32[]{:S(2)}) %collective-permute-start.16) | collective-permute-done | bytes 786464 | tf_op jit(solution)/shard_map/ppermute | solution.py:936
  111.5 2.5 branch.1
  118.7 2.7 up.1
  121.4 2.1 down.1
  128.5 3.3 %units.1 = (bf16[512,1536]{1,0:T(8,128)(2,1)S(1)}, f32[256,768]{1,0:T(8,128)S(1)}, bf16[256,768]{1,0:T(8,128)(2,1)S(1)}, f32[8,1536]{1,0:T(8,128)S(1)}) custom-call(s32[6]{0:T(128)S(1)} %stack.24.refs_0_, bf16[256,768]{1,0:T(8,128)(2,1)S(1)} %get-tuple-element.170.refs_1_, bf16[256,768]{1,0:T(8,128)(2,1)S(1)} %collective-permute-done.22.refs_2_, ...), custom_call_target="tpu_custom_call" | custom-call | flops 1 | bytes 1 | tf_op jit(solution)/shard_map/units/pallas_call | solution.py:288
  132.2 2.2 collective-permute-start.21
  134.4 2.1 grad_d.1
  139.0 2.0 grad_u.1.refs_3_.refs_1_
  145.8 9.5 %attend_cd.1 = (f32[384,512]{1,0:T(8,128)S(1)}, bf16[1024,768]{1,0:T(8,128)(2,1)S(1)}, f32[512,768]{1,0:T(8,128)S(1)}, bf16[512,768]{1,0:T(8,128)(2,1)S(1)}, f32...) custom-call(s32[6]{0:T(128)S(1)} %stack.24.refs_0_, ...), custom_call_target="tpu_custom_call" | custom-call | flops 1 | bytes 1 | tf_op jit(solution)/shard_map/attend_cd/pallas_call | solution.py:288
  155.7 2.0 collective-permute-done.28.refs_2_
  158.4 10.0 %attend_a.1 = (f32[384,512]{1,0:T(8,128)S(1)}, bf16[512,768]{1,0:T(8,128)(2,1)S(1)}, f32[512,768]{1,0:T(8,128)S(1)}, f32[8,768]{1,0:T(8,128)S(1)}) custom-call(s32[6]{0:T(128)S(1)} %stack.24.refs_0_, s32[2,2048]{1,0:T(2,128)S(1)} %copy-done.19, bf16[512,768]{1,0:T(8,128)(2,1)} %get-tuple-element.182.refs_2_, ...), custom_call_target="tpu_custom_call" | custom-call | flops 1 | bytes 1 | tf_op jit(solution)/shard_map/attend_a/pallas_call | solution.py:288
  170.7 4.8 %collective-permute-done.24.refs_2_ = bf16[256,768]{1,0:T(8,128)(2,1)S(1)} collective-permute-done((bf16[256,768]{1,0:T(8,128)(2,1)S(1)}, bf16[256,768]{1,0:T(8,128)(2,1)S(1)}, u32[]{:S(2)}, u32[]{:S(2)}) %collective-permute-start.24) | collective-permute-done | bytes 393248 | tf_op jit(solution)/shard_map/ppermute | solution.py:936
  176.1 11.1 %attend_b.1 = (bf16[512,512]{1,0:T(8,128)(2,1)S(1)}, bf16[512,768]{1,0:T(8,128)(2,1)S(1)}, f32[512,768]{1,0:T(8,128)S(1)}, bf16[512,768]{1,0:T(8,128)(2,1)S(1)},...) custom-call(s32[6]{0:T(128)S(1)} %stack.24.refs_0_, s32[2,2048]{1,0:T(2,128)S(1)} %copy-done.19, ...), custom_call_target="tpu_custom_call" | custom-call | flops 1 | bytes 1 | tf_op jit(solution)/shard_map/attend_b/pallas_call | solution.py:288
  188.4 5.2 %grad_qkv.1 = (bf16[208,1280]{1,0:T(8,128)(2,1)S(1)}, bf16[208,1280]{1,0:T(8,128)(2,1)S(1)}, bf16[208,1280]{1,0:T(8,128)(2,1)S(1)}, bf16[208,1280]{1,0:T(8,128)(2,1)S(1)}) custom-call(s32[6]{0:T(128)S(1)} %stack.24.refs_0_, bf16[512,768]{1,0:T(8,128)(2,1)S(1)} %get-tuple-element.134.refs_1_.refs_3_, ...), custom_call_target="tpu_custom_call" | custom-call | flops 1 | bytes 1 | tf_op jit(solution)/shard_map/grad_qkv/pallas_call | solution.py:288
  194.6 5.4 %collective-permute-done.32.refs_2_ = bf16[400,2048]{1,0:T(8,128)(2,1)S(1)} collective-permute-done((bf16[400,2048]{1,0:T(8,128)(2,1)S(1)}, bf16[400,2048]{1,0:T(8,128)(2,1)S(1)}, u32[]{:S(2)}, u32[]{:S(2)}) %collective-permute-start.32) | collective-permute-done | bytes 1638432 | tf_op jit(solution)/shard_map/ppermute | solution.py:936
  205.7 1.8 collective-permute-done.29.refs_2_
  207.5 6.3 %collective-permute-done.35.refs_2_ = bf16[2,96,768]{2,1,0:T(8,128)(2,1)S(1)} collective-permute-done((bf16[2,96,768]{2,1,0:T(8,128)(2,1)S(1)}, bf16[2,96,768]{2,1,0:T(8,128)(2,1)S(1)}, u32[]{:S(2)}, u32[]{:S(2)}) %collective-permute-start.35) | collective-permute-done | bytes 294944 | tf_op jit(solution)/shard_map/ppermute | solution.py:936
  213.8 2.3 collective-permute-start.40
  216.2 1.8 output.1.refs_3_
  220.1 2.2 collective-permute-done.34.refs_2_
  225.1 6.5 %collective-permute-done.38.refs_2_ = bf16[208,1280]{1,0:T(8,128)(2,1)S(1)} collective-permute-done((bf16[208,1280]{1,0:T(8,128)(2,1)S(1)}, bf16[208,1280]{1,0:T(8,128)(2,1)S(1)}, u32[]{:S(2)}, u32[]{:S(2)}) %collective-permute-start.38) | collective-permute-done | bytes 532512 | tf_op jit(solution)/shard_map/ppermute | solution.py:936
  231.6 2.6 collective-permute-start.36
  234.2 9.7 %collective-permute-done.40.refs_4_ = bf16[208,1280]{1,0:T(8,128)(2,1)S(1)} collective-permute-done((bf16[208,1280]{1,0:T(8,128)(2,1)S(1)}, bf16[208,1280]{1,0:T(8,128)(2,1)S(1)}, u32[]{:S(2)}, u32[]{:S(2)}) %collective-permute-start.40) | collective-permute-done | bytes 532512 | tf_op jit(solution)/shard_map/ppermute | solution.py:994
  245.5 1.8 collective-permute-start.42
  248.9 2.6 collective-permute-start.50
  251.5 14.8 %collective-permute-done.48.refs_2_ = bf16[96,768]{1,0:T(8,128)(2,1)S(1)} collective-permute-done((bf16[96,768]{1,0:T(8,128)(2,1)S(1)}, bf16[96,768]{1,0:T(8,128)(2,1)S(1)}, u32[]{:S(2)}, u32[]{:S(2)}) %collective-permute-start.48) | collective-permute-done | bytes 147488 | tf_op jit(solution)/shard_map/ppermute | solution.py:946
  266.3 1.9 collective-permute-start.49
  268.2 2.1 collective-permute-done.43.refs_2_
  270.3 4.1 %collective-permute-start.47 = (bf16[96,768]{1,0:T(8,128)(2,1)S(1)}, bf16[96,768]{1,0:T(8,128)(2,1)S(1)}, u32[]{:S(2)}, u32[]{:S(2)}) collective-permute-start(bf16[96,768]{1,0:T(8,128)(2,1)S(1)} %get-tuple-element.220.refs_3_), channel_id=1, source_target_pairs={{0,0},{1,1},{2,4},{3,5},{4,2},{5,3},{6,6},{7,7},{8,8},{9,9},{10,12... | collective-permute-start | bytes 442376 | tf_op jit(solution)/shard_map/ppermute | solution.py:946
  275.1 3.1 %collective-permute-start.45 = (bf16[112,640]{1,0:T(8,128)(2,1)S(1)}, bf16[112,640]{1,0:T(8,128)(2,1)S(1)}, u32[]{:S(2)}, u32[]{:S(2)}) collective-permute-start(bf16[112,640]{1,0:T(8,128)(2,1)S(1)} %get-tuple-element.230.refs_5_), channel_id=1, source_target_pairs={{0,0},{1,1},{2,4},{3,5},{4,2},{5,3},{6,6},{7,7},{8,8},{9,9},{10,12... | collective-permute-start | bytes 430088 | tf_op jit(solution)/shard_map/ppermute | solution.py:946
  278.2 1.8 place.1.refs_5_
  284.6 1.6 collective-permute-done.45.refs_1_
  (182 shorter events, 69.5 us)
Async XLA Ops:
  7.2 92.8 %all-gather.3.cloned.1.call-start = ((), (), s32[]{:S(2)}) async-start(), calls=%async_computation | async-start | bytes 2949120 | tf_op jit(solution)/shard_map/all_gather | solution.py:1057
  13.2 13.5 %collective-permute-start = (bf16[768,768]{1,0:T(8,128)(2,1)S(1)}, bf16[768,768]{1,0:T(8,128)(2,1)S(1)}, u32[]{:S(2)}, u32[]{:S(2)}) collective-permute-start(bf16[768,768]{1,0:T(8,128)(2,1)S(1)} %get-tuple-element.135), channel_id=1, source_target_pairs={{0,4},{4,0},{1,5},{5,1},{2,6},{6,2},{3,7},{7,3},{8,12},{12,8},{9,1... | collective-permute-start | bytes 3538952 | tf_op jit(solution)/shard_map/ppermute | solution.py:936
  13.4 23.8 %collective-permute-start.5 = (bf16[512,768]{1,0:T(8,128)(2,1)S(1)}, bf16[512,768]{1,0:T(8,128)(2,1)S(1)}, u32[]{:S(2)}, u32[]{:S(2)}) collective-permute-start(bf16[512,768]{1,0:T(8,128)(2,1)S(1)} %get-tuple-element.134.refs_1_.refs_3_), channel_id=1, source_target_pairs={{0,8},{8,0},{1,9},{9,1},{2,10},{10,2},{3,11},{11,3},{4,12},{12,4},... | collective-permute-start | bytes 2359304 | tf_op jit(solution)/shard_map/ppermute | solution.py:936
  16.0 10.7 %collective-permute-start.3 = (bf16[96,768]{1,0:T(8,128)(2,1)S(1)}, bf16[96,768]{1,0:T(8,128)(2,1)S(1)}, u32[]{:S(2)}, u32[]{:S(2)}) collective-permute-start(bf16[96,768]{1,0:T(8,128)(2,1)S(1)} %get-tuple-element.137.refs_6_), channel_id=1, source_target_pairs={{0,16},{16,0},{1,17},{17,1},{2,18},{18,2},{3,19},{19,3},{4,20},{20... | collective-permute-start | bytes 442376 | tf_op jit(solution)/shard_map/ppermute | solution.py:936
  17.3 8.8 %collective-permute-start.2 = (bf16[112,640]{1,0:T(8,128)(2,1)S(1)}, bf16[112,640]{1,0:T(8,128)(2,1)S(1)}, u32[]{:S(2)}, u32[]{:S(2)}) collective-permute-start(bf16[112,640]{1,0:T(8,128)(2,1)S(1)} %get-tuple-element.133.refs_3_), channel_id=1, source_target_pairs={{0,2},{1,3},{2,6},{3,7},{4,0},{5,1},{6,4},{7,5},{8,10},{9,11},{10,... | collective-permute-start | bytes 430088 | tf_op jit(solution)/shard_map/ppermute | solution.py:946
  17.9 8.8 %collective-permute-start.1 = (bf16[112,640]{1,0:T(8,128)(2,1)S(1)}, bf16[112,640]{1,0:T(8,128)(2,1)S(1)}, u32[]{:S(2)}, u32[]{:S(2)}) collective-permute-start(bf16[112,640]{1,0:T(8,128)(2,1)S(1)} %get-tuple-element.133.refs_3_), channel_id=1, source_target_pairs={{0,0},{1,1},{2,4},{3,5},{4,2},{5,3},{6,6},{7,7},{8,8},{9,9},{10,12... | collective-permute-start | bytes 430088 | tf_op jit(solution)/shard_map/ppermute | solution.py:946
  29.3 13.6 %collective-permute-start.8 = (bf16[2,96,768]{2,1,0:T(8,128)(2,1)S(1)}, bf16[2,96,768]{2,1,0:T(8,128)(2,1)S(1)}, u32[]{:S(2)}, u32[]{:S(2)}) collective-permute-start(bf16[2,96,768]{2,1,0:T(8,128)(2,1)S(1)} %get-tuple-element.141.refs_6_), channel_id=1, source_target_pairs={{0,8},{8,0},{1,9},{9,1},{2,10},{10,2},{3,11},{11,3},{4,12},{12,4},... | collective-permute-start | bytes 884744 | tf_op jit(solution)/shard_map/ppermute | solution.py:936
  29.5 13.4 %collective-permute-start.4 = (bf16[2,112,640]{2,1,0:T(8,128)(2,1)S(1)}, bf16[2,112,640]{2,1,0:T(8,128)(2,1)S(1)}, u32[]{:S(2)}, u32[]{:S(2)}) collective-permute-start(bf16[2,112,640]{2,1,0:T(8,128)(2,1)S(1)} %get-tuple-element.139.refs_1_), channel_id=1, source_target_pairs={{0,1},{1,0},{2,3},{3,2},{4,5},{5,4},{6,7},{7,6},{8,9},{9,8},{10,11... | collective-permute-start | bytes 860168 | tf_op jit(solution)/shard_map/ppermute | solution.py:936
  31.4 7.6 %collective-permute-start.7 = (bf16[96,1024]{1,0:T(8,128)(2,1)S(1)}, bf16[96,1024]{1,0:T(8,128)(2,1)S(1)}, u32[]{:S(2)}, u32[]{:S(2)}) collective-permute-start(bf16[96,1024]{1,0:T(8,128)(2,1)S(1)} %get-tuple-element.140.refs_8_), channel_id=1, source_target_pairs={{0,2},{1,3},{2,6},{3,7},{4,0},{5,1},{6,4},{7,5},{8,10},{9,11},{10,... | collective-permute-start | bytes 589832 | tf_op jit(solution)/shard_map/ppermute | solution.py:946
  32.2 10.7 %collective-permute-start.6 = (bf16[96,1024]{1,0:T(8,128)(2,1)S(1)}, bf16[96,1024]{1,0:T(8,128)(2,1)S(1)}, u32[]{:S(2)}, u32[]{:S(2)}) collective-permute-start(bf16[96,1024]{1,0:T(8,128)(2,1)S(1)} %get-tuple-element.140.refs_8_), channel_id=1, source_target_pairs={{0,0},{1,1},{2,4},{3,5},{4,2},{5,3},{6,6},{7,7},{8,8},{9,9},{10,12... | collective-permute-start | bytes 589832 | tf_op jit(solution)/shard_map/ppermute | solution.py:946
  47.5 16.2 %collective-permute-start.11 = (bf16[2,2,96,640]{3,2,1,0:T(8,128)(2,1)}, bf16[2,2,96,640]{3,2,1,0:T(8,128)(2,1)S(1)}, u32[]{:S(2)}, u32[]{:S(2)}) collective-permute-start(bf16[2,2,96,640]{3,2,1,0:T(8,128)(2,1)} %copy-done.15), channel_id=1, source_target_pairs={{0,24},{8,16},{16,8},{24,0},{1,25},{9,17},{17,9},{25,1},{2,26},{10... | collective-permute-start | bytes 1474568 | tf_op jit(solution)/shard_map/ppermute | solution.py:994
  48.7 23.8 %collective-permute-start.10 = (bf16[2,2,96,640]{3,2,1,0:T(8,128)(2,1)}, bf16[2,2,96,640]{3,2,1,0:T(8,128)(2,1)S(1)}, u32[]{:S(2)}, u32[]{:S(2)}) collective-permute-start(bf16[2,2,96,640]{3,2,1,0:T(8,128)(2,1)} %copy-done.15), channel_id=1, source_target_pairs={{0,16},{16,0},{1,17},{17,1},{2,18},{18,2},{3,19},{19,3},{4,20},{20... | collective-permute-start | bytes 1474568 | tf_op jit(solution)/shard_map/ppermute | solution.py:936
  50.0 22.5 %collective-permute-start.9 = (bf16[2,2,96,640]{3,2,1,0:T(8,128)(2,1)}, bf16[2,2,96,640]{3,2,1,0:T(8,128)(2,1)S(1)}, u32[]{:S(2)}, u32[]{:S(2)}) collective-permute-start(bf16[2,2,96,640]{3,2,1,0:T(8,128)(2,1)} %copy-done.15), channel_id=1, source_target_pairs={{0,8},{8,0},{1,9},{9,1},{2,10},{10,2},{3,11},{11,3},{4,12},{12,4},... | collective-permute-start | bytes 1474568 | tf_op jit(solution)/shard_map/ppermute | solution.py:936
  50.3 13.5 %collective-permute-start.12 = (bf16[2,96,1024]{2,1,0:T(8,128)(2,1)}, bf16[2,96,1024]{2,1,0:T(8,128)(2,1)S(1)}, u32[]{:S(2)}, u32[]{:S(2)}) collective-permute-start(bf16[2,96,1024]{2,1,0:T(8,128)(2,1)} %copy-done.22), channel_id=1, source_target_pairs={{0,1},{1,0},{2,3},{3,2},{4,5},{5,4},{6,7},{7,6},{8,9},{9,8},{10,11... | collective-permute-start | bytes 1179656 | tf_op jit(solution)/shard_map/ppermute | solution.py:936
  51.9 27.0 %collective-permute-start.13 = (bf16[512,768]{1,0:T(8,128)(2,1)}, bf16[512,768]{1,0:T(8,128)(2,1)S(1)}, u32[]{:S(2)}, u32[]{:S(2)}) collective-permute-start(bf16[512,768]{1,0:T(8,128)(2,1)} %get-tuple-element.148.refs_5_.refs_3_), channel_id=1, source_target_pairs={{0,4},{4,0},{1,5},{5,1},{2,6},{6,2},{3,7},{7,3},{8,12},{12,8},{9,1... | collective-permute-start | bytes 2359304 | tf_op jit(solution)/shard_map/ppermute | solution.py:936
  74.1 28.7 %collective-permute-start.17 = (bf16[2,2,96,1024]{3,2,1,0:T(8,128)(2,1)S(1)}, bf16[2,2,96,1024]{3,2,1,0:T(8,128)(2,1)}, u32[]{:S(2)}, u32[]{:S(2)}) collective-permute-start(bf16[2,2,96,1024]{3,2,1,0:T(8,128)(2,1)S(1)} %rows.1.refs_5_.refs_1_), channel_id=1, source_target_pairs={{0,24},{8,16},{16,8},{24,0},{1,25},{9,17},{17,9},{25,1},{2,26},{10... | collective-permute-start | bytes 2359304 | tf_op jit(solution)/shard_map/ppermute | solution.py:994
  75.4 36.2 %collective-permute-start.16 = (bf16[2,2,96,1024]{3,2,1,0:T(8,128)(2,1)S(1)}, bf16[2,2,96,1024]{3,2,1,0:T(8,128)(2,1)}, u32[]{:S(2)}, u32[]{:S(2)}) collective-permute-start(bf16[2,2,96,1024]{3,2,1,0:T(8,128)(2,1)S(1)} %rows.1.refs_5_.refs_1_), channel_id=1, source_target_pairs={{0,16},{16,0},{1,17},{17,1},{2,18},{18,2},{3,19},{19,3},{4,20},{20... | collective-permute-start | bytes 2359304 | tf_op jit(solution)/shard_map/ppermute | solution.py:936
  75.5 36.0 %collective-permute-start.15 = (bf16[2,2,96,1024]{3,2,1,0:T(8,128)(2,1)S(1)}, bf16[2,2,96,1024]{3,2,1,0:T(8,128)(2,1)}, u32[]{:S(2)}, u32[]{:S(2)}) collective-permute-start(bf16[2,2,96,1024]{3,2,1,0:T(8,128)(2,1)S(1)} %rows.1.refs_5_.refs_1_), channel_id=1, source_target_pairs={{0,8},{8,0},{1,9},{9,1},{2,10},{10,2},{3,11},{11,3},{4,12},{12,4},... | collective-permute-start | bytes 2359304 | tf_op jit(solution)/shard_map/ppermute | solution.py:936
  102.3 19.1 %collective-permute-start.14 = (bf16[2,4,96,768]{3,2,1,0:T(8,128)(2,1)S(1)}, bf16[2,4,96,768]{3,2,1,0:T(8,128)(2,1)S(1)}, u32[]{:S(2)}, u32[]{:S(2)}) collective-permute-start(bf16[2,4,96,768]{3,2,1,0:T(8,128)(2,1)S(1)} %give_d.1.refs_6_), channel_id=1, source_target_pairs={{0,4},{4,0},{1,5},{5,1},{2,6},{6,2},{3,7},{7,3},{8,12},{12,8},{9,1... | collective-permute-start | bytes 3538952 | tf_op jit(solution)/shard_map/ppermute | solution.py:936
  131.8 4.7 %collective-permute-start.23 = (bf16[256,768]{1,0:T(8,128)(2,1)S(1)}, bf16[256,768]{1,0:T(8,128)(2,1)S(1)}, u32[]{:S(2)}, u32[]{:S(2)}) collective-permute-start(bf16[256,768]{1,0:T(8,128)(2,1)S(1)} %get-tuple-element.175), channel_id=1, source_target_pairs={{0,4},{4,0},{1,5},{5,1},{2,6},{6,2},{3,7},{7,3},{8,12},{12,8},{9,1... | collective-permute-start | bytes 1179656 | tf_op jit(solution)/shard_map/ppermute | solution.py:936
  132.2 10.1 %collective-permute-start.21 = (bf16[256,768]{1,0:T(8,128)(2,1)S(1)}, bf16[256,768]{1,0:T(8,128)(2,1)S(1)}, u32[]{:S(2)}, u32[]{:S(2)}) collective-permute-start(bf16[256,768]{1,0:T(8,128)(2,1)S(1)} %get-tuple-element.169), channel_id=1, source_target_pairs={{0,0},{1,4},{2,2},{3,6},{4,1},{5,5},{6,3},{7,7},{8,8},{9,12},{10,1... | collective-permute-start | bytes 1179656 | tf_op jit(solution)/shard_map/ppermute | solution.py:946
  137.7 5.2 %collective-permute-start.26 = (bf16[256,768]{1,0:T(8,128)(2,1)S(1)}, bf16[256,768]{1,0:T(8,128)(2,1)S(1)}, u32[]{:S(2)}, u32[]{:S(2)}) collective-permute-start(bf16[256,768]{1,0:T(8,128)(2,1)S(1)} %get-tuple-element.187.refs_1_.refs_2_), channel_id=1, source_target_pairs={{0,4},{4,0},{1,5},{5,1},{2,6},{6,2},{3,7},{7,3},{8,12},{12,8},{9,1... | collective-permute-start | bytes 1179656 | tf_op jit(solution)/shard_map/ppermute | solution.py:936
  137.8 30.6 %collective-permute-start.25 = (bf16[384,1536]{1,0:T(8,128)(2,1)S(1)}, bf16[384,1536]{1,0:T(8,128)(2,1)S(1)}, u32[]{:S(2)}, u32[]{:S(2)}) collective-permute-start(bf16[384,1536]{1,0:T(8,128)(2,1)S(1)} %get-tuple-element.181), channel_id=1, source_target_pairs={{0,16},{16,0},{1,17},{17,1},{2,18},{18,2},{3,19},{19,3},{4,20},{20... | collective-permute-start | bytes 3538952 | tf_op jit(solution)/shard_map/ppermute | solution.py:936
  141.5 2.5 collective-permute-start.27
  145.4 54.7 %collective-permute-start.32 = (bf16[400,2048]{1,0:T(8,128)(2,1)S(1)}, bf16[400,2048]{1,0:T(8,128)(2,1)S(1)}, u32[]{:S(2)}, u32[]{:S(2)}) collective-permute-start(bf16[400,2048]{1,0:T(8,128)(2,1)S(1)} %get-tuple-element.205), channel_id=1, source_target_pairs={{0,16},{16,0},{1,17},{17,1},{2,18},{18,2},{3,19},{19,3},{4,20},{20... | collective-permute-start | bytes 4915208 | tf_op jit(solution)/shard_map/ppermute | solution.py:936
  155.3 2.4 collective-permute-start.28
  155.7 19.8 %collective-permute-start.24 = (bf16[256,768]{1,0:T(8,128)(2,1)S(1)}, bf16[256,768]{1,0:T(8,128)(2,1)S(1)}, u32[]{:S(2)}, u32[]{:S(2)}) collective-permute-start(bf16[256,768]{1,0:T(8,128)(2,1)S(1)} %keep.2.refs_4_.refs_1_), channel_id=1, source_target_pairs={{0,2},{2,0},{1,3},{3,1},{4,6},{6,4},{5,7},{7,5},{8,10},{10,8},{9,1... | collective-permute-start | bytes 1179656 | tf_op jit(solution)/shard_map/ppermute | solution.py:936
  169.2 24.3 %collective-permute-start.33 = (bf16[192,1536]{1,0:T(8,128)(2,1)S(1)}, bf16[192,1536]{1,0:T(8,128)(2,1)S(1)}, u32[]{:S(2)}, u32[]{:S(2)}) collective-permute-start(bf16[192,1536]{1,0:T(8,128)(2,1)S(1)} %get-tuple-element.206), channel_id=1, source_target_pairs={{0,8},{8,0},{1,9},{9,1},{2,10},{10,2},{3,11},{11,3},{4,12},{12,4},... | collective-permute-start | bytes 1769480 | tf_op jit(solution)/shard_map/ppermute | solution.py:936
  169.3 34.1 %collective-permute-start.31 = (bf16[512,768]{1,0:T(8,128)(2,1)S(1)}, bf16[512,768]{1,0:T(8,128)(2,1)S(1)}, u32[]{:S(2)}, u32[]{:S(2)}) collective-permute-start(bf16[512,768]{1,0:T(8,128)(2,1)S(1)} %add.1.refs_11_), channel_id=1, source_target_pairs={{0,8},{8,0},{1,9},{9,1},{2,10},{10,2},{3,11},{11,3},{4,12},{12,4},... | collective-permute-start | bytes 2359304 | tf_op jit(solution)/shard_map/ppermute | solution.py:936
  187.3 16.2 %collective-permute-start.30 = (bf16[512,768]{1,0:T(8,128)(2,1)S(1)}, bf16[512,768]{1,0:T(8,128)(2,1)S(1)}, u32[]{:S(2)}, u32[]{:S(2)}) collective-permute-start(bf16[512,768]{1,0:T(8,128)(2,1)S(1)} %get-tuple-element.204), channel_id=1, source_target_pairs={{0,4},{4,0},{1,5},{5,1},{2,6},{6,2},{3,7},{7,3},{8,12},{12,8},{9,1... | collective-permute-start | bytes 2359304 | tf_op jit(solution)/shard_map/ppermute | solution.py:936
  188.4 19.1 %collective-permute-start.29 = (bf16[2,256,768]{2,1,0:T(8,128)(2,1)S(1)}, bf16[2,256,768]{2,1,0:T(8,128)(2,1)S(1)}, u32[]{:S(2)}, u32[]{:S(2)}) collective-permute-start(bf16[2,256,768]{2,1,0:T(8,128)(2,1)S(1)} %pair.1.refs_14_.refs_1_), channel_id=1, source_target_pairs={{0,1},{1,0},{2,3},{3,2},{4,5},{5,4},{6,7},{7,6},{8,9},{9,8},{10,11... | collective-permute-start | bytes 2359304 | tf_op jit(solution)/shard_map/ppermute | solution.py:936
  201.0 22.0 %collective-permute-start.41 = (bf16[208,2048]{1,0:T(8,128)(2,1)S(1)}, bf16[208,2048]{1,0:T(8,128)(2,1)S(1)}, u32[]{:S(2)}, u32[]{:S(2)}) collective-permute-start(bf16[208,2048]{1,0:T(8,128)(2,1)S(1)} %get-tuple-element.224), channel_id=1, source_target_pairs={{0,8},{8,0},{1,9},{9,1},{2,10},{10,2},{3,11},{11,3},{4,12},{12,4},... | collective-permute-start | bytes 2555912 | tf_op jit(solution)/shard_map/ppermute | solution.py:936
  202.2 11.6 %collective-permute-start.35 = (bf16[2,96,768]{2,1,0:T(8,128)(2,1)S(1)}, bf16[2,96,768]{2,1,0:T(8,128)(2,1)S(1)}, u32[]{:S(2)}, u32[]{:S(2)}) collective-permute-start(bf16[2,96,768]{2,1,0:T(8,128)(2,1)S(1)} %get-tuple-element.219), channel_id=1, source_target_pairs={{0,1},{1,0},{2,3},{3,2},{4,5},{5,4},{6,7},{7,6},{8,9},{9,8},{10,11... | collective-permute-start | bytes 884744 | tf_op jit(solution)/shard_map/ppermute | solution.py:936
  204.3 17.9 %collective-permute-start.34 = (bf16[256,768]{1,0:T(8,128)(2,1)S(1)}, bf16[256,768]{1,0:T(8,128)(2,1)S(1)}, u32[]{:S(2)}, u32[]{:S(2)}) collective-permute-start(bf16[256,768]{1,0:T(8,128)(2,1)S(1)} %get-tuple-element.217.refs_3_), channel_id=1, source_target_pairs={{0,1},{1,0},{2,3},{3,2},{4,5},{5,4},{6,7},{7,6},{8,9},{9,8},{10,11... | collective-permute-start | bytes 1179656 | tf_op jit(solution)/shard_map/ppermute | solution.py:936
  204.7 26.9 %collective-permute-start.38 = (bf16[208,1280]{1,0:T(8,128)(2,1)S(1)}, bf16[208,1280]{1,0:T(8,128)(2,1)S(1)}, u32[]{:S(2)}, u32[]{:S(2)}) collective-permute-start(bf16[208,1280]{1,0:T(8,128)(2,1)S(1)} %get-tuple-element.221), channel_id=1, source_target_pairs={{0,8},{8,0},{1,9},{9,1},{2,10},{10,2},{3,11},{11,3},{4,12},{12,4},... | collective-permute-start | bytes 1597448 | tf_op jit(solution)/shard_map/ppermute | solution.py:936
  207.5 26.7 %collective-permute-start.39 = (bf16[208,1280]{1,0:T(8,128)(2,1)S(1)}, bf16[208,1280]{1,0:T(8,128)(2,1)S(1)}, u32[]{:S(2)}, u32[]{:S(2)}) collective-permute-start(bf16[208,1280]{1,0:T(8,128)(2,1)S(1)} %get-tuple-element.222), channel_id=1, source_target_pairs={{0,16},{16,0},{1,17},{17,1},{2,18},{18,2},{3,19},{19,3},{4,20},{20... | collective-permute-start | bytes 1597448 | tf_op jit(solution)/shard_map/ppermute | solution.py:936
  213.8 30.0 %collective-permute-start.40 = (bf16[208,1280]{1,0:T(8,128)(2,1)S(1)}, bf16[208,1280]{1,0:T(8,128)(2,1)S(1)}, u32[]{:S(2)}, u32[]{:S(2)}) collective-permute-start(bf16[208,1280]{1,0:T(8,128)(2,1)S(1)} %get-tuple-element.223), channel_id=1, source_target_pairs={{0,24},{8,16},{16,8},{24,0},{1,25},{9,17},{17,9},{25,1},{2,26},{10... | collective-permute-start | bytes 1597448 | tf_op jit(solution)/shard_map/ppermute | solution.py:994
  222.9 22.1 %collective-permute-start.37 = (bf16[256,768]{1,0:T(8,128)(2,1)S(1)}, bf16[256,768]{1,0:T(8,128)(2,1)S(1)}, u32[]{:S(2)}, u32[]{:S(2)}) collective-permute-start(bf16[256,768]{1,0:T(8,128)(2,1)S(1)} %final.1.refs_3_.refs_1_), channel_id=1, source_target_pairs={{0,2},{2,0},{1,3},{3,1},{4,6},{6,4},{5,7},{7,5},{8,10},{10,8},{9,1... | collective-permute-start | bytes 1179656 | tf_op jit(solution)/shard_map/ppermute | solution.py:936
  223.9 24.2 %collective-permute-start.44 = (bf16[2,112,1024]{2,1,0:T(8,128)(2,1)S(1)}, bf16[2,112,1024]{2,1,0:T(8,128)(2,1)S(1)}, u32[]{:S(2)}, u32[]{:S(2)}) collective-permute-start(bf16[2,112,1024]{2,1,0:T(8,128)(2,1)S(1)} %get-tuple-element.228), channel_id=1, source_target_pairs={{0,1},{1,0},{2,3},{3,2},{4,5},{5,4},{6,7},{7,6},{8,9},{9,8},{10,11... | collective-permute-start | bytes 1376264 | tf_op jit(solution)/shard_map/ppermute | solution.py:936
  231.6 43.4 %collective-permute-start.36 = (bf16[256,768]{1,0:T(8,128)(2,1)S(1)}, bf16[256,768]{1,0:T(8,128)(2,1)S(1)}, u32[]{:S(2)}, u32[]{:S(2)}) collective-permute-start(bf16[256,768]{1,0:T(8,128)(2,1)S(1)} %final.1.refs_3_.refs_1_), channel_id=1, source_target_pairs={{0,1},{1,0},{2,3},{3,2},{4,5},{5,4},{6,7},{7,6},{8,9},{9,8},{10,11... | collective-permute-start | bytes 1179656 | tf_op jit(solution)/shard_map/ppermute | solution.py:936
  245.5 29.6 %collective-permute-start.42 = (bf16[256,768]{1,0:T(8,128)(2,1)S(1)}, bf16[256,768]{1,0:T(8,128)(2,1)S(1)}, u32[]{:S(2)}, u32[]{:S(2)}) collective-permute-start(bf16[256,768]{1,0:T(8,128)(2,1)S(1)} %keep.3.refs_3_), channel_id=1, source_target_pairs={{0,1},{1,0},{2,3},{3,2},{4,5},{5,4},{6,7},{7,6},{8,9},{9,8},{10,11... | collective-permute-start | bytes 1179656 | tf_op jit(solution)/shard_map/ppermute | solution.py:936
  247.3 23.0 %collective-permute-start.43 = (bf16[2,112,640]{2,1,0:T(8,128)(2,1)S(1)}, bf16[2,112,640]{2,1,0:T(8,128)(2,1)S(1)}, u32[]{:S(2)}, u32[]{:S(2)}) collective-permute-start(bf16[2,112,640]{2,1,0:T(8,128)(2,1)S(1)} %get-tuple-element.227), channel_id=1, source_target_pairs={{0,1},{1,0},{2,3},{3,2},{4,5},{5,4},{6,7},{7,6},{8,9},{9,8},{10,11... | collective-permute-start | bytes 860168 | tf_op jit(solution)/shard_map/ppermute | solution.py:936
  247.4 18.9 %collective-permute-start.48 = (bf16[96,768]{1,0:T(8,128)(2,1)S(1)}, bf16[96,768]{1,0:T(8,128)(2,1)S(1)}, u32[]{:S(2)}, u32[]{:S(2)}) collective-permute-start(bf16[96,768]{1,0:T(8,128)(2,1)S(1)} %get-tuple-element.232), channel_id=1, source_target_pairs={{0,4},{1,5},{2,0},{3,1},{4,6},{5,7},{6,2},{7,3},{8,12},{9,13},{10,... | collective-permute-start | bytes 442376 | tf_op jit(solution)/shard_map/ppermute | solution.py:946
  248.9 32.7 %collective-permute-start.50 = (bf16[112,1024]{1,0:T(8,128)(2,1)S(1)}, bf16[112,1024]{1,0:T(8,128)(2,1)S(1)}, u32[]{:S(2)}, u32[]{:S(2)}) collective-permute-start(bf16[112,1024]{1,0:T(8,128)(2,1)S(1)} %get-tuple-element.233), channel_id=1, source_target_pairs={{0,4},{1,5},{2,0},{3,1},{4,6},{5,7},{6,2},{7,3},{8,12},{9,13},{10,... | collective-permute-start | bytes 688136 | tf_op jit(solution)/shard_map/ppermute | solution.py:946
  266.3 15.3 %collective-permute-start.49 = (bf16[112,1024]{1,0:T(8,128)(2,1)S(1)}, bf16[112,1024]{1,0:T(8,128)(2,1)S(1)}, u32[]{:S(2)}, u32[]{:S(2)}) collective-permute-start(bf16[112,1024]{1,0:T(8,128)(2,1)S(1)} %get-tuple-element.229.refs_3_), channel_id=1, source_target_pairs={{0,0},{1,1},{2,4},{3,5},{4,2},{5,3},{6,6},{7,7},{8,8},{9,9},{10,12... | collective-permute-start | bytes 688136 | tf_op jit(solution)/shard_map/ppermute | solution.py:946
  270.3 11.3 %collective-permute-start.47 = (bf16[96,768]{1,0:T(8,128)(2,1)S(1)}, bf16[96,768]{1,0:T(8,128)(2,1)S(1)}, u32[]{:S(2)}, u32[]{:S(2)}) collective-permute-start(bf16[96,768]{1,0:T(8,128)(2,1)S(1)} %get-tuple-element.220.refs_3_), channel_id=1, source_target_pairs={{0,0},{1,1},{2,4},{3,5},{4,2},{5,3},{6,6},{7,7},{8,8},{9,9},{10,12... | collective-permute-start | bytes 442376 | tf_op jit(solution)/shard_map/ppermute | solution.py:946
  275.1 9.5 %collective-permute-start.46 = (bf16[112,640]{1,0:T(8,128)(2,1)S(1)}, bf16[112,640]{1,0:T(8,128)(2,1)S(1)}, u32[]{:S(2)}, u32[]{:S(2)}) collective-permute-start(bf16[112,640]{1,0:T(8,128)(2,1)S(1)} %get-tuple-element.231), channel_id=1, source_target_pairs={{0,4},{1,5},{2,0},{3,1},{4,6},{5,7},{6,2},{7,3},{8,12},{9,13},{10,... | collective-permute-start | bytes 430088 | tf_op jit(solution)/shard_map/ppermute | solution.py:946
  275.1 11.1 %collective-permute-start.45 = (bf16[112,640]{1,0:T(8,128)(2,1)S(1)}, bf16[112,640]{1,0:T(8,128)(2,1)S(1)}, u32[]{:S(2)}, u32[]{:S(2)}) collective-permute-start(bf16[112,640]{1,0:T(8,128)(2,1)S(1)} %get-tuple-element.230.refs_5_), channel_id=1, source_target_pairs={{0,0},{1,1},{2,4},{3,5},{4,2},{5,3},{6,6},{7,7},{8,8},{9,9},{10,12... | collective-permute-start | bytes 430088 | tf_op jit(solution)/shard_map/ppermute | solution.py:946
  (44 other events, 344.7 us)
Sparse Core Ops, SparseCore 0:
  47.6 52.3 all-gather.2

commit v5 on v4

--- a/solution.py
+++ b/solution.py
@@ -1205,7 +1205,7 @@
     sent = flip(sent, "tl")
     layer_output = call(
         output_kernel, "output", spot, [out_pair, out_got], [((2, 2, half, width), LOW)],
-        far=(False, True),
+
     )[0].reshape(2, rows, width)
     n = quarter
 
@@ -1280,7 +1280,7 @@
         sums_a = lax.dynamic_index_in_dim(both, l, 0, keepdims=True)
     grad_inputs = call(
         place_kernel, "place", spot, [final, beside, across, beyond],
-        [((2, 2, half, width), LOW)], far=(False, True),
+        [((2, 2, half, width), LOW)],
     )[0].reshape(2, rows, width)
     if square:
         grad_down, grad_up, grad_output, *shared = call(

time: 296 us -> 296 us (level)
  no operation moved by 1% of the time
where the time goes in v5:
time: 296 us; the launch traced here: 295 us
  waiting for transfers between devices  104 us (35%)
  Pallas kernels  103 us (35%)
  starting transfers between devices  57.9 us (20%)
  local copies, waits for them, and re-layouts  15.1 us (5%)
  between operations  14.8 us (5%)
    pallas_call x44, Pallas kernels, __call__(): pl.pallas_call(run, out_shape=tuple((pltpu.HBM(shape, kind) if out else j...  103 us
    ppermute x37, waiting for transfers between devices, flip(): return lax.ppermute(value, axis, FLIP)  66.4 us
    ppermute x37, starting transfers between devices, flip(): return lax.ppermute(value, axis, FLIP)  30.6 us
    ppermute x11, starting transfers between devices, move(): return lax.ppermute(value, ('cc', 'th', 'tl'), pairs)  24.9 us
    ppermute x11, waiting for transfers between devices, move(): return lax.ppermute(value, ('cc', 'th', 'tl'), pairs)  24.6 us
    unnamed x80, local copies, waits for them, and re-layouts  15.1 us
    ppermute x3, waiting for transfers between devices, exchange(): lax.ppermute(far, plane, [(i, i ^ 3) for i in range(4)])  9.7 us
  transfers between devices with their start and end apart: 52, of which 23 were waited for; matrix products, arithmetic and copies ran while one was open for 0% of the time, Pallas kernels for 30%

profile of v5, /device:TPU:1, one launch (start us, length us, event | category | flops | bytes accessed | tf_op | source)
XLA Modules:
  0.0 295.2 jit_solution(16754172795077910634)
XLA Ops:
  9.4 1.8 pack.1
  11.3 2.0 pick.1
  13.4 2.7 collective-permute-start.5
  17.9 4.1 %collective-permute-start.1 = (bf16[112,640]{1,0:T(8,128)(2,1)S(1)}, bf16[112,640]{1,0:T(8,128)(2,1)S(1)}, u32[]{:S(2)}, u32[]{:S(2)}) collective-permute-start(bf16[112,640]{1,0:T(8,128)(2,1)S(1)} %get-tuple-element.133.refs_3_), channel_id=1, source_target_pairs={{0,0},{1,1},{2,4},{3,5},{4,2},{5,3},{6,6},{7,7},{8,8},{9,9},{10,12... | collective-permute-start | bytes 430088 | tf_op jit(solution)/shard_map/ppermute | solution.py:946
  26.7 1.8 settle.1
  29.5 1.9 collective-permute-start.4
  32.2 5.0 %collective-permute-start.6 = (bf16[96,1024]{1,0:T(8,128)(2,1)S(1)}, bf16[96,1024]{1,0:T(8,128)(2,1)S(1)}, u32[]{:S(2)}, u32[]{:S(2)}) collective-permute-start(bf16[96,1024]{1,0:T(8,128)(2,1)S(1)} %get-tuple-element.140.refs_8_), channel_id=1, source_target_pairs={{0,0},{1,1},{2,4},{3,5},{4,2},{5,3},{6,6},{7,7},{8,8},{9,9},{10,12... | collective-permute-start | bytes 589832 | tf_op jit(solution)/shard_map/ppermute | solution.py:946
  37.2 1.8 collective-permute-done.7.refs_5_
  39.0 3.9 %collective-permute-done.6.refs_4_ = bf16[96,1024]{1,0:T(8,128)(2,1)S(1)} collective-permute-done((bf16[96,1024]{1,0:T(8,128)(2,1)S(1)}, bf16[96,1024]{1,0:T(8,128)(2,1)S(1)}, u32[]{:S(2)}, u32[]{:S(2)}) %collective-permute-start.6) | collective-permute-done | bytes 196640 | tf_op jit(solution)/shard_map/ppermute | solution.py:946
  42.9 1.6 spread.1
  51.9 11.9 %collective-permute-done.12.refs_2_ = bf16[2,96,1024]{2,1,0:T(8,128)(2,1)S(1)} collective-permute-done((bf16[2,96,1024]{2,1,0:T(8,128)(2,1)}, bf16[2,96,1024]{2,1,0:T(8,128)(2,1)S(1)}, u32[]{:S(2)}, u32[]{:S(2)}) %collective-permute-start.12) | collective-permute-done | bytes 393248 | tf_op jit(solution)/shard_map/ppermute | solution.py:936
  63.7 8.8 %collective-permute-done.10.refs_5_.refs_3_ = bf16[2,2,96,640]{3,2,1,0:T(8,128)(2,1)S(1)} collective-permute-done((bf16[2,2,96,640]{3,2,1,0:T(8,128)(2,1)}, bf16[2,2,96,640]{3,2,1,0:T(8,128)(2,1)S(1)}, u32[]{:S(2)}, u32[]{:S(2)}) %collective-permute-start.10) | collective-permute-done | bytes 491552 | tf_op jit(solution)/shard_map/ppermute | solution.py:936
  76.9 2.0 join.1
  78.9 7.1 %project.1 = (bf16[2048,768]{1,0:T(8,128)(2,1)S(1)}, bf16[512,512]{1,0:T(8,128)(2,1)S(1)}, bf16[512,768]{1,0:T(8,128)(2,1)}, bf16[512,768]{1,0:T(8,128)(2,1)}, b...) custom-call(s32[6]{0:T(128)S(1)} %stack.24.refs_0_, bf16[768,768]{1,0:T(8,128)(2,1)} %bitcast.23, ...), custom_call_target="tpu_custom_call" | custom-call | flops 1 | bytes 1 | tf_op jit(solution)/shard_map/project/pallas_call | solution.py:288
  86.1 10.2 %attend.1 = (bf16[512,512]{1,0:T(8,128)(2,1)S(1)}, f32[8,512]{1,0:T(8,128)S(1)}) custom-call(s32[6]{0:T(128)S(1)} %stack.24.refs_0_, s32[2,2048]{1,0:T(2,128)S(1)} %copy-done.18, bf16[512,512]{1,0:T(8,128)(2,1)S(1)} %get-tuple-element.152.refs_2_.refs_6_, bf16[2048,768]{1,0:T(8,128)(2,1)S(1)} %get-tuple-element.153.refs_3_, ...), custom_call_target="tpu_custom_call" | custom-call | flops 1 | bytes 1 | tf_op jit(solution)/shard_map/attend/pallas_call | solution.py:288
  96.3 3.7 %all-gather.3.cloned.1.call-done = bf16[16,96,768]{2,1,0:T(8,128)(2,1)} async-done(((bf16[4,96,768]{2,1,0:T(8,128)(2,1)}), bf16[16,96,768]{2,1,0:T(8,128)(2,1)}) %all-gather.3.cloned.1.call-update) | async-done | bytes 2359312 | tf_op jit(solution)/shard_map/all_gather | solution.py:1057
  100.0 1.7 copy-done
  102.8 8.7 %collective-permute-done.16.refs_3_ = bf16[2,2,96,1024]{3,2,1,0:T(8,128)(2,1)} collective-permute-done((bf16[2,2,96,1024]{3,2,1,0:T(8,128)(2,1)S(1)}, bf16[2,2,96,1024]{3,2,1,0:T(8,128)(2,1)}, u32[]{:S(2)}, u32[]{:S(2)}) %collective-permute-start.16) | collective-permute-done | bytes 786464 | tf_op jit(solution)/shard_map/ppermute | solution.py:936
  111.5 2.5 branch.1
  118.7 2.7 up.1
  121.4 2.1 down.1
  128.5 3.3 %units.1 = (bf16[512,1536]{1,0:T(8,128)(2,1)S(1)}, f32[256,768]{1,0:T(8,128)S(1)}, bf16[256,768]{1,0:T(8,128)(2,1)S(1)}, f32[8,1536]{1,0:T(8,128)S(1)}) custom-call(s32[6]{0:T(128)S(1)} %stack.24.refs_0_, bf16[256,768]{1,0:T(8,128)(2,1)S(1)} %get-tuple-element.170.refs_1_, bf16[256,768]{1,0:T(8,128)(2,1)S(1)} %collective-permute-done.22.refs_2_, ...), custom_call_target="tpu_custom_call" | custom-call | flops 1 | bytes 1 | tf_op jit(solution)/shard_map/units/pallas_call | solution.py:288
  132.2 2.2 collective-permute-start.21
  134.4 2.1 grad_d.1
  139.0 2.0 grad_u.1.refs_3_.refs_1_
  145.8 9.5 %attend_cd.1 = (f32[384,512]{1,0:T(8,128)S(1)}, bf16[1024,768]{1,0:T(8,128)(2,1)S(1)}, f32[512,768]{1,0:T(8,128)S(1)}, bf16[512,768]{1,0:T(8,128)(2,1)S(1)}, f32...) custom-call(s32[6]{0:T(128)S(1)} %stack.24.refs_0_, ...), custom_call_target="tpu_custom_call" | custom-call | flops 1 | bytes 1 | tf_op jit(solution)/shard_map/attend_cd/pallas_call | solution.py:288
  158.4 10.0 %attend_a.1 = (f32[384,512]{1,0:T(8,128)S(1)}, bf16[512,768]{1,0:T(8,128)(2,1)S(1)}, f32[512,768]{1,0:T(8,128)S(1)}, f32[8,768]{1,0:T(8,128)S(1)}) custom-call(s32[6]{0:T(128)S(1)} %stack.24.refs_0_, s32[2,2048]{1,0:T(2,128)S(1)} %copy-done.19, bf16[512,768]{1,0:T(8,128)(2,1)} %get-tuple-element.182.refs_2_, ...), custom_call_target="tpu_custom_call" | custom-call | flops 1 | bytes 1 | tf_op jit(solution)/shard_map/attend_a/pallas_call | solution.py:288
  169.2 1.6 collective-permute-start.33
  170.9 4.6 %collective-permute-done.24.refs_2_ = bf16[256,768]{1,0:T(8,128)(2,1)S(1)} collective-permute-done((bf16[256,768]{1,0:T(8,128)(2,1)S(1)}, bf16[256,768]{1,0:T(8,128)(2,1)S(1)}, u32[]{:S(2)}, u32[]{:S(2)}) %collective-permute-start.24) | collective-permute-done | bytes 393248 | tf_op jit(solution)/shard_map/ppermute | solution.py:936
  176.1 11.1 %attend_b.1 = (bf16[512,512]{1,0:T(8,128)(2,1)S(1)}, bf16[512,768]{1,0:T(8,128)(2,1)S(1)}, f32[512,768]{1,0:T(8,128)S(1)}, bf16[512,768]{1,0:T(8,128)(2,1)S(1)},...) custom-call(s32[6]{0:T(128)S(1)} %stack.24.refs_0_, s32[2,2048]{1,0:T(2,128)S(1)} %copy-done.19, ...), custom_call_target="tpu_custom_call" | custom-call | flops 1 | bytes 1 | tf_op jit(solution)/shard_map/attend_b/pallas_call | solution.py:288
  188.4 5.2 %grad_qkv.1 = (bf16[208,1280]{1,0:T(8,128)(2,1)S(1)}, bf16[208,1280]{1,0:T(8,128)(2,1)S(1)}, bf16[208,1280]{1,0:T(8,128)(2,1)S(1)}, bf16[208,1280]{1,0:T(8,128)(2,1)S(1)}) custom-call(s32[6]{0:T(128)S(1)} %stack.24.refs_0_, bf16[512,768]{1,0:T(8,128)(2,1)S(1)} %get-tuple-element.134.refs_1_.refs_3_, ...), custom_call_target="tpu_custom_call" | custom-call | flops 1 | bytes 1 | tf_op jit(solution)/shard_map/grad_qkv/pallas_call | solution.py:288
  194.6 5.4 %collective-permute-done.32.refs_2_ = bf16[400,2048]{1,0:T(8,128)(2,1)S(1)} collective-permute-done((bf16[400,2048]{1,0:T(8,128)(2,1)S(1)}, bf16[400,2048]{1,0:T(8,128)(2,1)S(1)}, u32[]{:S(2)}, u32[]{:S(2)}) %collective-permute-start.32) | collective-permute-done | bytes 1638432 | tf_op jit(solution)/shard_map/ppermute | solution.py:936
  205.7 1.8 collective-permute-done.29.refs_2_
  207.5 6.3 %collective-permute-done.35.refs_2_ = bf16[2,96,768]{2,1,0:T(8,128)(2,1)S(1)} collective-permute-done((bf16[2,96,768]{2,1,0:T(8,128)(2,1)S(1)}, bf16[2,96,768]{2,1,0:T(8,128)(2,1)S(1)}, u32[]{:S(2)}, u32[]{:S(2)}) %collective-permute-start.35) | collective-permute-done | bytes 294944 | tf_op jit(solution)/shard_map/ppermute | solution.py:936
  213.8 1.8 output.1.refs_3_
  217.7 4.6 %collective-permute-done.34.refs_2_ = bf16[256,768]{1,0:T(8,128)(2,1)S(1)} collective-permute-done((bf16[256,768]{1,0:T(8,128)(2,1)S(1)}, bf16[256,768]{1,0:T(8,128)(2,1)S(1)}, u32[]{:S(2)}, u32[]{:S(2)}) %collective-permute-start.34) | collective-permute-done | bytes 393248 | tf_op jit(solution)/shard_map/ppermute | solution.py:936
  226.0 5.6 %collective-permute-done.38.refs_2_ = bf16[208,1280]{1,0:T(8,128)(2,1)S(1)} collective-permute-done((bf16[208,1280]{1,0:T(8,128)(2,1)S(1)}, bf16[208,1280]{1,0:T(8,128)(2,1)S(1)}, u32[]{:S(2)}, u32[]{:S(2)}) %collective-permute-start.38) | collective-permute-done | bytes 532512 | tf_op jit(solution)/shard_map/ppermute | solution.py:936
  231.6 2.6 collective-permute-start.36
  234.2 9.7 %collective-permute-done.40.refs_4_ = bf16[208,1280]{1,0:T(8,128)(2,1)S(1)} collective-permute-done((bf16[208,1280]{1,0:T(8,128)(2,1)S(1)}, bf16[208,1280]{1,0:T(8,128)(2,1)S(1)}, u32[]{:S(2)}, u32[]{:S(2)}) %collective-permute-start.40) | collective-permute-done | bytes 532512 | tf_op jit(solution)/shard_map/ppermute | solution.py:994
  245.5 1.8 collective-permute-start.42
  248.9 2.6 collective-permute-start.50
  251.5 15.6 %collective-permute-done.48.refs_2_ = bf16[96,768]{1,0:T(8,128)(2,1)S(1)} collective-permute-done((bf16[96,768]{1,0:T(8,128)(2,1)S(1)}, bf16[96,768]{1,0:T(8,128)(2,1)S(1)}, u32[]{:S(2)}, u32[]{:S(2)}) %collective-permute-start.48) | collective-permute-done | bytes 147488 | tf_op jit(solution)/shard_map/ppermute | solution.py:946
  267.1 1.9 collective-permute-start.49
  269.0 2.2 collective-permute-done.43.refs_2_
  271.2 3.2 %collective-permute-start.47 = (bf16[96,768]{1,0:T(8,128)(2,1)S(1)}, bf16[96,768]{1,0:T(8,128)(2,1)S(1)}, u32[]{:S(2)}, u32[]{:S(2)}) collective-permute-start(bf16[96,768]{1,0:T(8,128)(2,1)S(1)} %get-tuple-element.220.refs_3_), channel_id=1, source_target_pairs={{0,0},{1,1},{2,4},{3,5},{4,2},{5,3},{6,6},{7,7},{8,8},{9,9},{10,12... | collective-permute-start | bytes 442376 | tf_op jit(solution)/shard_map/ppermute | solution.py:946
  275.2 3.7 %collective-permute-start.45 = (bf16[112,640]{1,0:T(8,128)(2,1)S(1)}, bf16[112,640]{1,0:T(8,128)(2,1)S(1)}, u32[]{:S(2)}, u32[]{:S(2)}) collective-permute-start(bf16[112,640]{1,0:T(8,128)(2,1)S(1)} %get-tuple-element.230.refs_5_), channel_id=1, source_target_pairs={{0,0},{1,1},{2,4},{3,5},{4,2},{5,3},{6,6},{7,7},{8,8},{9,9},{10,12... | collective-permute-start | bytes 430088 | tf_op jit(solution)/shard_map/ppermute | solution.py:946
  278.9 1.8 place.1.refs_5_
  284.7 1.6 collective-permute-done.45.refs_1_
  (182 shorter events, 68.7 us)
Async XLA Ops:
  7.2 92.8 %all-gather.3.cloned.1.call-start = ((), (), s32[]{:S(2)}) async-start(), calls=%async_computation | async-start | bytes 2949120 | tf_op jit(solution)/shard_map/all_gather | solution.py:1057
  13.2 13.5 %collective-permute-start = (bf16[768,768]{1,0:T(8,128)(2,1)S(1)}, bf16[768,768]{1,0:T(8,128)(2,1)S(1)}, u32[]{:S(2)}, u32[]{:S(2)}) collective-permute-start(bf16[768,768]{1,0:T(8,128)(2,1)S(1)} %get-tuple-element.135), channel_id=1, source_target_pairs={{0,4},{4,0},{1,5},{5,1},{2,6},{6,2},{3,7},{7,3},{8,12},{12,8},{9,1... | collective-permute-start | bytes 3538952 | tf_op jit(solution)/shard_map/ppermute | solution.py:936
  13.4 23.8 %collective-permute-start.5 = (bf16[512,768]{1,0:T(8,128)(2,1)S(1)}, bf16[512,768]{1,0:T(8,128)(2,1)S(1)}, u32[]{:S(2)}, u32[]{:S(2)}) collective-permute-start(bf16[512,768]{1,0:T(8,128)(2,1)S(1)} %get-tuple-element.134.refs_1_.refs_3_), channel_id=1, source_target_pairs={{0,8},{8,0},{1,9},{9,1},{2,10},{10,2},{3,11},{11,3},{4,12},{12,4},... | collective-permute-start | bytes 2359304 | tf_op jit(solution)/shard_map/ppermute | solution.py:936
  16.0 10.7 %collective-permute-start.3 = (bf16[96,768]{1,0:T(8,128)(2,1)S(1)}, bf16[96,768]{1,0:T(8,128)(2,1)S(1)}, u32[]{:S(2)}, u32[]{:S(2)}) collective-permute-start(bf16[96,768]{1,0:T(8,128)(2,1)S(1)} %get-tuple-element.137.refs_6_), channel_id=1, source_target_pairs={{0,16},{16,0},{1,17},{17,1},{2,18},{18,2},{3,19},{19,3},{4,20},{20... | collective-permute-start | bytes 442376 | tf_op jit(solution)/shard_map/ppermute | solution.py:936
  17.3 8.8 %collective-permute-start.2 = (bf16[112,640]{1,0:T(8,128)(2,1)S(1)}, bf16[112,640]{1,0:T(8,128)(2,1)S(1)}, u32[]{:S(2)}, u32[]{:S(2)}) collective-permute-start(bf16[112,640]{1,0:T(8,128)(2,1)S(1)} %get-tuple-element.133.refs_3_), channel_id=1, source_target_pairs={{0,2},{1,3},{2,6},{3,7},{4,0},{5,1},{6,4},{7,5},{8,10},{9,11},{10,... | collective-permute-start | bytes 430088 | tf_op jit(solution)/shard_map/ppermute | solution.py:946
  17.9 8.8 %collective-permute-start.1 = (bf16[112,640]{1,0:T(8,128)(2,1)S(1)}, bf16[112,640]{1,0:T(8,128)(2,1)S(1)}, u32[]{:S(2)}, u32[]{:S(2)}) collective-permute-start(bf16[112,640]{1,0:T(8,128)(2,1)S(1)} %get-tuple-element.133.refs_3_), channel_id=1, source_target_pairs={{0,0},{1,1},{2,4},{3,5},{4,2},{5,3},{6,6},{7,7},{8,8},{9,9},{10,12... | collective-permute-start | bytes 430088 | tf_op jit(solution)/shard_map/ppermute | solution.py:946
  29.3 13.6 %collective-permute-start.8 = (bf16[2,96,768]{2,1,0:T(8,128)(2,1)S(1)}, bf16[2,96,768]{2,1,0:T(8,128)(2,1)S(1)}, u32[]{:S(2)}, u32[]{:S(2)}) collective-permute-start(bf16[2,96,768]{2,1,0:T(8,128)(2,1)S(1)} %get-tuple-element.141.refs_6_), channel_id=1, source_target_pairs={{0,8},{8,0},{1,9},{9,1},{2,10},{10,2},{3,11},{11,3},{4,12},{12,4},... | collective-permute-start | bytes 884744 | tf_op jit(solution)/shard_map/ppermute | solution.py:936
  29.5 13.4 %collective-permute-start.4 = (bf16[2,112,640]{2,1,0:T(8,128)(2,1)S(1)}, bf16[2,112,640]{2,1,0:T(8,128)(2,1)S(1)}, u32[]{:S(2)}, u32[]{:S(2)}) collective-permute-start(bf16[2,112,640]{2,1,0:T(8,128)(2,1)S(1)} %get-tuple-element.139.refs_1_), channel_id=1, source_target_pairs={{0,1},{1,0},{2,3},{3,2},{4,5},{5,4},{6,7},{7,6},{8,9},{9,8},{10,11... | collective-permute-start | bytes 860168 | tf_op jit(solution)/shard_map/ppermute | solution.py:936
  31.4 7.6 %collective-permute-start.7 = (bf16[96,1024]{1,0:T(8,128)(2,1)S(1)}, bf16[96,1024]{1,0:T(8,128)(2,1)S(1)}, u32[]{:S(2)}, u32[]{:S(2)}) collective-permute-start(bf16[96,1024]{1,0:T(8,128)(2,1)S(1)} %get-tuple-element.140.refs_8_), channel_id=1, source_target_pairs={{0,2},{1,3},{2,6},{3,7},{4,0},{5,1},{6,4},{7,5},{8,10},{9,11},{10,... | collective-permute-start | bytes 589832 | tf_op jit(solution)/shard_map/ppermute | solution.py:946
  32.2 10.7 %collective-permute-start.6 = (bf16[96,1024]{1,0:T(8,128)(2,1)S(1)}, bf16[96,1024]{1,0:T(8,128)(2,1)S(1)}, u32[]{:S(2)}, u32[]{:S(2)}) collective-permute-start(bf16[96,1024]{1,0:T(8,128)(2,1)S(1)} %get-tuple-element.140.refs_8_), channel_id=1, source_target_pairs={{0,0},{1,1},{2,4},{3,5},{4,2},{5,3},{6,6},{7,7},{8,8},{9,9},{10,12... | collective-permute-start | bytes 589832 | tf_op jit(solution)/shard_map/ppermute | solution.py:946
  47.5 16.2 %collective-permute-start.11 = (bf16[2,2,96,640]{3,2,1,0:T(8,128)(2,1)}, bf16[2,2,96,640]{3,2,1,0:T(8,128)(2,1)S(1)}, u32[]{:S(2)}, u32[]{:S(2)}) collective-permute-start(bf16[2,2,96,640]{3,2,1,0:T(8,128)(2,1)} %copy-done.15), channel_id=1, source_target_pairs={{0,24},{8,16},{16,8},{24,0},{1,25},{9,17},{17,9},{25,1},{2,26},{10... | collective-permute-start | bytes 1474568 | tf_op jit(solution)/shard_map/ppermute | solution.py:994
  48.7 23.8 %collective-permute-start.10 = (bf16[2,2,96,640]{3,2,1,0:T(8,128)(2,1)}, bf16[2,2,96,640]{3,2,1,0:T(8,128)(2,1)S(1)}, u32[]{:S(2)}, u32[]{:S(2)}) collective-permute-start(bf16[2,2,96,640]{3,2,1,0:T(8,128)(2,1)} %copy-done.15), channel_id=1, source_target_pairs={{0,16},{16,0},{1,17},{17,1},{2,18},{18,2},{3,19},{19,3},{4,20},{20... | collective-permute-start | bytes 1474568 | tf_op jit(solution)/shard_map/ppermute | solution.py:936
  50.0 22.5 %collective-permute-start.9 = (bf16[2,2,96,640]{3,2,1,0:T(8,128)(2,1)}, bf16[2,2,96,640]{3,2,1,0:T(8,128)(2,1)S(1)}, u32[]{:S(2)}, u32[]{:S(2)}) collective-permute-start(bf16[2,2,96,640]{3,2,1,0:T(8,128)(2,1)} %copy-done.15), channel_id=1, source_target_pairs={{0,8},{8,0},{1,9},{9,1},{2,10},{10,2},{3,11},{11,3},{4,12},{12,4},... | collective-permute-start | bytes 1474568 | tf_op jit(solution)/shard_map/ppermute | solution.py:936
  50.3 13.5 %collective-permute-start.12 = (bf16[2,96,1024]{2,1,0:T(8,128)(2,1)}, bf16[2,96,1024]{2,1,0:T(8,128)(2,1)S(1)}, u32[]{:S(2)}, u32[]{:S(2)}) collective-permute-start(bf16[2,96,1024]{2,1,0:T(8,128)(2,1)} %copy-done.22), channel_id=1, source_target_pairs={{0,1},{1,0},{2,3},{3,2},{4,5},{5,4},{6,7},{7,6},{8,9},{9,8},{10,11... | collective-permute-start | bytes 1179656 | tf_op jit(solution)/shard_map/ppermute | solution.py:936
  51.9 27.0 %collective-permute-start.13 = (bf16[512,768]{1,0:T(8,128)(2,1)}, bf16[512,768]{1,0:T(8,128)(2,1)S(1)}, u32[]{:S(2)}, u32[]{:S(2)}) collective-permute-start(bf16[512,768]{1,0:T(8,128)(2,1)} %get-tuple-element.148.refs_5_.refs_3_), channel_id=1, source_target_pairs={{0,4},{4,0},{1,5},{5,1},{2,6},{6,2},{3,7},{7,3},{8,12},{12,8},{9,1... | collective-permute-start | bytes 2359304 | tf_op jit(solution)/shard_map/ppermute | solution.py:936
  74.1 28.7 %collective-permute-start.17 = (bf16[2,2,96,1024]{3,2,1,0:T(8,128)(2,1)S(1)}, bf16[2,2,96,1024]{3,2,1,0:T(8,128)(2,1)}, u32[]{:S(2)}, u32[]{:S(2)}) collective-permute-start(bf16[2,2,96,1024]{3,2,1,0:T(8,128)(2,1)S(1)} %rows.1.refs_5_.refs_1_), channel_id=1, source_target_pairs={{0,24},{8,16},{16,8},{24,0},{1,25},{9,17},{17,9},{25,1},{2,26},{10... | collective-permute-start | bytes 2359304 | tf_op jit(solution)/shard_map/ppermute | solution.py:994
  75.4 36.2 %collective-permute-start.16 = (bf16[2,2,96,1024]{3,2,1,0:T(8,128)(2,1)S(1)}, bf16[2,2,96,1024]{3,2,1,0:T(8,128)(2,1)}, u32[]{:S(2)}, u32[]{:S(2)}) collective-permute-start(bf16[2,2,96,1024]{3,2,1,0:T(8,128)(2,1)S(1)} %rows.1.refs_5_.refs_1_), channel_id=1, source_target_pairs={{0,16},{16,0},{1,17},{17,1},{2,18},{18,2},{3,19},{19,3},{4,20},{20... | collective-permute-start | bytes 2359304 | tf_op jit(solution)/shard_map/ppermute | solution.py:936
  75.5 36.0 %collective-permute-start.15 = (bf16[2,2,96,1024]{3,2,1,0:T(8,128)(2,1)S(1)}, bf16[2,2,96,1024]{3,2,1,0:T(8,128)(2,1)}, u32[]{:S(2)}, u32[]{:S(2)}) collective-permute-start(bf16[2,2,96,1024]{3,2,1,0:T(8,128)(2,1)S(1)} %rows.1.refs_5_.refs_1_), channel_id=1, source_target_pairs={{0,8},{8,0},{1,9},{9,1},{2,10},{10,2},{3,11},{11,3},{4,12},{12,4},... | collective-permute-start | bytes 2359304 | tf_op jit(solution)/shard_map/ppermute | solution.py:936
  102.3 19.1 %collective-permute-start.14 = (bf16[2,4,96,768]{3,2,1,0:T(8,128)(2,1)S(1)}, bf16[2,4,96,768]{3,2,1,0:T(8,128)(2,1)S(1)}, u32[]{:S(2)}, u32[]{:S(2)}) collective-permute-start(bf16[2,4,96,768]{3,2,1,0:T(8,128)(2,1)S(1)} %give_d.1.refs_6_), channel_id=1, source_target_pairs={{0,4},{4,0},{1,5},{5,1},{2,6},{6,2},{3,7},{7,3},{8,12},{12,8},{9,1... | collective-permute-start | bytes 3538952 | tf_op jit(solution)/shard_map/ppermute | solution.py:936
  131.8 4.7 %collective-permute-start.23 = (bf16[256,768]{1,0:T(8,128)(2,1)S(1)}, bf16[256,768]{1,0:T(8,128)(2,1)S(1)}, u32[]{:S(2)}, u32[]{:S(2)}) collective-permute-start(bf16[256,768]{1,0:T(8,128)(2,1)S(1)} %get-tuple-element.175), channel_id=1, source_target_pairs={{0,4},{4,0},{1,5},{5,1},{2,6},{6,2},{3,7},{7,3},{8,12},{12,8},{9,1... | collective-permute-start | bytes 1179656 | tf_op jit(solution)/shard_map/ppermute | solution.py:936
  132.2 10.1 %collective-permute-start.21 = (bf16[256,768]{1,0:T(8,128)(2,1)S(1)}, bf16[256,768]{1,0:T(8,128)(2,1)S(1)}, u32[]{:S(2)}, u32[]{:S(2)}) collective-permute-start(bf16[256,768]{1,0:T(8,128)(2,1)S(1)} %get-tuple-element.169), channel_id=1, source_target_pairs={{0,0},{1,4},{2,2},{3,6},{4,1},{5,5},{6,3},{7,7},{8,8},{9,12},{10,1... | collective-permute-start | bytes 1179656 | tf_op jit(solution)/shard_map/ppermute | solution.py:946
  137.7 5.2 %collective-permute-start.26 = (bf16[256,768]{1,0:T(8,128)(2,1)S(1)}, bf16[256,768]{1,0:T(8,128)(2,1)S(1)}, u32[]{:S(2)}, u32[]{:S(2)}) collective-permute-start(bf16[256,768]{1,0:T(8,128)(2,1)S(1)} %get-tuple-element.187.refs_1_.refs_2_), channel_id=1, source_target_pairs={{0,4},{4,0},{1,5},{5,1},{2,6},{6,2},{3,7},{7,3},{8,12},{12,8},{9,1... | collective-permute-start | bytes 1179656 | tf_op jit(solution)/shard_map/ppermute | solution.py:936
  137.8 30.6 %collective-permute-start.25 = (bf16[384,1536]{1,0:T(8,128)(2,1)S(1)}, bf16[384,1536]{1,0:T(8,128)(2,1)S(1)}, u32[]{:S(2)}, u32[]{:S(2)}) collective-permute-start(bf16[384,1536]{1,0:T(8,128)(2,1)S(1)} %get-tuple-element.181), channel_id=1, source_target_pairs={{0,16},{16,0},{1,17},{17,1},{2,18},{18,2},{3,19},{19,3},{4,20},{20... | collective-permute-start | bytes 3538952 | tf_op jit(solution)/shard_map/ppermute | solution.py:936
  141.5 2.5 collective-permute-start.27
  145.4 54.7 %collective-permute-start.32 = (bf16[400,2048]{1,0:T(8,128)(2,1)S(1)}, bf16[400,2048]{1,0:T(8,128)(2,1)S(1)}, u32[]{:S(2)}, u32[]{:S(2)}) collective-permute-start(bf16[400,2048]{1,0:T(8,128)(2,1)S(1)} %get-tuple-element.205), channel_id=1, source_target_pairs={{0,16},{16,0},{1,17},{17,1},{2,18},{18,2},{3,19},{19,3},{4,20},{20... | collective-permute-start | bytes 4915208 | tf_op jit(solution)/shard_map/ppermute | solution.py:936
  155.3 2.4 collective-permute-start.28
  155.7 19.8 %collective-permute-start.24 = (bf16[256,768]{1,0:T(8,128)(2,1)S(1)}, bf16[256,768]{1,0:T(8,128)(2,1)S(1)}, u32[]{:S(2)}, u32[]{:S(2)}) collective-permute-start(bf16[256,768]{1,0:T(8,128)(2,1)S(1)} %keep.2.refs_4_.refs_1_), channel_id=1, source_target_pairs={{0,2},{2,0},{1,3},{3,1},{4,6},{6,4},{5,7},{7,5},{8,10},{10,8},{9,1... | collective-permute-start | bytes 1179656 | tf_op jit(solution)/shard_map/ppermute | solution.py:936
  169.2 24.3 %collective-permute-start.33 = (bf16[192,1536]{1,0:T(8,128)(2,1)S(1)}, bf16[192,1536]{1,0:T(8,128)(2,1)S(1)}, u32[]{:S(2)}, u32[]{:S(2)}) collective-permute-start(bf16[192,1536]{1,0:T(8,128)(2,1)S(1)} %get-tuple-element.206), channel_id=1, source_target_pairs={{0,8},{8,0},{1,9},{9,1},{2,10},{10,2},{3,11},{11,3},{4,12},{12,4},... | collective-permute-start | bytes 1769480 | tf_op jit(solution)/shard_map/ppermute | solution.py:936
  170.8 32.6 %collective-permute-start.31 = (bf16[512,768]{1,0:T(8,128)(2,1)S(1)}, bf16[512,768]{1,0:T(8,128)(2,1)S(1)}, u32[]{:S(2)}, u32[]{:S(2)}) collective-permute-start(bf16[512,768]{1,0:T(8,128)(2,1)S(1)} %add.1.refs_11_), channel_id=1, source_target_pairs={{0,8},{8,0},{1,9},{9,1},{2,10},{10,2},{3,11},{11,3},{4,12},{12,4},... | collective-permute-start | bytes 2359304 | tf_op jit(solution)/shard_map/ppermute | solution.py:936
  187.3 16.2 %collective-permute-start.30 = (bf16[512,768]{1,0:T(8,128)(2,1)S(1)}, bf16[512,768]{1,0:T(8,128)(2,1)S(1)}, u32[]{:S(2)}, u32[]{:S(2)}) collective-permute-start(bf16[512,768]{1,0:T(8,128)(2,1)S(1)} %get-tuple-element.204), channel_id=1, source_target_pairs={{0,4},{4,0},{1,5},{5,1},{2,6},{6,2},{3,7},{7,3},{8,12},{12,8},{9,1... | collective-permute-start | bytes 2359304 | tf_op jit(solution)/shard_map/ppermute | solution.py:936
  188.4 19.1 %collective-permute-start.29 = (bf16[2,256,768]{2,1,0:T(8,128)(2,1)S(1)}, bf16[2,256,768]{2,1,0:T(8,128)(2,1)S(1)}, u32[]{:S(2)}, u32[]{:S(2)}) collective-permute-start(bf16[2,256,768]{2,1,0:T(8,128)(2,1)S(1)} %pair.1.refs_14_.refs_1_), channel_id=1, source_target_pairs={{0,1},{1,0},{2,3},{3,2},{4,5},{5,4},{6,7},{7,6},{8,9},{9,8},{10,11... | collective-permute-start | bytes 2359304 | tf_op jit(solution)/shard_map/ppermute | solution.py:936
  201.0 22.7 %collective-permute-start.41 = (bf16[208,2048]{1,0:T(8,128)(2,1)S(1)}, bf16[208,2048]{1,0:T(8,128)(2,1)S(1)}, u32[]{:S(2)}, u32[]{:S(2)}) collective-permute-start(bf16[208,2048]{1,0:T(8,128)(2,1)S(1)} %get-tuple-element.224), channel_id=1, source_target_pairs={{0,8},{8,0},{1,9},{9,1},{2,10},{10,2},{3,11},{11,3},{4,12},{12,4},... | collective-permute-start | bytes 2555912 | tf_op jit(solution)/shard_map/ppermute | solution.py:936
  202.2 11.6 %collective-permute-start.35 = (bf16[2,96,768]{2,1,0:T(8,128)(2,1)S(1)}, bf16[2,96,768]{2,1,0:T(8,128)(2,1)S(1)}, u32[]{:S(2)}, u32[]{:S(2)}) collective-permute-start(bf16[2,96,768]{2,1,0:T(8,128)(2,1)S(1)} %get-tuple-element.219), channel_id=1, source_target_pairs={{0,1},{1,0},{2,3},{3,2},{4,5},{5,4},{6,7},{7,6},{8,9},{9,8},{10,11... | collective-permute-start | bytes 884744 | tf_op jit(solution)/shard_map/ppermute | solution.py:936
  204.3 17.9 %collective-permute-start.34 = (bf16[256,768]{1,0:T(8,128)(2,1)S(1)}, bf16[256,768]{1,0:T(8,128)(2,1)S(1)}, u32[]{:S(2)}, u32[]{:S(2)}) collective-permute-start(bf16[256,768]{1,0:T(8,128)(2,1)S(1)} %get-tuple-element.217.refs_3_), channel_id=1, source_target_pairs={{0,1},{1,0},{2,3},{3,2},{4,5},{5,4},{6,7},{7,6},{8,9},{9,8},{10,11... | collective-permute-start | bytes 1179656 | tf_op jit(solution)/shard_map/ppermute | solution.py:936
  204.7 26.9 %collective-permute-start.38 = (bf16[208,1280]{1,0:T(8,128)(2,1)S(1)}, bf16[208,1280]{1,0:T(8,128)(2,1)S(1)}, u32[]{:S(2)}, u32[]{:S(2)}) collective-permute-start(bf16[208,1280]{1,0:T(8,128)(2,1)S(1)} %get-tuple-element.221), channel_id=1, source_target_pairs={{0,8},{8,0},{1,9},{9,1},{2,10},{10,2},{3,11},{11,3},{4,12},{12,4},... | collective-permute-start | bytes 1597448 | tf_op jit(solution)/shard_map/ppermute | solution.py:936
  207.5 26.7 %collective-permute-start.39 = (bf16[208,1280]{1,0:T(8,128)(2,1)S(1)}, bf16[208,1280]{1,0:T(8,128)(2,1)S(1)}, u32[]{:S(2)}, u32[]{:S(2)}) collective-permute-start(bf16[208,1280]{1,0:T(8,128)(2,1)S(1)} %get-tuple-element.222), channel_id=1, source_target_pairs={{0,16},{16,0},{1,17},{17,1},{2,18},{18,2},{3,19},{19,3},{4,20},{20... | collective-permute-start | bytes 1597448 | tf_op jit(solution)/shard_map/ppermute | solution.py:936
  213.8 30.0 %collective-permute-start.40 = (bf16[208,1280]{1,0:T(8,128)(2,1)S(1)}, bf16[208,1280]{1,0:T(8,128)(2,1)S(1)}, u32[]{:S(2)}, u32[]{:S(2)}) collective-permute-start(bf16[208,1280]{1,0:T(8,128)(2,1)S(1)} %get-tuple-element.223), channel_id=1, source_target_pairs={{0,24},{8,16},{16,8},{24,0},{1,25},{9,17},{17,9},{25,1},{2,26},{10... | collective-permute-start | bytes 1597448 | tf_op jit(solution)/shard_map/ppermute | solution.py:994
  222.9 22.1 %collective-permute-start.37 = (bf16[256,768]{1,0:T(8,128)(2,1)S(1)}, bf16[256,768]{1,0:T(8,128)(2,1)S(1)}, u32[]{:S(2)}, u32[]{:S(2)}) collective-permute-start(bf16[256,768]{1,0:T(8,128)(2,1)S(1)} %final.1.refs_3_.refs_1_), channel_id=1, source_target_pairs={{0,2},{2,0},{1,3},{3,1},{4,6},{6,4},{5,7},{7,5},{8,10},{10,8},{9,1... | collective-permute-start | bytes 1179656 | tf_op jit(solution)/shard_map/ppermute | solution.py:936
  224.7 23.4 %collective-permute-start.44 = (bf16[2,112,1024]{2,1,0:T(8,128)(2,1)S(1)}, bf16[2,112,1024]{2,1,0:T(8,128)(2,1)S(1)}, u32[]{:S(2)}, u32[]{:S(2)}) collective-permute-start(bf16[2,112,1024]{2,1,0:T(8,128)(2,1)S(1)} %get-tuple-element.228), channel_id=1, source_target_pairs={{0,1},{1,0},{2,3},{3,2},{4,5},{5,4},{6,7},{7,6},{8,9},{9,8},{10,11... | collective-permute-start | bytes 1376264 | tf_op jit(solution)/shard_map/ppermute | solution.py:936
  231.6 43.5 %collective-permute-start.36 = (bf16[256,768]{1,0:T(8,128)(2,1)S(1)}, bf16[256,768]{1,0:T(8,128)(2,1)S(1)}, u32[]{:S(2)}, u32[]{:S(2)}) collective-permute-start(bf16[256,768]{1,0:T(8,128)(2,1)S(1)} %final.1.refs_3_.refs_1_), channel_id=1, source_target_pairs={{0,1},{1,0},{2,3},{3,2},{4,5},{5,4},{6,7},{7,6},{8,9},{9,8},{10,11... | collective-permute-start | bytes 1179656 | tf_op jit(solution)/shard_map/ppermute | solution.py:936
  245.5 29.7 %collective-permute-start.42 = (bf16[256,768]{1,0:T(8,128)(2,1)S(1)}, bf16[256,768]{1,0:T(8,128)(2,1)S(1)}, u32[]{:S(2)}, u32[]{:S(2)}) collective-permute-start(bf16[256,768]{1,0:T(8,128)(2,1)S(1)} %keep.3.refs_3_), channel_id=1, source_target_pairs={{0,1},{1,0},{2,3},{3,2},{4,5},{5,4},{6,7},{7,6},{8,9},{9,8},{10,11... | collective-permute-start | bytes 1179656 | tf_op jit(solution)/shard_map/ppermute | solution.py:936
  247.3 23.9 %collective-permute-start.43 = (bf16[2,112,640]{2,1,0:T(8,128)(2,1)S(1)}, bf16[2,112,640]{2,1,0:T(8,128)(2,1)S(1)}, u32[]{:S(2)}, u32[]{:S(2)}) collective-permute-start(bf16[2,112,640]{2,1,0:T(8,128)(2,1)S(1)} %get-tuple-element.227), channel_id=1, source_target_pairs={{0,1},{1,0},{2,3},{3,2},{4,5},{5,4},{6,7},{7,6},{8,9},{9,8},{10,11... | collective-permute-start | bytes 860168 | tf_op jit(solution)/shard_map/ppermute | solution.py:936
  247.4 19.7 %collective-permute-start.48 = (bf16[96,768]{1,0:T(8,128)(2,1)S(1)}, bf16[96,768]{1,0:T(8,128)(2,1)S(1)}, u32[]{:S(2)}, u32[]{:S(2)}) collective-permute-start(bf16[96,768]{1,0:T(8,128)(2,1)S(1)} %get-tuple-element.232), channel_id=1, source_target_pairs={{0,4},{1,5},{2,0},{3,1},{4,6},{5,7},{6,2},{7,3},{8,12},{9,13},{10,... | collective-permute-start | bytes 442376 | tf_op jit(solution)/shard_map/ppermute | solution.py:946
  248.9 32.8 %collective-permute-start.50 = (bf16[112,1024]{1,0:T(8,128)(2,1)S(1)}, bf16[112,1024]{1,0:T(8,128)(2,1)S(1)}, u32[]{:S(2)}, u32[]{:S(2)}) collective-permute-start(bf16[112,1024]{1,0:T(8,128)(2,1)S(1)} %get-tuple-element.233), channel_id=1, source_target_pairs={{0,4},{1,5},{2,0},{3,1},{4,6},{5,7},{6,2},{7,3},{8,12},{9,13},{10,... | collective-permute-start | bytes 688136 | tf_op jit(solution)/shard_map/ppermute | solution.py:946
  267.1 14.6 %collective-permute-start.49 = (bf16[112,1024]{1,0:T(8,128)(2,1)S(1)}, bf16[112,1024]{1,0:T(8,128)(2,1)S(1)}, u32[]{:S(2)}, u32[]{:S(2)}) collective-permute-start(bf16[112,1024]{1,0:T(8,128)(2,1)S(1)} %get-tuple-element.229.refs_3_), channel_id=1, source_target_pairs={{0,0},{1,1},{2,4},{3,5},{4,2},{5,3},{6,6},{7,7},{8,8},{9,9},{10,12... | collective-permute-start | bytes 688136 | tf_op jit(solution)/shard_map/ppermute | solution.py:946
  271.2 10.5 %collective-permute-start.47 = (bf16[96,768]{1,0:T(8,128)(2,1)S(1)}, bf16[96,768]{1,0:T(8,128)(2,1)S(1)}, u32[]{:S(2)}, u32[]{:S(2)}) collective-permute-start(bf16[96,768]{1,0:T(8,128)(2,1)S(1)} %get-tuple-element.220.refs_3_), channel_id=1, source_target_pairs={{0,0},{1,1},{2,4},{3,5},{4,2},{5,3},{6,6},{7,7},{8,8},{9,9},{10,12... | collective-permute-start | bytes 442376 | tf_op jit(solution)/shard_map/ppermute | solution.py:946
  275.1 9.5 %collective-permute-start.46 = (bf16[112,640]{1,0:T(8,128)(2,1)S(1)}, bf16[112,640]{1,0:T(8,128)(2,1)S(1)}, u32[]{:S(2)}, u32[]{:S(2)}) collective-permute-start(bf16[112,640]{1,0:T(8,128)(2,1)S(1)} %get-tuple-element.231), channel_id=1, source_target_pairs={{0,4},{1,5},{2,0},{3,1},{4,6},{5,7},{6,2},{7,3},{8,12},{9,13},{10,... | collective-permute-start | bytes 430088 | tf_op jit(solution)/shard_map/ppermute | solution.py:946
  275.2 11.1 %collective-permute-start.45 = (bf16[112,640]{1,0:T(8,128)(2,1)S(1)}, bf16[112,640]{1,0:T(8,128)(2,1)S(1)}, u32[]{:S(2)}, u32[]{:S(2)}) collective-permute-start(bf16[112,640]{1,0:T(8,128)(2,1)S(1)} %get-tuple-element.230.refs_5_), channel_id=1, source_target_pairs={{0,0},{1,1},{2,4},{3,5},{4,2},{5,3},{6,6},{7,7},{8,8},{9,9},{10,12... | collective-permute-start | bytes 430088 | tf_op jit(solution)/shard_map/ppermute | solution.py:946
  (44 other events, 344.7 us)
Sparse Core Ops, SparseCore 0:
  47.6 52.3 all-gather.2
